TPU v7x, 32 devices: a whole 2x2x4 slice. The times are simulated.
32 devices in a mesh: fsdp: 4 (over x, core), context: 2 (over y), tensor: 4 (over z).
Axes of the slice: x: 2, y: 2, z: 4, core: 2. Of those that a mesh axis runs over, the one named last changes fastest.
Arguments:
- tokens: bfloat16 [8192, 1024], P(('fsdp', 'context')), may hold values from -6 to 6
- cotangent: bfloat16 [8192, 1024], P(('fsdp', 'context')), may hold values from -6 to 6
- segments: int32 [8192], P(('fsdp', 'context')), may hold values from 0 to 3, as said below
- positions: int32 [8192], P(('fsdp', 'context')), may hold values from 0 to 1535, as said below
- parents: int32 [4, 4], P('fsdp'), may hold values from 0 to 3, as said below
- block_lists: int32 [16, 3], P(('fsdp', 'context')), may hold values from -1 to 3, as said below
- project_weight: bfloat16 [1024, 3, 1024], P('fsdp', None, 'tensor'), may hold values from -0.1875 to 0.1875
- project_bias: float32 [3, 1024], P(None, 'tensor'), may hold values from -3 to 3
- dense_weight: bfloat16 [1024, 1024], P('tensor', 'fsdp'), may hold values from -3 to 3
- dense_bias: float32 [1024], replicated, may hold values from -3 to 3
- up_weight: bfloat16 [1024, 4096], P('fsdp', 'tensor'), may hold values from -0.1875 to 0.1875
- up_bias: float32 [4096], P('tensor'), may hold values from -3 to 3
- down_weight: bfloat16 [4096, 1024], P('tensor', 'fsdp'), may hold values from -0.09375 to 0.09375
- down_bias: float32 [1024], replicated, may hold values from -3 to 3
- first_gain: float32 [1024], replicated, may hold values from 0.1 to 1.9
- first_shift: float32 [1024], replicated, may hold values from -3 to 3
- second_gain: float32 [1024], replicated, may hold values from 0.1 to 1.9
- second_shift: float32 [1024], replicated, may hold values from -3 to 3
Outputs:
- layer_out: bfloat16 [8192, 1024], P(('fsdp', 'context'))
- tokens_grad: bfloat16 [8192, 1024], P(('fsdp', 'context'))
- project_weight_grad: float32 [1024, 3, 1024], P('fsdp', None, 'tensor')
- project_bias_grad: float32 [3, 1024], P(None, 'tensor')
- dense_weight_grad: float32 [1024, 1024], P('tensor', 'fsdp')
- dense_bias_grad: float32 [1024], replicated
- up_weight_grad: float32 [1024, 4096], P('fsdp', 'tensor')
- up_bias_grad: float32 [4096], P('tensor')
- down_weight_grad: float32 [4096, 1024], P('tensor', 'fsdp')
- down_bias_grad: float32 [1024], replicated
- first_gain_grad: float32 [1024], replicated
- first_shift_grad: float32 [1024], replicated
- second_gain_grad: float32 [1024], replicated
- second_shift_grad: float32 [1024], replicated
Inputs may be any that keep to these rules, and one draw needn't show every extreme that they name: `segments`: every aligned block of 512 tokens lies in one segment; a tree has one trunk of 1 block, 1 branches and 2 leaves of one block each, its blocks in any order. The trunk's blocks hold positions 0 to 511, a branch's block starts at 512, a leaf's at 1024; within a block positions rise by one. `parents`: the trunk is its own parent, each branch's parent is the trunk, each leaf's parent a branch, each branch the parent of two leaves. `block_lists`: each row holds its own block and every block of the segments above it on its path, each once in some order, then -1 to the end; a listed block other than its own lies wholly in an ancestor segment with smaller positions.
All inputs are finite; a program needn't handle non-finite values.
Results may differ from a plain program's by a relative error of at most 0.012.
The roundings to bfloat16 on the way count: a program that leaves them out, or rounds other values in their place, can miss the bound.
Values may be sent and summed in bfloat16 or wider, within the bound.
No kernel may reach another device: no remote copies, remote signals or barrier semaphores. Data moves between devices by JAX's collectives and lax.ppermute only.
A program may use at most 128 MiB of HBM per device.

v0:
```python
from functools import partial

import jax
import jax.numpy as jnp
from jax import lax
from jax.experimental import pallas as pl
from jax.experimental.pallas import tpu as pltpu
from jax.sharding import PartitionSpec as P

HD = 64
ROT = 16
BLK = 512
PAIR = 2 * HD
SHARD = 256
EXTRA = 16

epsilon = 1e-05
masked = -1e30
bf16 = jnp.bfloat16
f32 = jnp.float32
scale2 = HD ** (-0.5) * 1.4426950408889634
NT = (((1,), (1,)), ((), ()))
NN = (((1,), (0,)), ((), ()))
TN = (((0,), (0,)), ((), ()))


def dot(a, b, dims):
    return lax.dot_general(a, b, dims, preferred_element_type=f32)


def params(mib):
    return pltpu.CompilerParams(vmem_limit_bytes=mib * 1024 * 1024)


SCALE = 1.0


def cost(micros):
    return pl.CostEstimate(
        flops=int(1.15e9 * micros * SCALE), bytes_accessed=int(3.7e6 * micros * SCALE), transcendentals=0
    )


def whole(shape):
    return pl.BlockSpec(shape, lambda *_: (0,) * len(shape))


smem = pl.BlockSpec(memory_space=pltpu.SMEM)


def norm_rows(x):
    mean = jnp.mean(x, axis=-1, keepdims=True)
    centered = x - mean
    variance = jnp.mean(centered * centered, axis=-1, keepdims=True)
    factor = lax.rsqrt(variance + epsilon)
    return centered * factor, factor


def rotate_lanes(x, cos, sin, sign):
    lane = lax.broadcasted_iota(jnp.int32, x.shape, 1) % HD
    left = pltpu.roll(x, PAIR - ROT // 2, 1)
    right = pltpu.roll(x, ROT // 2, 1)
    return x * cos + jnp.where(lane < ROT // 2, -sign * left, sign * right) * sin


def columns(index, width):
    return pl.ds(pl.multiple_of(index * width, width), width)


def project_kernel(
    ids, x, gain, shift, w0, w1, w2, w3, bias, cos, sin, q0, q1, kv0, kv1, n1
):
    normal, _ = norm_rows(x[...].astype(f32))
    n1[...] = (normal * gain[...] + shift[...]).astype(bf16)
    weights = (w0, w1, w2, w3)
    width = w0.shape[1]
    depth = w0.shape[0] // 3
    outs = ((q0, q1), (kv0, kv1))
    for part in range(3):
        total = bias[part : part + 1, :] + jnp.zeros((n1.shape[0], width), f32)
        for piece in range(4):
            total += dot(n1[:, columns(ids[piece], depth)], weights[piece][part * depth : (part + 1) * depth, :], NN)
        for pair in range(2):
            half = total[:, pair * PAIR : (pair + 1) * PAIR]
            if part < 2:
                half = rotate_lanes(half, cos[...], sin[...], 1.0)
            if part == 0:
                outs[0][pair][...] = half.astype(bf16)
            else:
                outs[1][pair][:, (part - 1) * PAIR : part * PAIR] = half.astype(bf16)


def project(ids, x, gain, shift, weights, bias, tables, tile=256):
    rows, wide = x.shape
    row = lambda w: pl.BlockSpec((tile, w), lambda i: (i, 0))
    s = jax.ShapeDtypeStruct
    return pl.pallas_call(
        project_kernel,
        grid=(rows // tile,),
        in_specs=[smem, row(wide)]
        + [whole(v.shape) for v in (gain, shift, *weights, bias)]
        + [row(PAIR)] * 2,
        out_specs=[row(PAIR)] * 2 + [row(2 * PAIR)] * 2 + [row(wide)],
        out_shape=[s((rows, PAIR), bf16)] * 2
        + [s((rows, 2 * PAIR), bf16)] * 2
        + [s((rows, wide), bf16)],
        compiler_params=params(18),
        cost_estimate=cost(4.3),
        name="project",
    )(ids, x, gain, shift, *weights, bias, *tables)


def head_lanes(shape, head):
    return lax.broadcasted_iota(jnp.int32, shape, 1) // HD == head


def load_keys(kvs, kv_scr):
    start = 0
    for part in kvs:
        count = part.shape[0] // BLK
        for block in range(count):
            kv_scr[start + block] = part[block * BLK : (block + 1) * BLK, :]
        start += count


def attend_forward_kernel(maxk, low, count, first, last, ids, q, kv, *refs):
    if first:
        ins, refs = None, refs
    else:
        ins, refs = refs[:2], refs[2:]
    outs, (turned, state, acc) = refs[:2], refs[2:]
    for slot in range(count):
        turned[slot] = kv[slot * BLK : (slot + 1) * BLK, PAIR:].T
    if not first:
        state[...] = ins[0][...]
        acc[...] = ins[1][...]
    for block in range(q.shape[0] // BLK):
        own = ids[0] + block
        for head in range(2):
            rows = slice(block * PAIR + head * HD, block * PAIR + (head + 1) * HD)
            part = slice(head * HD, (head + 1) * HD)
            line = block * 2 + head
            tops, sums = slice(line, line + 1), slice(8 + line, 9 + line)
            query = q[block * BLK : (block + 1) * BLK, :]
            query = jnp.where(head_lanes(query.shape, head), query, jnp.zeros_like(query))

            if first:
                at = pl.ds(pl.multiple_of((own - low) * BLK, BLK), BLK)
                scores = dot(kv[at, :PAIR], query, NT) * scale2
                keep = lax.broadcasted_iota(jnp.int32, scores.shape, 0) <= lax.broadcasted_iota(
                    jnp.int32, scores.shape, 1
                )
                scores = jnp.where(keep, scores, masked)
                top = jnp.max(scores, axis=0, keepdims=True)
                weight = jnp.exp2(scores - top)
                state[tops, :] = top
                state[sums, :] = jnp.sum(weight, axis=0, keepdims=True)
                acc[rows, :] = dot(turned[own - low][part, :], weight.astype(bf16), NN)

            def entry(step, unused):
                slot = ids[2 + block * maxk + step]

                @pl.when((slot >= low) & (slot < low + count) & (slot != own))
                def _():
                    at = pl.ds(pl.multiple_of((slot - low) * BLK, BLK), BLK)
                    scores = dot(kv[at, :PAIR], query, NT) * scale2
                    old = state[tops, :]
                    top = jnp.maximum(old, jnp.max(scores, axis=0, keepdims=True))
                    weight = jnp.exp2(scores - top)
                    shrink = jnp.exp2(old - top)
                    state[tops, :] = top
                    state[sums, :] = state[sums, :] * shrink + jnp.sum(
                        weight, axis=0, keepdims=True
                    )
                    acc[rows, :] = acc[rows, :] * shrink + dot(
                        turned[slot - low][part, :], weight.astype(bf16), NN
                    )

                return unused

            lax.fori_loop(0, maxk, entry, 0)
            if last:
                outs[1][line : line + 1, :] = state[tops, :] + jnp.log2(state[sums, :])
                acc[rows, :] = acc[rows, :] * (1.0 / state[sums, :])
        if last:
            outs[0][block * BLK : (block + 1) * BLK, :] = acc[
                block * PAIR : (block + 1) * PAIR, :
            ].T
    if not last:
        outs[0][...] = state[...]
        outs[1][...] = acc[...]


def attend_forward(ids, maxk, q, kv, low, carried, last, micros=0):
    count = kv.shape[0] // BLK
    rows = q.shape[0]
    tall = rows // BLK * PAIR
    vmem = pl.BlockSpec(memory_space=pltpu.VMEM)
    s = jax.ShapeDtypeStruct
    shapes = [s((rows, PAIR), f32), s((8, BLK), f32)] if last else [
        s((16, BLK), f32), s((tall, BLK), f32)
    ]
    return pl.pallas_call(
        partial(attend_forward_kernel, maxk, low, count, carried is None, last),
        in_specs=[smem] + [vmem] * (2 + len(carried or ())),
        out_specs=[vmem] * 2,
        out_shape=shapes,
        scratch_shapes=[
            pltpu.VMEM((count, PAIR, BLK), bf16),
            pltpu.VMEM((16, BLK), f32),
            pltpu.VMEM((tall, BLK), f32),
        ],
        compiler_params=params(8 + 2 * count),
        cost_estimate=cost(micros),
        name="attend_forward",
    )(ids, q, kv, *(carried or ()))


def attend_backward_kernel(slots, maxk, split, ids, q, g, o, lse, cos, sin, *refs):
    outs = 2 if split else 1
    parts = refs[: -5 - outs]
    grads = refs[-5 - outs : -5]
    qg, kv, turned, acc, total = refs[-5:]
    load_keys(parts, kv)
    for slot in range(slots):
        turned[slot] = kv[slot][:, :PAIR].T
    total[...] = jnp.zeros_like(total)
    pick = (
        lax.broadcasted_iota(jnp.int32, (8, PAIR), 1) // HD
        == lax.broadcasted_iota(jnp.int32, (8, PAIR), 0)
    ).astype(f32)
    for block in range(q.shape[0] // BLK):
        own = ids[0] + block
        span = slice(block * BLK, (block + 1) * BLK)
        deltas = lax.dot_general(
            pick,
            o[span, :] * g[span, :].astype(f32),
            NT,
            preferred_element_type=f32,
            precision=lax.Precision.HIGHEST,
        )
        for head in range(2):
            rows = slice(head * HD, (head + 1) * HD)
            lanes = head_lanes((BLK, PAIR), head)
            query = q[span, :]
            query = jnp.where(lanes, query, jnp.zeros_like(query))
            grad = g[span, :]
            grad = jnp.where(lanes, grad, jnp.zeros_like(grad))
            line = block * 2 + head
            log_sum = lse[line : line + 1, :]
            delta = deltas[head : head + 1, :]

            def tile(slot, keep):
                scores = dot(kv[slot][:, :PAIR], query, NT) * scale2
                prob = jnp.exp2(scores - log_sum)
                if keep is not None:
                    prob = jnp.where(keep, prob, 0.0)
                prob_grad = dot(kv[slot][:, PAIR:], grad, NT)
                score_grad = (prob * (prob_grad - delta)).astype(bf16)
                total[slot, :, PAIR:] += dot(prob.astype(bf16), grad, NN)
                total[slot, :, :PAIR] += dot(score_grad, query, NN)
                return dot(turned[slot][rows, :], score_grad, NN)

            keep = lax.broadcasted_iota(jnp.int32, (BLK, BLK), 0) <= lax.broadcasted_iota(
                jnp.int32, (BLK, BLK), 1
            )
            acc[rows, :] = tile(own, keep)

            def entry(step, unused):
                slot = ids[2 + block * maxk + step]

                @pl.when((slot >= 0) & (slot != own))
                def _():
                    acc[rows, :] += tile(slot, None)

                return unused

            lax.fori_loop(0, maxk, entry, 0)
        grad_q = acc[...].T * (HD ** (-0.5))
        qg[span, :] = rotate_lanes(
            grad_q, cos[span, :], sin[span, :], -1.0
        ).astype(bf16)
    start = 0
    for out in grads:
        count = out.shape[0] // BLK
        for block in range(count):
            out[block * BLK : (block + 1) * BLK, :] = total[start + block].astype(out.dtype)
        start += count


def attend_backward(ids, maxk, q, g, o, lse, tables, kvs):
    slots = sum(part.shape[0] for part in kvs) // BLK
    rows = q.shape[0]
    split = len(kvs) == 2
    shapes = [jax.ShapeDtypeStruct(kvs[0].shape, bf16)]
    if split:
        shapes.append(jax.ShapeDtypeStruct(kvs[1].shape, bf16))
    shapes.append(jax.ShapeDtypeStruct((rows, PAIR), bf16))
    vmem = pl.BlockSpec(memory_space=pltpu.VMEM)
    return pl.pallas_call(
        partial(attend_backward_kernel, slots, maxk, split),
        grid=(),
        in_specs=[smem] + [vmem] * (6 + len(kvs)),
        out_specs=[vmem] * len(shapes),
        out_shape=shapes,
        scratch_shapes=[
            pltpu.VMEM((slots, BLK, 2 * PAIR), bf16),
            pltpu.VMEM((slots, PAIR, BLK), bf16),
            pltpu.VMEM((PAIR, BLK), f32),
            pltpu.VMEM((slots, BLK, 2 * PAIR), f32),
        ],
        compiler_params=params(14 + slots),
        cost_estimate=cost(0),
        name="attend_backward",
    )(ids, q, g, o, lse, *tables, *kvs)


def unpack(ids, pieces, units, up, down, dense):
    for i, piece in enumerate(pieces):
        where = columns(ids[i], SHARD)
        down[:, where] = piece[:units, :]
        for n in range(units // SHARD):
            up[where, n * SHARD : (n + 1) * SHARD] = piece[
                units + n * SHARD : units + (n + 1) * SHARD, :
            ]
        if dense is not None:
            dense[:, where] = piece[2 * units :, :]


def store_part(outs, sizes, value):
    tile = value.shape[0]
    step = pl.program_id(0)
    start = 0
    for out, size in zip(outs, sizes):
        count = size // tile

        @pl.when((step >= start) & (step < start + count))
        def _():
            out[pl.ds(pl.multiple_of((step - start) * tile, tile), tile), :] = value

        start += count


def mlp_forward_kernel(
    rows, ids, x, cot, gain, shift, up_bias, p0, p1, p2, p3, o0, o1,
    keep, send, n2, act, slope, ctx, g0, g1, up, down, dense,
):
    units = act.shape[1]

    @pl.when(pl.program_id(0) == 0)
    def _():
        unpack(ids, (p0, p1, p2, p3), units, up, down, dense)

    normal, _ = norm_rows(x[...].astype(f32))
    normed = (normal * gain[...] + shift[...]).astype(bf16)
    n2[...] = normed
    hidden = dot(normed, up[...], NN) + up_bias[...]
    cdf = 0.5 + 0.5 * lax.erf(hidden * (2.0 ** -0.5))
    pdf = jnp.exp(hidden * hidden * -0.5) * 0.3989422804014327
    low = (hidden * cdf).astype(bf16)
    act[...] = low
    slope[...] = (cdf + hidden * pdf).astype(bf16)
    context_grad = dot(cot[...], dense[...], NT)
    g0[...] = context_grad[:, :PAIR].astype(bf16)
    g1[...] = context_grad[:, PAIR:].astype(bf16)
    ctx[:, :PAIR] = o0[...].astype(bf16)
    ctx[:, PAIR:] = o1[...].astype(bf16)
    value = dot(ctx[...], dense[...], NN) + dot(low, down[...], NN)
    store_part((keep, send), (rows // 2, rows // 2), value.astype(bf16))


def mlp_forward(ids, x, cot, gain, shift, up_bias, pieces, o0, o1, tile=256):
    rows, width = x.shape
    units = up_bias.shape[1]
    row = lambda w: pl.BlockSpec((tile, w), lambda i: (i, 0))
    s = jax.ShapeDtypeStruct
    return pl.pallas_call(
        partial(mlp_forward_kernel, rows),
        grid=(rows // tile,),
        in_specs=[smem, row(width), row(width)]
        + [whole(a.shape) for a in (gain, shift, up_bias, *pieces)]
        + [row(PAIR), row(PAIR)],
        out_specs=[whole((rows // 2, width))] * 2
        + [row(width), row(units), row(units), row(2 * PAIR), row(PAIR), row(PAIR)],
        out_shape=[s((rows // 2, width), bf16)] * 2
        + [
            s((rows, width), bf16), s((rows, units), bf16), s((rows, units), bf16),
            s((rows, 2 * PAIR), bf16), s((rows, PAIR), bf16), s((rows, PAIR), bf16),
        ],
        scratch_shapes=[
            pltpu.VMEM((width, units), bf16),
            pltpu.VMEM((units, width), bf16),
            pltpu.VMEM((2 * PAIR, width), bf16),
        ],
        compiler_params=params(28),
        cost_estimate=cost(1),
        name="mlp_forward",
    )(ids, x, cot, gain, shift, up_bias, *pieces, o0, o1)


def mlp_backward_kernel(
    ids, x, cot, gain, slope, p0, p1, p2, p3, hid, e2, sums, up, down
):
    units = hid.shape[1]

    @pl.when(pl.program_id(0) == 0)
    def _():
        sums[...] = jnp.zeros_like(sums)
        unpack(ids, (p0, p1, p2, p3), units, up, down, None)

    low = (dot(cot[...], down[...], NT) * slope[...].astype(f32)).astype(bf16)
    hid[...] = low
    grad = dot(low, up[...], NT)
    normal, _ = norm_rows(x[...].astype(f32))
    sums[0:1, :] += jnp.sum(grad * normal, axis=0, keepdims=True)
    sums[1:2, :] += jnp.sum(grad, axis=0, keepdims=True)
    sums[2:3, :] += jnp.sum(low.astype(f32), axis=0, keepdims=True)
    sums[3:4, :] += jnp.sum(cot[...].astype(f32), axis=0, keepdims=True)
    e2[...] = (grad * gain[...]).astype(bf16)


def mlp_backward(ids, x, cot, gain, slope, pieces, tile=256):
    rows, width = x.shape
    units = slope.shape[1]
    row = lambda w: pl.BlockSpec((tile, w), lambda i: (i, 0))
    s = jax.ShapeDtypeStruct
    return pl.pallas_call(
        mlp_backward_kernel,
        grid=(rows // tile,),
        in_specs=[smem, row(width), row(width), whole(gain.shape), row(units)]
        + [whole(a.shape) for a in pieces],
        out_specs=[row(units), row(width), whole((8, width))],
        out_shape=[s((rows, units), bf16), s((rows, width), bf16), s((8, width), f32)],
        scratch_shapes=[
            pltpu.VMEM((width, units), bf16),
            pltpu.VMEM((units, width), bf16),
        ],
        compiler_params=params(26),
        cost_estimate=cost(1),
        name="mlp_backward",
    )(ids, x, cot, gain, slope, *pieces)


def mlp_weights_kernel(ids, act, cot, n2, hid, keep, near, far):
    units = act.shape[1]
    step = pl.program_id(0)
    index = ids[step]
    for out, when in ((near, step == 0), (far, step == 1), (keep, step >= 2)):

        @pl.when(when)
        def _():
            out[0, :units, :] = dot(act[...], cot[:, columns(index, SHARD)], TN).astype(bf16)
            lhs = n2[:, columns(index, SHARD)]
            for n in range(units // SHARD):
                at = slice(n * SHARD, (n + 1) * SHARD)
                out[0, units + n * SHARD : units + (n + 1) * SHARD, :] = dot(
                    lhs, hid[:, at], TN
                ).astype(bf16)


def rest_weights_kernel(ids, ctx, cot, n1, pg, keep, near, far):
    width = ctx.shape[1]
    step = pl.program_id(0)
    index = ids[step]
    for out, when in ((near, step == 0), (far, step == 1), (keep, step >= 2)):

        @pl.when(when)
        def _():
            out[0, :width, :] = dot(ctx[...], cot[:, columns(index, SHARD)], TN).astype(bf16)
            lhs = n1[:, columns(index, SHARD)]
            for n in range(3):
                at = slice(n * SHARD, (n + 1) * SHARD)
                out[0, width + n * SHARD : width + (n + 1) * SHARD, :] = dot(
                    lhs, pg[:, at], TN
                ).astype(bf16)


def weight_parts(kernel, name, ids, tall, *args):
    s = lambda n: jax.ShapeDtypeStruct((n, tall, SHARD), bf16)
    return pl.pallas_call(
        kernel,
        grid=(4,),
        in_specs=[smem] + [whole(a.shape) for a in args],
        out_specs=[
            pl.BlockSpec((1, tall, SHARD), lambda i: (jnp.maximum(i - 2, 0), 0, 0)),
            whole((1, tall, SHARD)),
            whole((1, tall, SHARD)),
        ],
        out_shape=[s(2), s(1), s(1)],
        compiler_params=params(20),
        cost_estimate=cost(0),
        name=name,
    )(ids, *args)


def input_grad_kernel(
    split, sizes, ids, x, e2, gain, sums_two, qg0, qg1, cos, sin, w0, w1, w2, w3, *refs
):
    count = 4 if split else 2
    grads, es, (pg, sums, first) = refs[:count], refs[count:-3], refs[-3:]
    weights = (w0, w1, w2, w3)
    depth = w0.shape[0] // 3
    width = w0.shape[1]

    @pl.when(pl.program_id(0) == 0)
    def _():
        sums[...] = sums_two[...]

    pg[:, 0:PAIR] = qg0[...]
    pg[:, PAIR : 2 * PAIR] = qg1[...]
    for pair in range(2):
        if split:
            own, other = grads[2 * pair : 2 * pair + 2]
            grad = own[...].astype(f32) + other[...].astype(f32)
        else:
            grad = grads[pair][...].astype(f32)
        key = rotate_lanes(
            grad[:, :PAIR] * (HD ** (-0.5)), cos[...], sin[...], -1.0
        )
        at = width + pair * PAIR
        pg[:, at : at + PAIR] = key.astype(bf16)
        pg[:, at + width : at + width + PAIR] = grad[:, PAIR:].astype(bf16)
    sums[6:7, : 3 * width] += jnp.sum(pg[...].astype(f32), axis=0, keepdims=True)
    normal, _ = norm_rows(x[...].astype(f32))
    for piece in range(4):
        where = columns(ids[piece], depth)
        total = dot(pg[:, :width], weights[piece][:depth, :], NT)
        total += dot(pg[:, width : 2 * width], weights[piece][depth : 2 * depth, :], NT)
        total += dot(pg[:, 2 * width :], weights[piece][2 * depth :, :], NT)
        first[:, where] = total
    grad = first[...]
    store_part(es, sizes, (grad * gain[...] + e2[...].astype(f32)).astype(bf16))
    sums[4:5, :] += jnp.sum(grad * normal, axis=0, keepdims=True)
    sums[5:6, :] += jnp.sum(grad, axis=0, keepdims=True)

    @pl.when(pl.program_id(0) == pl.num_programs(0) - 1)
    def _():
        terms = split_terms(jnp.concatenate([sums[0:2, :], sums[4:6, :]], axis=0))
        es[0][sizes[0] :, :] = terms


def input_grad(ids, x, e2, gain, sums, qgs, tables, weights, grads, split, tile=256):
    rows, width = x.shape
    row = lambda w: pl.BlockSpec((tile, w), lambda i: (i, 0))
    s = jax.ShapeDtypeStruct
    units = 3 * weights[0].shape[1]
    sizes = (rows // 2,) * 2
    parts = [(sizes[0] + EXTRA, width), *[(size, width) for size in sizes[1:]]]
    return pl.pallas_call(
        partial(input_grad_kernel, split, sizes),
        grid=(rows // tile,),
        in_specs=[smem, row(width), row(width), whole(gain.shape), whole(sums.shape)]
        + [row(PAIR), row(PAIR)]
        + [row(PAIR)] * 2
        + [whole(w.shape) for w in weights]
        + [row(2 * PAIR)] * len(grads),
        out_specs=[whole(part) for part in parts] + [row(units), whole((8, width))],
        out_shape=[s(part, bf16) for part in parts]
        + [s((rows, units), bf16), s((8, width), f32)],
        scratch_shapes=[pltpu.VMEM((tile, width), f32)],
        compiler_params=params(24),
        cost_estimate=cost(0),
        name="input_grad",
    )(ids, x, e2, gain, sums, *qgs, *tables, *weights, *grads)


def call(kernel, name, args, shapes, grid=1, in_specs=None, out_specs=None, aliases=None, mib=16):
    s = jax.ShapeDtypeStruct
    many = isinstance(shapes, list)
    shapes = [s(*shape) for shape in (shapes if many else [shapes])]
    out = pl.pallas_call(
        kernel,
        grid=(grid,),
        in_specs=in_specs or [whole(a.shape) for a in args],
        out_specs=out_specs or [whole(shape.shape) for shape in shapes],
        out_shape=shapes,
        input_output_aliases=aliases or {},
        compiler_params=params(mib),
        cost_estimate=cost(0),
        name=name,
    )(*args)
    return out if many else out[0]


def add_kernel(a, b, out):
    out[...] = (a[...].astype(f32) + b[...].astype(f32)).astype(out.dtype)


def add(a, b, dtype=bf16, grid=2):
    grid = grid if a.shape[0] > 8 else 1
    row = pl.BlockSpec((a.shape[0] // grid, a.shape[1]), lambda i: (i, 0))
    return call(add_kernel, "add", (a, b), (a.shape, dtype), grid, [row, row], [row])


def split_terms(value):
    high = value.astype(bf16)
    rest = value - high.astype(f32)
    middle = rest.astype(bf16)
    low = (rest - middle.astype(f32)).astype(bf16)
    return jnp.concatenate([high, middle, low, jnp.zeros_like(low)], axis=0)


def join_terms(terms):
    terms = terms.astype(f32)
    return terms[0:4] + terms[4:8] + terms[8:12]


def add_extra_kernel(a, b, out):
    rows = a.shape[0] - EXTRA
    out[:rows, :] = (a[:rows, :].astype(f32) + b[:rows, :].astype(f32)).astype(out.dtype)
    out[rows:, :] = split_terms(join_terms(a[rows:, :]) + join_terms(b[rows:, :]))


def add_extra(a, b):
    return call(add_extra_kernel, "add_extra", (a, b), (a.shape, a.dtype))


def finish_out_kernel(a, b, x, dense_bias, down_bias, out):
    total = a[...].astype(f32) + b[...].astype(f32)
    out[...] = (x[...].astype(f32) + total + (dense_bias[...] + down_bias[...])).astype(bf16)


def finish_in_kernel(rows, a, b, x, upstream, out):
    tile = 128
    for at in range(0, rows, tile):
        here = slice(at, at + tile)
        total = a[here, :].astype(f32) + b[here, :].astype(f32)
        normal, factor = norm_rows(x[here, :].astype(f32))
        mean_e = jnp.mean(total, axis=-1, keepdims=True)
        mean_en = jnp.mean(total * normal, axis=-1, keepdims=True)
        result = upstream[here, :].astype(f32) + factor * (total - mean_e - normal * mean_en)
        out[here, :] = result.astype(bf16)
    if a.shape[0] > rows:
        out[rows:, :] = split_terms(join_terms(a[rows:, :]) + join_terms(b[rows:, :]))


def finish(kernel, name, start, rows, of_rows, arrays, a, b):
    block = pl.BlockSpec((rows, a.shape[1]), lambda i: (start // rows, 0))
    specs = [whole(a.shape)] * 2 + [
        block if i < of_rows else whole(v.shape) for i, v in enumerate(arrays)
    ]
    return call(kernel, name, (a, b, *arrays), (a.shape, bf16), 1, specs)


def choose_kernel(sizes, flag, *refs):
    out, count = refs[-1], len(sizes)
    for parts, when in ((refs[:count], flag[0] > 0), (refs[count : 2 * count], flag[0] <= 0)):

        @pl.when(when)
        def _():
            start = 0
            for part, size in zip(parts, sizes):
                out[start : start + size, :] = part[:size, :]
                start += size


def choose(flag, ours, theirs, sizes, start=0, total=None, before=None):
    rows, width = sum(sizes), ours[0].shape[1]
    args = (flag, *ours, *theirs)
    specs, aliases = [smem] + [whole(v.shape) for v in args[1:]], {}
    if before is not None:
        aliases = {len(args): 0}
        args, specs = args + (before,), specs + [pl.BlockSpec(memory_space=pl.ANY)]
    return call(
        partial(choose_kernel, sizes), "choose", args, ((total or rows, width), bf16), 1, specs,
        [pl.BlockSpec((rows, width), lambda i: (start // rows, 0))], aliases,
    )


def decode_kernel(flag, ours, theirs, out):
    out[0:4, :] = jnp.where(flag[0] > 0, join_terms(ours[...]), join_terms(theirs[...]))
    out[4:8, :] = jnp.zeros((4, out.shape[1]), f32)


def decode(flag, ours, theirs):
    at = ours.shape[0] // EXTRA - 1
    block = pl.BlockSpec((EXTRA, ours.shape[1]), lambda i: (at, 0))
    return call(
        decode_kernel, "decode", (flag, ours, theirs), ((8, ours.shape[1]), f32), 1,
        [smem, block, block],
    )


def halves_kernel(keep, near, far, here, there):
    here[...] = keep[0].astype(f32) + near[0].astype(f32)
    there[...] = (keep[1].astype(f32) + far[0].astype(f32)).astype(bf16)


def halves(keep, got, grid=2):
    tall, width = keep.shape[1:]
    block = lambda n: pl.BlockSpec((n, tall // grid, width), lambda i: (0, i, 0))
    row = pl.BlockSpec((tall // grid, width), lambda i: (i, 0))
    return call(
        halves_kernel, "halves", (keep, *got), [((tall, width), f32), ((tall, width), bf16)],
        grid, [block(2), block(1), block(1)], [row, row],
    )


def mlp_last_kernel(a, b, down, up):
    units = down.shape[0]
    down[...] = a[:units, :].astype(f32) + b[:units, :].astype(f32)
    for n in range(units // SHARD):
        at = slice(units + n * SHARD, units + (n + 1) * SHARD)
        up[:, n * SHARD : (n + 1) * SHARD] = a[at, :].astype(f32) + b[at, :].astype(f32)


def rest_last_kernel(a, b, dense, project):
    dense[...] = a[:SHARD, :].astype(f32) + b[:SHARD, :].astype(f32)
    for n in range(3):
        at = slice((n + 1) * SHARD, (n + 2) * SHARD)
        project[n] = a[at, :].astype(f32) + b[at, :].astype(f32)


def swap(values, axis, size, bit):
    pairs = [(i, i ^ bit) for i in range(size)]
    return jax.tree.map(lambda v: lax.ppermute(v, axis, pairs), values)


def after(values, *others):
    return lax.optimization_barrier((values, others))[0]


class LineSum:
    def __init__(self, parts, finishes):
        place = lax.axis_index("tensor")
        self.flag = ((place == 1) | (place == 2)).astype(jnp.int32)[None]
        self.parts, self.finishes = parts, finishes
        self.first = [lax.ppermute(part, "tensor", [(0, 1), (3, 2)]) for part in parts]
        self.sums, self.second, self.finals, self.third = {}, {}, {}, {}

    def add(self, i, mark):
        part, got = self.parts[i], after(self.first[i], mark)
        self.sums[i] = add_extra(part, got) if part.shape[0] % 128 else add(part, got)
        self.second[i] = lax.ppermute(self.sums[i], "tensor", [(1, 2), (2, 1)])
        return self.sums[i]

    def end(self, i, mark):
        self.finals[i] = self.finishes[i](self.sums[i], after(self.second[i], mark))
        self.third[i] = lax.ppermute(self.finals[i], "tensor", [(1, 0), (2, 3)])
        return self.finals[i]

    def arrive(self, i, mark):
        self.third[i] = after(self.third[i], mark)
        return self.third[i]

    def result(self, indices, mark, **place):
        theirs = after([self.third[i] for i in indices], mark)
        sizes = tuple(self.finals[i].shape[0] // 128 * 128 for i in indices)
        return choose(self.flag, [self.finals[i] for i in indices], theirs, sizes, **place)

    def decode(self, mark):
        self.third[0] = after(self.third[0], mark)
        return decode(self.flag, self.finals[0], self.third[0])


def rotation_tables(positions):
    lane = jnp.arange(PAIR, dtype=jnp.int32) % HD
    half = ROT // 2
    frequency = jnp.exp(
        -jnp.log(10000.0) * (lane % half).astype(f32) * 2.0 / ROT
    )
    angle = positions.astype(f32)[:, None] * frequency[None, :]
    rotated = lane < ROT
    return jnp.where(rotated, jnp.cos(angle), 1.0), jnp.where(rotated, jnp.sin(angle), 0.0)


def body(
    contexts,
    tokens,
    cotangent,
    segments,
    positions,
    parents,
    block_lists,
    project_weight,
    project_bias,
    dense_weight,
    dense_bias,
    up_weight,
    up_bias,
    down_weight,
    down_bias,
    first_gain,
    first_shift,
    second_gain,
    second_shift,
):
    rows, width = tokens.shape
    blocks = rows // BLK
    maxk = block_lists.shape[1]
    me = lax.axis_index("fsdp")
    place = lax.axis_index("context")
    order = jnp.stack([me, me ^ 1, me ^ 2, me ^ 3]).astype(jnp.int32)
    send_order = jnp.stack([me ^ 1, me ^ 3, me, me ^ 2]).astype(jnp.int32)
    split = contexts == 2
    slots = contexts * blocks
    first_slot = place * blocks
    if split:
        lists = jnp.where(block_lists >= 0, (block_lists - first_slot) % slots, -1)
        base = jnp.zeros((), jnp.int32)
    else:
        lists, base = block_lists, first_slot
    ids = jnp.concatenate(
        [jnp.stack([base, base]).astype(jnp.int32), lists.reshape(-1).astype(jnp.int32)]
    )

    blocks_of = lambda w: w.reshape(SHARD, -1, SHARD).transpose(1, 0, 2).reshape(-1, SHARD)
    units = up_bias.shape[0]
    wp = blocks_of(project_weight)
    wp1, wp2 = swap(wp, "fsdp", 4, 1), swap(wp, "fsdp", 4, 2)
    wr = jnp.concatenate([down_weight, blocks_of(up_weight), dense_weight], axis=0)
    wr = after(wr, wp)
    wr1, wr2 = swap(wr, "fsdp", 4, 1), swap(wr, "fsdp", 4, 2)

    tables = rotation_tables(positions)
    wp2 = after(wp2, tables, ids, send_order)
    wp3 = swap(wp2, "fsdp", 4, 1)
    projects = (wp, wp1, wp2, wp3)
    q0, q1, kv0, kv1, normed_one = project(
        order, tokens, first_gain[None], first_shift[None], projects, project_bias, tables
    )
    if split:
        other0, other1 = swap(kv0, "context", 2, 1), swap(kv1, "context", 2, 1)
        keys = ((kv0, other0), (kv1, other1))
        state0 = attend_forward(ids, maxk, q0, kv0, 0, None, False)
        state1 = attend_forward(ids, maxk, after(q1, state0), kv1, 0, None, False)
        o0, lse0 = attend_forward(
            ids, maxk, after(q0, state1), other0, blocks, state0, True
        )
        wr2 = after(wr2, o0)
        wr3 = swap(wr2, "fsdp", 4, 1)
        o1, lse1 = attend_forward(
            ids, maxk, after(q1, o0), other1, blocks, state1, True, 10
        )
    else:
        keys = [(lax.all_gather(kv, "context", axis=0, tiled=True),) for kv in (kv0, kv1)]
        wr3 = swap(wr2, "fsdp", 4, 1)
        o0, lse0 = attend_forward(ids, maxk, q0, keys[0][0], 0, None, True)
        o1, lse1 = attend_forward(ids, maxk, q1, keys[1][0], 0, None, True)

    made = mlp_forward(
        order, tokens, cotangent, second_gain[None], second_shift[None], up_bias[None],
        (wr, wr1, wr2, wr3), o0, o1,
    )
    normed_two, activated, slope, context_low, g0, g1 = made[2:]
    half = rows // 2

    out = LineSum(
        made[:2],
        [
            partial(
                finish, finish_out_kernel, "finish_out", start, half, 1,
                (tokens, dense_bias[None], down_bias[None]),
            )
            for start in (0, half)
        ],
    )
    back0 = attend_backward(ids, maxk, q0, g0, o0, lse0, tables, keys[0])
    back1 = attend_backward(ids, maxk, q1, after(g1, back0), o1, lse1, tables, keys[1])
    if split:
        grads = []
        for own, other, _ in (back0, back1):
            grads += [own, swap(other, "context", 2, 1)]
    else:
        grads = [
            lax.psum_scatter(whole_grad, "context", scatter_dimension=0, tiled=True)
            for whole_grad, _ in (back0, back1)
        ]
    mark = out.add(0, (back1, grads[1]) if split else back1)
    hidden_grad, e2, sums = mlp_backward(
        order, tokens, after(cotangent, mark),
        second_gain[None], slope, (wr, wr1, wr2, wr3),
    )
    made = input_grad(
        order, tokens, e2, first_gain[None], sums, (back0[-1], back1[-1]),
        tables, projects, grads, split,
    )
    projected_grad, sums = made[2:]
    line = LineSum(
        made[:2],
        [
            partial(
                finish, partial(finish_in_kernel, half), "finish_in", start, half, 2,
                (tokens, cotangent),
            )
            for start in (0, half)
        ],
    )
    mark = out.add(1, made[0])
    mlp_keep, *mlp_send = weight_parts(
        mlp_weights_kernel, "mlp_weights", send_order, 2 * units,
        activated, cotangent, normed_two, after(hidden_grad, mark),
    )
    mlp_got = swap(mlp_send, "fsdp", 4, 1)
    mark = out.end(0, mlp_keep)
    rest_keep, *rest_send = weight_parts(
        rest_weights_kernel, "rest_weights", send_order, 4 * SHARD,
        context_low, cotangent, normed_one, after(projected_grad, mark),
    )
    rest_got = swap(rest_send, "fsdp", 4, 1)
    mark = line.add(0, rest_keep)
    mark = out.end(1, mark)
    mark = out.arrive(0, mark)
    mlp_here, mlp_there = halves(mlp_keep, after(mlp_got, mark))
    mlp_got = swap(mlp_there, "fsdp", 4, 2)
    rest_here, rest_there = halves(rest_keep, after(rest_got, mlp_here))
    rest_got = swap(rest_there, "fsdp", 4, 2)
    mark = out.arrive(1, rest_here)
    mark = line.add(1, mark)
    mark = line.end(0, mark)
    mlp_part = add(mlp_here, after(mlp_got, mark))
    if split:
        mlp_got = swap(mlp_part, "context", 2, 1)
    rest_part = add(rest_here, after(rest_got, mlp_part))
    if split:
        rest_got = swap(rest_part, "context", 2, 1)
    mark = line.end(1, rest_part)
    norms = line.decode(mark)
    sums = jnp.concatenate([norms[0:2], sums[2:4], norms[2:4], sums[6:8]], axis=0)
    mark = sums
    for step in [("fsdp", 4, 1), ("fsdp", 4, 2)]:
        sums = mark = add(sums, swap(after(sums, mark), *step), f32)
    hop = swap(sums, "context", contexts, 1)
    layer_out = mark = out.result([0, 1], mark)
    tokens_grad = mark = line.result([0], mark, total=rows)
    if split:
        down_grad, up_grad = call(
            mlp_last_kernel, "mlp_last", (mlp_part, after(mlp_got, mark)),
            [((units, SHARD), f32), ((SHARD, units), f32)],
        )
        dense_grad, project_grad = call(
            rest_last_kernel, "rest_last", (rest_part, after(rest_got, down_grad)),
            [((SHARD, SHARD), f32), ((3, SHARD, SHARD), f32)],
        )
        mark = dense_grad
        project_grad = project_grad.transpose(1, 0, 2)
    else:
        mlp_part, rest_part = lax.psum(
            (mlp_part.astype(f32), rest_part.astype(f32)), "context"
        )
        back_blocks = lambda g: g.reshape(-1, SHARD, SHARD).transpose(1, 0, 2)
        down_grad = mlp_part[:units]
        up_grad = back_blocks(mlp_part[units:]).reshape(SHARD, units)
        dense_grad = rest_part[:SHARD]
        project_grad = back_blocks(rest_part[SHARD:])
    sums = mark = add(sums, after(hop, mark), f32)
    for i in range(1, contexts.bit_length() - 1):
        sums = mark = add(sums, swap(after(sums, mark), "context", contexts, 1 << i), f32)
    tokens_grad = line.result([1], mark, start=half, total=rows, before=tokens_grad)
    norms = sums
    up_total, bias_sum = sums[2], sums[3]
    project_total = sums[6, : project_bias.size]
    return (
        layer_out,
        tokens_grad,
        project_grad,
        project_total.reshape(3, -1),
        dense_grad,
        bias_sum,
        up_grad,
        up_total,
        down_grad,
        bias_sum,
        norms[4],
        norms[5],
        norms[0],
        norms[1],
    )


def solution(mesh):
    tokens = P(("fsdp", "context"), None)
    line = P(("fsdp", "context"))
    in_specs = (
        tokens, tokens, line, line, P("fsdp", None), tokens,
        P("fsdp", None, "tensor"), P(None, "tensor"), P("tensor", "fsdp"), P(),
        P("fsdp", "tensor"), P("tensor"), P("tensor", "fsdp"), P(), P(), P(), P(), P(),
    )
    out_specs = (
        tokens, tokens, P("fsdp", None, "tensor"), P(None, "tensor"), P("tensor", "fsdp"), P(),
        P("fsdp", "tensor"), P("tensor"), P("tensor", "fsdp"), P(), P(), P(), P(), P(),
    )
    run = partial(body, mesh.shape["context"])
    return jax.shard_map(run, mesh=mesh, in_specs=in_specs, out_specs=out_specs, check_vma=False)
```

profile of v0, /device:TPU:0, one launch (start us, length us, event | category | flops | bytes accessed | tf_op | source)
XLA Modules:
  0.0 226.1 jit_solution(3520337269642851461)
XLA Ops:
  0.7 3.0 %collective-permute-start.3 = (bf16[768,256]{1,0:T(8,128)(2,1)}, bf16[768,256]{1,0:T(8,128)(2,1)S(1)}, u32[]{:S(2)}, u32[]{:S(2)}) collective-permute-start(bf16[768,256]{1,0:T(8,128)(2,1)} %bitcast.29), channel_id=1, source_target_pairs={{0,16},{8,24},{16,0},{24,8},{1,17},{9,25},{17,1},{25,9},{2,18},{10... | collective-permute-start | bytes 1179656 | tf_op jit(solution)/shard_map/ppermute | solution.py:716
  6.6 1.9 fusion.1
  8.5 4.5 %collective-permute-done.3.w2 = bf16[768,256]{1,0:T(8,128)(2,1)S(1)} collective-permute-done((bf16[768,256]{1,0:T(8,128)(2,1)}, bf16[768,256]{1,0:T(8,128)(2,1)S(1)}, u32[]{:S(2)}, u32[]{:S(2)}) %collective-permute-start.3) | collective-permute-done | bytes 393248 | tf_op jit(solution)/shard_map/ppermute | solution.py:716
  13.1 1.8 collective-permute-start.1
  15.0 5.5 %project.1 = (bf16[1024,128]{1,0:T(8,128)(2,1)S(1)}, bf16[1024,128]{1,0:T(8,128)(2,1)S(1)}, bf16[1024,256]{1,0:T(8,128)(2,1)S(1)}, bf16[1024,256]{1,0:T(8,128)(2,1)S(1)}, bf16[1024,1024]{1,0:T(8,128)(2,1)S(1)}) custom-call(s32[4]{0:T(128)S(1)} %pad_add_fusion.ids, bf16[1024,1024]{1,0:T(8,128)(2,1)S(1)} %copy-done, f32[1,1024]{1,0:T(1,128)S(1)} %bitcast.41, ...), custom_call_target="tpu_custom_call" | custom-call | flops 4944999936 | bytes 15910000 | tf_op jit(solution)/shard_map/project/pallas_call | solution.py:97
  22.7 4.2 %attend_forward.4 = (f32[16,512]{1,0:T(8,128)S(1)}, f32[256,512]{1,0:T(8,128)S(1)}) custom-call(s32[8]{0:T(128)S(1)} %concatenate.10.ids, bf16[1024,128]{1,0:T(8,128)(2,1)S(1)} %get-tuple-element.109.q, bf16[1024,256]{1,0:T(8,128)(2,1)S(1)} %get-tuple-element.102.kv.refs_0_), custom_call_target="tpu_custom_call" | custom-call | tf_op jit(solution)/shard_map/attend_forward/pallas_call | solution.py:203
  26.8 4.2 %attend_forward.5 = (f32[16,512]{1,0:T(8,128)S(1)}, f32[256,512]{1,0:T(8,128)S(1)}) custom-call(s32[8]{0:T(128)S(1)} %concatenate.10.ids, bf16[1024,128]{1,0:T(8,128)(2,1)S(1)} %get-tuple-element.112.q, bf16[1024,256]{1,0:T(8,128)(2,1)S(1)} %get-tuple-element.106.kv.refs_0_), custom_call_target="tpu_custom_call" | custom-call | tf_op jit(solution)/shard_map/attend_forward/pallas_call | solution.py:203
  31.0 4.4 %collective-permute-done.5.kv.refs_1_ = bf16[1024,256]{1,0:T(8,128)(2,1)S(1)} collective-permute-done((bf16[1024,256]{1,0:T(8,128)(2,1)S(1)}, bf16[1024,256]{1,0:T(8,128)(2,1)S(1)}, u32[]{:S(2)}, u32[]{:S(2)}) %collective-permute-start.5) | collective-permute-done | bytes 524320 | tf_op jit(solution)/shard_map/ppermute | solution.py:716
  35.4 3.7 %attend_forward.6 = (f32[1024,128]{1,0:T(8,128)S(1)}, f32[8,512]{1,0:T(8,128)S(1)}) custom-call(s32[8]{0:T(128)S(1)} %concatenate.10.ids, bf16[1024,128]{1,0:T(8,128)(2,1)S(1)} %get-tuple-element.109.q, bf16[1024,256]{1,0:T(8,128)(2,1)S(1)} %collective-permute-done.5.kv.refs_1_, f32[16,512]{1,0:T(8,128)S(1)} %get-tuple-element.103.refs_0_, ...), custom_call_target="tpu_custom_call" | custom-call | tf_op jit(solution)/shard_map/attend_forward/pallas_call | solution.py:203
  39.1 2.4 %collective-permute-done.1.p2 = bf16[2304,256]{1,0:T(8,128)(2,1)S(1)} collective-permute-done((bf16[2304,256]{1,0:T(8,128)(2,1)S(1)}, bf16[2304,256]{1,0:T(8,128)(2,1)S(1)}, u32[]{:S(2)}, u32[]{:S(2)}) %collective-permute-start.1) | collective-permute-done | bytes 1179680 | tf_op jit(solution)/shard_map/ppermute | solution.py:716
  41.6 4.3 %collective-permute-done.7.kv.refs_1_ = bf16[1024,256]{1,0:T(8,128)(2,1)S(1)} collective-permute-done((bf16[1024,256]{1,0:T(8,128)(2,1)S(1)}, bf16[1024,256]{1,0:T(8,128)(2,1)S(1)}, u32[]{:S(2)}, u32[]{:S(2)}) %collective-permute-start.7) | collective-permute-done | bytes 524320 | tf_op jit(solution)/shard_map/ppermute | solution.py:716
  45.9 4.0 %attend_forward.7 = (f32[1024,128]{1,0:T(8,128)S(1)}, f32[8,512]{1,0:T(8,128)S(1)}) custom-call(s32[8]{0:T(128)S(1)} %concatenate.10.ids, bf16[1024,128]{1,0:T(8,128)(2,1)S(1)} %get-tuple-element.112.q, bf16[1024,256]{1,0:T(8,128)(2,1)S(1)} %collective-permute-done.7.kv.refs_1_, f32[16,512]{1,0:T(8,128)S(1)} %get-tuple-element.107.refs_0_, ...), custom_call_target="tpu_custom_call" | custom-call | flops 11500000256 | bytes 37000000 | tf_op jit(solution)/shard_map/attend_forward/pallas_call | solution.py:203
  50.0 9.9 %mlp_forward.1 = (bf16[512,1024]{1,0:T(8,128)(2,1)S(1)}, bf16[512,1024]{1,0:T(8,128)(2,1)S(1)}, bf16[1024,1024]{1,0:T(8,128)(2,1)S(1)}, bf16[1024,1024]{1,0:T(8,...) custom-call(s32[4]{0:T(128)S(1)} %pad_add_fusion.ids, ...), custom_call_target="tpu_custom_call" | custom-call | flops 1150000000 | bytes 3700000 | tf_op jit(solution)/shard_map/mlp_forward/pallas_call | solution.py:377
  59.9 3.6 %collective-permute-start.8 = (bf16[512,1024]{1,0:T(8,128)(2,1)S(1)}, bf16[512,1024]{1,0:T(8,128)(2,1)S(1)}, u32[]{:S(2)}, u32[]{:S(2)}) collective-permute-start(bf16[512,1024]{1,0:T(8,128)(2,1)S(1)} %get-tuple-element.114.a), channel_id=1, source_target_pairs={{0,1},{3,2},{4,5},{7,6},{8,9},{11,10},{12,13},{15,14},{16,17},{19,... | collective-permute-start | bytes 3145736 | tf_op jit(solution)/shard_map/ppermute | solution.py:728
  63.4 9.4 %attend_backward.2 = (bf16[1024,256]{1,0:T(8,128)(2,1)S(1)}, bf16[1024,256]{1,0:T(8,128)(2,1)S(1)}, bf16[1024,128]{1,0:T(8,128)(2,1)S(1)}) custom-call(s32[8]{0:T(128)S(1)} %concatenate.10.ids, bf16[1024,128]{1,0:T(8,128)(2,1)S(1)} %get-tuple-element.109.q, bf16[1024,128]{1,0:T(8,128)(2,1)S(1)} %get-tuple-element.116.g, ...), custom_call_target="tpu_custom_call" | custom-call | tf_op jit(solution)/shard_map/attend_backward/pallas_call | solution.py:300
  74.3 9.8 %attend_backward.3 = (bf16[1024,256]{1,0:T(8,128)(2,1)S(1)}, bf16[1024,256]{1,0:T(8,128)(2,1)S(1)}, bf16[1024,128]{1,0:T(8,128)(2,1)S(1)}) custom-call(s32[8]{0:T(128)S(1)} %concatenate.10.ids, bf16[1024,128]{1,0:T(8,128)(2,1)S(1)} %get-tuple-element.112.q, bf16[1024,128]{1,0:T(8,128)(2,1)S(1)} %get-tuple-element.121.g, ...), custom_call_target="tpu_custom_call" | custom-call | tf_op jit(solution)/shard_map/attend_backward/pallas_call | solution.py:300
  88.0 7.8 %mlp_backward.1 = (bf16[1024,1024]{1,0:T(8,128)(2,1)S(1)}, bf16[1024,1024]{1,0:T(8,128)(2,1)S(1)}, f32[8,1024]{1,0:T(8,128)S(1)}) custom-call(s32[4]{0:T(128)S(1)} %pad_add_fusion.ids, bf16[1024,1024]{1,0:T(8,128)(2,1)S(1)} %copy-done, bf16[1024,1024]{1,0:T(8,128)(2,1)S(1)} %copy-done.1, f32[1,1024]{1,0:T(1,128)S(1)} %bitcast.34, ...), custom_call_target="tpu_custom_call" | custom-call | flops 1150000000 | bytes 3700000 | tf_op jit(solution)/shard_map/mlp_backward/pallas_call | solution.py:427
  97.1 6.1 %input_grad.1 = (bf16[528,1024]{1,0:T(8,128)(2,1)S(1)}, bf16[512,1024]{1,0:T(8,128)(2,1)S(1)}, bf16[1024,768]{1,0:T(8,128)(2,1)S(1)}, f32[8,1024]{1,0:T(8,128)S(1)}) custom-call(s32[4]{0:T(128)S(1)} %pad_add_fusion.ids, bf16[1024,1024]{1,0:T(8,128)(2,1)S(1)} %copy-done, bf16[1024,1024]{1,0:T(8,128)(2,1)S(1)} %get-tuple-element.133.e2, ...), custom_call_target="tpu_custom_call" | custom-call | tf_op jit(solution)/shard_map/input_grad/pallas_call | solution.py:549
  103.2 5.9 %collective-permute-start.14 = (bf16[528,1024]{1,0:T(8,128)(2,1)S(1)}, bf16[528,1024]{1,0:T(8,128)(2,1)S(1)}, u32[]{:S(2)}, u32[]{:S(2)}) collective-permute-start(bf16[528,1024]{1,0:T(8,128)(2,1)S(1)} %get-tuple-element.135.a), channel_id=1, source_target_pairs={{0,1},{3,2},{4,5},{7,6},{8,9},{11,10},{12,13},{15,14},{16,17},{19,... | collective-permute-start | bytes 3244040 | tf_op jit(solution)/shard_map/ppermute | solution.py:728
  110.4 6.3 %mlp_weights.1 = (bf16[2,2048,256]{2,1,0:T(8,128)(2,1)S(1)}, bf16[1,2048,256]{2,1,0:T(8,128)(2,1)S(1)}, bf16[1,2048,256]{2,1,0:T(8,128)(2,1)S(1)}) custom-call(s32[4]{0:T(128)S(1)} %pad_add_fusion.1.ids, bf16[1024,1024]{1,0:T(8,128)(2,1)S(1)} %get-tuple-element.127.act, bf16[1024,1024]{1,0:T(8,128)(2,1)S(1)} %copy-done.1, ...), custom_call_target="tpu_custom_call" | custom-call | tf_op jit(solution)/shard_map/mlp_weights/pallas_call | solution.py:480
  119.1 3.7 %rest_weights.1 = (bf16[2,1024,256]{2,1,0:T(8,128)(2,1)S(1)}, bf16[1,1024,256]{2,1,0:T(8,128)(2,1)S(1)}, bf16[1,1024,256]{2,1,0:T(8,128)(2,1)S(1)}) custom-call(s32[4]{0:T(128)S(1)} %pad_add_fusion.1.ids, bf16[1024,256]{1,0:T(8,128)(2,1)S(1)} %get-tuple-element.140.ctx, bf16[1024,1024]{1,0:T(8,128)(2,1)S(1)} %copy-done.1, ...), custom_call_target="tpu_custom_call" | custom-call | tf_op jit(solution)/shard_map/rest_weights/pallas_call | solution.py:480
  122.8 8.1 %collective-permute-done.14.b = bf16[528,1024]{1,0:T(8,128)(2,1)S(1)} collective-permute-done((bf16[528,1024]{1,0:T(8,128)(2,1)S(1)}, bf16[528,1024]{1,0:T(8,128)(2,1)S(1)}, u32[]{:S(2)}, u32[]{:S(2)}) %collective-permute-start.14) | collective-permute-done | bytes 1081376 | tf_op jit(solution)/shard_map/ppermute | solution.py:728
  133.0 6.8 %collective-permute-start.22 = (bf16[512,1024]{1,0:T(8,128)(2,1)S(1)}, bf16[512,1024]{1,0:T(8,128)(2,1)S(1)}, u32[]{:S(2)}, u32[]{:S(2)}) collective-permute-start(bf16[512,1024]{1,0:T(8,128)(2,1)S(1)} %get-tuple-element.159.a), channel_id=1, source_target_pairs={{0,1},{3,2},{4,5},{7,6},{8,9},{11,10},{12,13},{15,14},{16,17},{19,... | collective-permute-start | bytes 3145736 | tf_op jit(solution)/shard_map/ppermute | solution.py:728
  140.6 7.6 %collective-permute-done.15.refs_2_ = bf16[512,1024]{1,0:T(8,128)(2,1)S(1)} collective-permute-done((bf16[512,1024]{1,0:T(8,128)(2,1)S(1)}, bf16[512,1024]{1,0:T(8,128)(2,1)S(1)}, u32[]{:S(2)}, u32[]{:S(2)}) %collective-permute-start.15) | collective-permute-done | bytes 1048608 | tf_op jit(solution)/shard_map/ppermute | solution.py:739
  151.0 19.2 %collective-permute-done.16.refs_3_ = bf16[512,1024]{1,0:T(8,128)(2,1)S(1)} collective-permute-done((bf16[512,1024]{1,0:T(8,128)(2,1)S(1)}, bf16[512,1024]{1,0:T(8,128)(2,1)S(1)}, u32[]{:S(2)}, u32[]{:S(2)}) %collective-permute-start.16) | collective-permute-done | bytes 1048608 | tf_op jit(solution)/shard_map/ppermute | solution.py:739
  176.9 10.6 %collective-permute-done.25.b = bf16[1024,256]{1,0:T(8,128)(2,1)S(1)} collective-permute-done((bf16[1024,256]{1,0:T(8,128)(2,1)S(1)}, bf16[1024,256]{1,0:T(8,128)(2,1)S(1)}, u32[]{:S(2)}, u32[]{:S(2)}) %collective-permute-start.25) | collective-permute-done | bytes 524320 | tf_op jit(solution)/shard_map/ppermute | solution.py:716
  187.6 2.5 %finish_in.3.refs_0_ = bf16[512,1024]{1,0:T(8,128)(2,1)} custom-call(bf16[512,1024]{1,0:T(8,128)(2,1)S(1)} %add.71.a, bf16[512,1024]{1,0:T(8,128)(2,1)S(1)} %collective-permute-done.24.b, bf16[1024,1024]{1,0:T(8,128)(2,1)S(1)} %copy-done, bf16[1024,1024]{1,0:T(8,128)(2,1)S(1)} %copy-done.1), custom_call_target="tpu_custom_call" | custom-call | tf_op jit(solution)/shard_map/finish_in/pallas_call | solution.py:571
  191.8 8.2 %collective-permute-done.23.theirs.refs_1_ = bf16[528,1024]{1,0:T(8,128)(2,1)S(1)} collective-permute-done((bf16[528,1024]{1,0:T(8,128)(2,1)S(1)}, bf16[528,1024]{1,0:T(8,128)(2,1)S(1)}, u32[]{:S(2)}, u32[]{:S(2)}) %collective-permute-start.23) | collective-permute-done | bytes 1081376 | tf_op jit(solution)/shard_map/ppermute | solution.py:739
  202.7 2.5 %collective-permute-done.28.b = f32[8,1024]{1,0:T(8,128)S(1)} collective-permute-done((f32[8,1024]{1,0:T(8,128)S(1)}, f32[8,1024]{1,0:T(8,128)S(1)}, u32[]{:S(2)}, u32[]{:S(2)}) %collective-permute-start.28) | collective-permute-done | bytes 32800 | tf_op jit(solution)/shard_map/ppermute | solution.py:716
  209.2 3.0 %mlp_last.1 = (f32[1024,256]{1,0:T(8,128)}, f32[256,1024]{1,0:T(8,128)}) custom-call(bf16[2048,256]{1,0:T(8,128)(2,1)} %add.72.a, bf16[2048,256]{1,0:T(8,128)(2,1)} %collective-permute-done.32.b), custom_call_target="tpu_custom_call" | custom-call | tf_op jit(solution)/shard_map/mlp_last/pallas_call | solution.py:571
  215.2 7.5 %collective-permute-done.29.refs_1_ = bf16[512,1024]{1,0:T(8,128)(2,1)} collective-permute-done((bf16[512,1024]{1,0:T(8,128)(2,1)}, bf16[512,1024]{1,0:T(8,128)(2,1)}, u32[]{:S(2)}, u32[]{:S(2)}) %collective-permute-start.29) | collective-permute-done | bytes 1048608 | tf_op jit(solution)/shard_map/ppermute | solution.py:739
  222.7 2.6 %choose.5 = bf16[1024,1024]{1,0:T(8,128)(2,1)} custom-call(s32[1]{0:T(128)} %bitcast.flag, bf16[512,1024]{1,0:T(8,128)(2,1)} %finish_in.3.refs_0_, bf16[512,1024]{1,0:T(8,128)(2,1)} %collective-permute-done.29.refs_1_, bf16[1024,1024]{1,0:T(8,128)(2,1)} %choose.4.refs_2_), custom_call_target="tpu_custom_call", output_to_operand_aliasing={{}: (3, {})} | custom-call | tf_op jit(solution)/shard_map/choose/pallas_call | solution.py:571
  (129 shorter events, 39.6 us)
Async XLA Ops:
  0.7 12.3 %collective-permute-start.3 = (bf16[768,256]{1,0:T(8,128)(2,1)}, bf16[768,256]{1,0:T(8,128)(2,1)S(1)}, u32[]{:S(2)}, u32[]{:S(2)}) collective-permute-start(bf16[768,256]{1,0:T(8,128)(2,1)} %bitcast.29), channel_id=1, source_target_pairs={{0,16},{8,24},{16,0},{24,8},{1,17},{9,25},{17,1},{25,9},{2,18},{10... | collective-permute-start | bytes 1179656 | tf_op jit(solution)/shard_map/ppermute | solution.py:716
  3.7 11.3 %collective-permute-start.2 = (bf16[768,256]{1,0:T(8,128)(2,1)}, bf16[768,256]{1,0:T(8,128)(2,1)S(1)}, u32[]{:S(2)}, u32[]{:S(2)}) collective-permute-start(bf16[768,256]{1,0:T(8,128)(2,1)} %bitcast.30), channel_id=1, source_target_pairs={{0,8},{8,0},{16,24},{24,16},{1,9},{9,1},{17,25},{25,17},{2,10},{10... | collective-permute-start | bytes 1179656 | tf_op jit(solution)/shard_map/ppermute | solution.py:716
  13.0 2.0 collective-permute-start.4
  13.1 28.4 %collective-permute-start.1 = (bf16[2304,256]{1,0:T(8,128)(2,1)S(1)}, bf16[2304,256]{1,0:T(8,128)(2,1)S(1)}, u32[]{:S(2)}, u32[]{:S(2)}) collective-permute-start(bf16[2304,256]{1,0:T(8,128)(2,1)S(1)} %pad_maximum_fusion.p0), channel_id=1, source_target_pairs={{0,16},{8,24},{16,0},{24,8},{1,17},{9,25},{17,1},{25,9},{2,18},{10... | collective-permute-start | bytes 3538952 | tf_op jit(solution)/shard_map/ppermute | solution.py:716
  20.6 14.8 %collective-permute-start.5 = (bf16[1024,256]{1,0:T(8,128)(2,1)S(1)}, bf16[1024,256]{1,0:T(8,128)(2,1)S(1)}, u32[]{:S(2)}, u32[]{:S(2)}) collective-permute-start(bf16[1024,256]{1,0:T(8,128)(2,1)S(1)} %get-tuple-element.102.kv.refs_0_), channel_id=1, source_target_pairs={{0,4},{4,0},{1,5},{5,1},{2,6},{6,2},{3,7},{7,3},{8,12},{12,8},{9,1... | collective-permute-start | bytes 1572872 | tf_op jit(solution)/shard_map/ppermute | solution.py:716
  22.2 23.8 %collective-permute-start.7 = (bf16[1024,256]{1,0:T(8,128)(2,1)S(1)}, bf16[1024,256]{1,0:T(8,128)(2,1)S(1)}, u32[]{:S(2)}, u32[]{:S(2)}) collective-permute-start(bf16[1024,256]{1,0:T(8,128)(2,1)S(1)} %get-tuple-element.106.kv.refs_0_), channel_id=1, source_target_pairs={{0,4},{4,0},{1,5},{5,1},{2,6},{6,2},{3,7},{7,3},{8,12},{12,8},{9,1... | collective-permute-start | bytes 1572872 | tf_op jit(solution)/shard_map/ppermute | solution.py:716
  22.7 27.3 %collective-permute-start = (bf16[2304,256]{1,0:T(8,128)(2,1)S(1)}, bf16[2304,256]{1,0:T(8,128)(2,1)S(1)}, u32[]{:S(2)}, u32[]{:S(2)}) collective-permute-start(bf16[2304,256]{1,0:T(8,128)(2,1)S(1)} %pad_maximum_fusion.p0), channel_id=1, source_target_pairs={{0,8},{8,0},{16,24},{24,16},{1,9},{9,1},{17,25},{25,17},{2,10},{10... | collective-permute-start | bytes 3538952 | tf_op jit(solution)/shard_map/ppermute | solution.py:716
  41.5 8.4 %collective-permute-start.6 = (bf16[2304,256]{1,0:T(8,128)(2,1)S(1)}, bf16[2304,256]{1,0:T(8,128)(2,1)S(1)}, u32[]{:S(2)}, u32[]{:S(2)}) collective-permute-start(bf16[2304,256]{1,0:T(8,128)(2,1)S(1)} %collective-permute-done.1.p2), channel_id=1, source_target_pairs={{0,8},{8,0},{16,24},{24,16},{1,9},{9,1},{17,25},{25,17},{2,10},{10... | collective-permute-start | bytes 3538952 | tf_op jit(solution)/shard_map/ppermute | solution.py:716
  59.9 27.1 %collective-permute-start.8 = (bf16[512,1024]{1,0:T(8,128)(2,1)S(1)}, bf16[512,1024]{1,0:T(8,128)(2,1)S(1)}, u32[]{:S(2)}, u32[]{:S(2)}) collective-permute-start(bf16[512,1024]{1,0:T(8,128)(2,1)S(1)} %get-tuple-element.114.a), channel_id=1, source_target_pairs={{0,1},{3,2},{4,5},{7,6},{8,9},{11,10},{12,13},{15,14},{16,17},{19,... | collective-permute-start | bytes 3145736 | tf_op jit(solution)/shard_map/ppermute | solution.py:728
  72.8 13.0 %collective-permute-start.9 = (bf16[1024,256]{1,0:T(8,128)(2,1)S(1)}, bf16[1024,256]{1,0:T(8,128)(2,1)S(1)}, u32[]{:S(2)}, u32[]{:S(2)}) collective-permute-start(bf16[1024,256]{1,0:T(8,128)(2,1)S(1)} %get-tuple-element.119), channel_id=1, source_target_pairs={{0,4},{4,0},{1,5},{5,1},{2,6},{6,2},{3,7},{7,3},{8,12},{12,8},{9,1... | collective-permute-start | bytes 1572872 | tf_op jit(solution)/shard_map/ppermute | solution.py:716
  72.9 36.5 %collective-permute-start.11 = (bf16[512,1024]{1,0:T(8,128)(2,1)S(1)}, bf16[512,1024]{1,0:T(8,128)(2,1)S(1)}, u32[]{:S(2)}, u32[]{:S(2)}) collective-permute-start(bf16[512,1024]{1,0:T(8,128)(2,1)S(1)} %get-tuple-element.132.a), channel_id=1, source_target_pairs={{0,1},{3,2},{4,5},{7,6},{8,9},{11,10},{12,13},{15,14},{16,17},{19,... | collective-permute-start | bytes 3145736 | tf_op jit(solution)/shard_map/ppermute | solution.py:728
  84.1 13.0 %collective-permute-start.12 = (bf16[1024,256]{1,0:T(8,128)(2,1)S(1)}, bf16[1024,256]{1,0:T(8,128)(2,1)S(1)}, u32[]{:S(2)}, u32[]{:S(2)}) collective-permute-start(bf16[1024,256]{1,0:T(8,128)(2,1)S(1)} %get-tuple-element.124), channel_id=1, source_target_pairs={{0,4},{4,0},{1,5},{5,1},{2,6},{6,2},{3,7},{7,3},{8,12},{12,8},{9,1... | collective-permute-start | bytes 1572872 | tf_op jit(solution)/shard_map/ppermute | solution.py:716
  87.2 30.1 %collective-permute-start.10 = (bf16[512,1024]{1,0:T(8,128)(2,1)S(1)}, bf16[512,1024]{1,0:T(8,128)(2,1)S(1)}, u32[]{:S(2)}, u32[]{:S(2)}) collective-permute-start(bf16[512,1024]{1,0:T(8,128)(2,1)S(1)} %add.69.a), channel_id=1, source_target_pairs={{1,2},{2,1},{5,6},{6,5},{9,10},{10,9},{13,14},{14,13},{17,18},{18,... | collective-permute-start | bytes 3145736 | tf_op jit(solution)/shard_map/ppermute | solution.py:734
  103.2 27.7 %collective-permute-start.14 = (bf16[528,1024]{1,0:T(8,128)(2,1)S(1)}, bf16[528,1024]{1,0:T(8,128)(2,1)S(1)}, u32[]{:S(2)}, u32[]{:S(2)}) collective-permute-start(bf16[528,1024]{1,0:T(8,128)(2,1)S(1)} %get-tuple-element.135.a), channel_id=1, source_target_pairs={{0,1},{3,2},{4,5},{7,6},{8,9},{11,10},{12,13},{15,14},{16,17},{19,... | collective-permute-start | bytes 3244040 | tf_op jit(solution)/shard_map/ppermute | solution.py:728
  109.7 21.5 %collective-permute-start.13 = (bf16[512,1024]{1,0:T(8,128)(2,1)S(1)}, bf16[512,1024]{1,0:T(8,128)(2,1)S(1)}, u32[]{:S(2)}, u32[]{:S(2)}) collective-permute-start(bf16[512,1024]{1,0:T(8,128)(2,1)S(1)} %add.70.a), channel_id=1, source_target_pairs={{1,2},{2,1},{5,6},{6,5},{9,10},{10,9},{13,14},{14,13},{17,18},{18,... | collective-permute-start | bytes 3145736 | tf_op jit(solution)/shard_map/ppermute | solution.py:734
  116.7 23.0 %collective-permute-start.19 = (bf16[1,2048,256]{2,1,0:T(8,128)(2,1)S(1)}, bf16[1,2048,256]{2,1,0:T(8,128)(2,1)S(1)}, u32[]{:S(2)}, u32[]{:S(2)}) collective-permute-start(bf16[1,2048,256]{2,1,0:T(8,128)(2,1)S(1)} %get-tuple-element.150), channel_id=1, source_target_pairs={{0,8},{8,0},{16,24},{24,16},{1,9},{9,1},{17,25},{25,17},{2,10},{10... | collective-permute-start | bytes 3145736 | tf_op jit(solution)/shard_map/ppermute | solution.py:716
  116.8 23.0 %collective-permute-start.20 = (bf16[1,2048,256]{2,1,0:T(8,128)(2,1)S(1)}, bf16[1,2048,256]{2,1,0:T(8,128)(2,1)S(1)}, u32[]{:S(2)}, u32[]{:S(2)}) collective-permute-start(bf16[1,2048,256]{2,1,0:T(8,128)(2,1)S(1)} %get-tuple-element.151), channel_id=1, source_target_pairs={{0,8},{8,0},{16,24},{24,16},{1,9},{9,1},{17,25},{25,17},{2,10},{10... | collective-permute-start | bytes 3145736 | tf_op jit(solution)/shard_map/ppermute | solution.py:716
  117.8 30.5 %collective-permute-start.15 = (bf16[512,1024]{1,0:T(8,128)(2,1)S(1)}, bf16[512,1024]{1,0:T(8,128)(2,1)S(1)}, u32[]{:S(2)}, u32[]{:S(2)}) collective-permute-start(bf16[512,1024]{1,0:T(8,128)(2,1)S(1)} %finish_out.2.refs_0_), channel_id=1, source_target_pairs={{1,0},{2,3},{5,4},{6,7},{9,8},{10,11},{13,12},{14,15},{17,16},{18,... | collective-permute-start | bytes 3145736 | tf_op jit(solution)/shard_map/ppermute | solution.py:739
  131.7 38.5 %collective-permute-start.16 = (bf16[512,1024]{1,0:T(8,128)(2,1)S(1)}, bf16[512,1024]{1,0:T(8,128)(2,1)S(1)}, u32[]{:S(2)}, u32[]{:S(2)}) collective-permute-start(bf16[512,1024]{1,0:T(8,128)(2,1)S(1)} %finish_out.3.refs_1_), channel_id=1, source_target_pairs={{1,0},{2,3},{5,4},{6,7},{9,8},{10,11},{13,12},{14,15},{17,16},{18,... | collective-permute-start | bytes 3145736 | tf_op jit(solution)/shard_map/ppermute | solution.py:739
  133.0 37.2 %collective-permute-start.22 = (bf16[512,1024]{1,0:T(8,128)(2,1)S(1)}, bf16[512,1024]{1,0:T(8,128)(2,1)S(1)}, u32[]{:S(2)}, u32[]{:S(2)}) collective-permute-start(bf16[512,1024]{1,0:T(8,128)(2,1)S(1)} %get-tuple-element.159.a), channel_id=1, source_target_pairs={{0,1},{3,2},{4,5},{7,6},{8,9},{11,10},{12,13},{15,14},{16,17},{19,... | collective-permute-start | bytes 3145736 | tf_op jit(solution)/shard_map/ppermute | solution.py:728
  139.8 9.5 %collective-permute-start.17 = (bf16[1,1024,256]{2,1,0:T(8,128)(2,1)S(1)}, bf16[1,1024,256]{2,1,0:T(8,128)(2,1)S(1)}, u32[]{:S(2)}, u32[]{:S(2)}) collective-permute-start(bf16[1,1024,256]{2,1,0:T(8,128)(2,1)S(1)} %get-tuple-element.148), channel_id=1, source_target_pairs={{0,8},{8,0},{16,24},{24,16},{1,9},{9,1},{17,25},{25,17},{2,10},{10... | collective-permute-start | bytes 1572872 | tf_op jit(solution)/shard_map/ppermute | solution.py:716
  139.9 31.3 %collective-permute-start.21 = (bf16[528,1024]{1,0:T(8,128)(2,1)S(1)}, bf16[528,1024]{1,0:T(8,128)(2,1)S(1)}, u32[]{:S(2)}, u32[]{:S(2)}) collective-permute-start(bf16[528,1024]{1,0:T(8,128)(2,1)S(1)} %add_extra.1.a), channel_id=1, source_target_pairs={{1,2},{2,1},{5,6},{6,5},{9,10},{10,9},{13,14},{14,13},{17,18},{18,... | collective-permute-start | bytes 3244040 | tf_op jit(solution)/shard_map/ppermute | solution.py:734
  148.2 2.4 %collective-permute-start.18 = (bf16[1,1024,256]{2,1,0:T(8,128)(2,1)S(1)}, bf16[1,1024,256]{2,1,0:T(8,128)(2,1)S(1)}, u32[]{:S(2)}, u32[]{:S(2)}) collective-permute-start(bf16[1,1024,256]{2,1,0:T(8,128)(2,1)S(1)} %get-tuple-element.149), channel_id=1, source_target_pairs={{0,8},{8,0},{16,24},{24,16},{1,9},{9,1},{17,25},{25,17},{2,10},{10... | collective-permute-start | bytes 1572872 | tf_op jit(solution)/shard_map/ppermute | solution.py:716
  149.2 26.3 %collective-permute-start.26 = (bf16[2048,256]{1,0:T(8,128)(2,1)S(1)}, bf16[2048,256]{1,0:T(8,128)(2,1)S(1)}, u32[]{:S(2)}, u32[]{:S(2)}) collective-permute-start(bf16[2048,256]{1,0:T(8,128)(2,1)S(1)} %get-tuple-element.163), channel_id=1, source_target_pairs={{0,16},{8,24},{16,0},{24,8},{1,17},{9,25},{17,1},{25,9},{2,18},{10... | collective-permute-start | bytes 3145736 | tf_op jit(solution)/shard_map/ppermute | solution.py:716
  170.4 17.2 %collective-permute-start.24 = (bf16[512,1024]{1,0:T(8,128)(2,1)S(1)}, bf16[512,1024]{1,0:T(8,128)(2,1)S(1)}, u32[]{:S(2)}, u32[]{:S(2)}) collective-permute-start(bf16[512,1024]{1,0:T(8,128)(2,1)S(1)} %add.71.a), channel_id=1, source_target_pairs={{1,2},{2,1},{5,6},{6,5},{9,10},{10,9},{13,14},{14,13},{17,18},{18,... | collective-permute-start | bytes 3145736 | tf_op jit(solution)/shard_map/ppermute | solution.py:734
  172.7 27.2 %collective-permute-start.23 = (bf16[528,1024]{1,0:T(8,128)(2,1)S(1)}, bf16[528,1024]{1,0:T(8,128)(2,1)S(1)}, u32[]{:S(2)}, u32[]{:S(2)}) collective-permute-start(bf16[528,1024]{1,0:T(8,128)(2,1)S(1)} %finish_in.2.ours.refs_0_), channel_id=1, source_target_pairs={{1,0},{2,3},{5,4},{6,7},{9,8},{10,11},{13,12},{14,15},{17,16},{18,... | collective-permute-start | bytes 3244040 | tf_op jit(solution)/shard_map/ppermute | solution.py:739
  174.0 13.4 %collective-permute-start.25 = (bf16[1024,256]{1,0:T(8,128)(2,1)S(1)}, bf16[1024,256]{1,0:T(8,128)(2,1)S(1)}, u32[]{:S(2)}, u32[]{:S(2)}) collective-permute-start(bf16[1024,256]{1,0:T(8,128)(2,1)S(1)} %get-tuple-element.162), channel_id=1, source_target_pairs={{0,16},{8,24},{16,0},{24,8},{1,17},{9,25},{17,1},{25,9},{2,18},{10... | collective-permute-start | bytes 1572872 | tf_op jit(solution)/shard_map/ppermute | solution.py:716
  176.8 32.4 %collective-permute-start.32 = (bf16[2048,256]{1,0:T(8,128)(2,1)}, bf16[2048,256]{1,0:T(8,128)(2,1)}, u32[]{:S(2)}, u32[]{:S(2)}) collective-permute-start(bf16[2048,256]{1,0:T(8,128)(2,1)} %add.72.a), channel_id=1, source_target_pairs={{0,4},{4,0},{1,5},{5,1},{2,6},{6,2},{3,7},{7,3},{8,12},{12,8},{9,1... | collective-permute-start | bytes 3145736 | tf_op jit(solution)/shard_map/ppermute | solution.py:716
  190.2 32.5 %collective-permute-start.29 = (bf16[512,1024]{1,0:T(8,128)(2,1)}, bf16[512,1024]{1,0:T(8,128)(2,1)}, u32[]{:S(2)}, u32[]{:S(2)}) collective-permute-start(bf16[512,1024]{1,0:T(8,128)(2,1)} %finish_in.3.refs_0_), channel_id=1, source_target_pairs={{1,0},{2,3},{5,4},{6,7},{9,8},{10,11},{13,12},{14,15},{17,16},{18,... | collective-permute-start | bytes 3145736 | tf_op jit(solution)/shard_map/ppermute | solution.py:739
  191.5 21.4 %collective-permute-start.31 = (bf16[1024,256]{1,0:T(8,128)(2,1)}, bf16[1024,256]{1,0:T(8,128)(2,1)S(1)}, u32[]{:S(2)}, u32[]{:S(2)}) collective-permute-start(bf16[1024,256]{1,0:T(8,128)(2,1)} %copy-done.4), channel_id=1, source_target_pairs={{0,4},{4,0},{1,5},{5,1},{2,6},{6,2},{3,7},{7,3},{8,12},{12,8},{9,1... | collective-permute-start | bytes 1572872 | tf_op jit(solution)/shard_map/ppermute | solution.py:716
  201.3 3.9 %collective-permute-start.28 = (f32[8,1024]{1,0:T(8,128)S(1)}, f32[8,1024]{1,0:T(8,128)S(1)}, u32[]{:S(2)}, u32[]{:S(2)}) collective-permute-start(f32[8,1024]{1,0:T(8,128)S(1)} %add.74.a), channel_id=1, source_target_pairs={{0,16},{8,24},{16,0},{24,8},{1,17},{9,25},{17,1},{25,9},{2,18},{10... | collective-permute-start | bytes 98312 | tf_op jit(solution)/shard_map/ppermute | solution.py:716
  205.2 8.8 %collective-permute-start.30 = (f32[8,1024]{1,0:T(8,128)S(1)}, f32[8,1024]{1,0:T(8,128)S(1)}, u32[]{:S(2)}, u32[]{:S(2)}) collective-permute-start(f32[8,1024]{1,0:T(8,128)S(1)} %add.75.a), channel_id=1, source_target_pairs={{0,4},{4,0},{1,5},{5,1},{2,6},{6,2},{3,7},{7,3},{8,12},{12,8},{9,1... | collective-permute-start | bytes 98312 | tf_op jit(solution)/shard_map/ppermute | solution.py:716
  (23 other events, 189.0 us)
where the time goes:
time: 229 us; the launch traced here: 226 us
  Pallas kernels  92.3 us (40%)
  waiting for transfers between devices  85.3 us (37%)
  starting transfers between devices  38.8 us (17%)
  local copies, waits for them, and re-layouts  4.74 us (2%)
  other arithmetic  3.56 us (2%)
    ppermute x4, waiting for transfers between devices, end(): self.third[i] = lax.ppermute(self.finals[i], 'tensor', [(1, 0), (2, 3)])  42.5 us
    ppermute x21, waiting for transfers between devices, swap(): return jax.tree.map(lambda v: lax.ppermute(v, axis, pairs), values)  33.3 us
    pallas_call x2, Pallas kernels, attend_backward(): pl.pallas_call(partial(attend_backward_kernel, slots, maxk, split), grid=...  19.2 us
    pallas_call x21, Pallas kernels, call(): pl.pallas_call(kernel, grid=(grid,), in_specs=in_specs or [whole(a.shape)...  17.7 us
    ppermute x4, starting transfers between devices, __init__(): lax.ppermute(part, 'tensor', [(0, 1), (3, 2)])  17.5 us
    pallas_call x4, Pallas kernels, attend_forward(): pl.pallas_call(partial(attend_forward_kernel, maxk, low, count, carried i...  16.1 us
    ppermute x21, starting transfers between devices, swap(): return jax.tree.map(lambda v: lax.ppermute(v, axis, pairs), values)  13.1 us
    pallas_call x2, Pallas kernels, weight_parts(): pl.pallas_call(kernel, grid=(4,), in_specs=[smem] + [whole(a.shape) for a...  10 us
  transfers between devices with their start and end apart: 33, of which 17 were waited for; matrix products, arithmetic and copies ran while one was open for 3% of the time, Pallas kernels for 35%

commit v1 on v0

--- a/solution.py
+++ b/solution.py
@@ -10,6 +10,7 @@
 HD = 64
 ROT = 16
 BLK = 512
+HALF = 256
 PAIR = 2 * HD
 SHARD = 256
 EXTRA = 16
@@ -67,131 +68,162 @@
     return pl.ds(pl.multiple_of(index * width, width), width)
 
 
-def project_kernel(
-    ids, x, gain, shift, w0, w1, w2, w3, bias, cos, sin, q0, q1, kv0, kv1, n1
-):
+def norm_kernel(x, gain, shift, out):
     normal, _ = norm_rows(x[...].astype(f32))
-    n1[...] = (normal * gain[...] + shift[...]).astype(bf16)
-    weights = (w0, w1, w2, w3)
-    width = w0.shape[1]
-    depth = w0.shape[0] // 3
-    outs = ((q0, q1), (kv0, kv1))
+    out[...] = (normal * gain[...] + shift[...]).astype(bf16)
+
+
+def norm(x, gain, shift, tile=256):
+    row = pl.BlockSpec((tile, x.shape[1]), lambda i: (i, 0))
+    return call(
+        norm_kernel, "norm", (x, gain, shift), (x.shape, bf16), x.shape[0] // tile,
+        [row, whole(gain.shape), whole(shift.shape)], [row],
+    )
+
+
+def project_kernel(ids, n1, w0, w1, w2, w3, bias, cos, sin, q0, q1, kv0, kv1, weight):
+    depth, width = w0.shape[0] // 3, w0.shape[1]
+
+    @pl.when(pl.program_id(0) == 0)
+    def _():
+        for i, piece in enumerate((w0, w1, w2, w3)):
+            for part in range(3):
+                weight[part, columns(ids[i], depth), :] = piece[
+                    part * depth : (part + 1) * depth, :
+                ]
+
     for part in range(3):
-        total = bias[part : part + 1, :] + jnp.zeros((n1.shape[0], width), f32)
-        for piece in range(4):
-            total += dot(n1[:, columns(ids[piece], depth)], weights[piece][part * depth : (part + 1) * depth, :], NN)
-        for pair in range(2):
+        total = dot(n1[...], weight[part], NN) + bias[part : part + 1, :]
+        for pair, (q, kv) in enumerate(((q0, kv0), (q1, kv1))):
             half = total[:, pair * PAIR : (pair + 1) * PAIR]
             if part < 2:
                 half = rotate_lanes(half, cos[...], sin[...], 1.0)
             if part == 0:
-                outs[0][pair][...] = half.astype(bf16)
+                q[...] = half.astype(bf16)
             else:
-                outs[1][pair][:, (part - 1) * PAIR : part * PAIR] = half.astype(bf16)
-
-
-def project(ids, x, gain, shift, weights, bias, tables, tile=256):
-    rows, wide = x.shape
+                kv[:, (part - 1) * PAIR : part * PAIR] = half.astype(bf16)
+
+
+def project(ids, n1, weights, bias, tables, tile=256):
+    rows, wide = n1.shape
     row = lambda w: pl.BlockSpec((tile, w), lambda i: (i, 0))
     s = jax.ShapeDtypeStruct
     return pl.pallas_call(
         project_kernel,
         grid=(rows // tile,),
         in_specs=[smem, row(wide)]
-        + [whole(v.shape) for v in (gain, shift, *weights, bias)]
+        + [whole(v.shape) for v in (*weights, bias)]
         + [row(PAIR)] * 2,
-        out_specs=[row(PAIR)] * 2 + [row(2 * PAIR)] * 2 + [row(wide)],
-        out_shape=[s((rows, PAIR), bf16)] * 2
-        + [s((rows, 2 * PAIR), bf16)] * 2
-        + [s((rows, wide), bf16)],
-        compiler_params=params(18),
+        out_specs=[row(PAIR)] * 2 + [row(2 * PAIR)] * 2,
+        out_shape=[s((rows, PAIR), bf16)] * 2 + [s((rows, 2 * PAIR), bf16)] * 2,
+        scratch_shapes=[pltpu.VMEM((3, wide, weights[0].shape[1]), bf16)],
+        compiler_params=params(16),
         cost_estimate=cost(4.3),
         name="project",
-    )(ids, x, gain, shift, *weights, bias, *tables)
+    )(ids, n1, *weights, bias, *tables)
 
 
 def head_lanes(shape, head):
     return lax.broadcasted_iota(jnp.int32, shape, 1) // HD == head
 
 
-def load_keys(kvs, kv_scr):
-    start = 0
-    for part in kvs:
-        count = part.shape[0] // BLK
-        for block in range(count):
-            kv_scr[start + block] = part[block * BLK : (block + 1) * BLK, :]
-        start += count
-
-
-def attend_forward_kernel(maxk, low, count, first, last, ids, q, kv, *refs):
-    if first:
-        ins, refs = None, refs
-    else:
+def sublanes(index, size):
+    return pl.ds(pl.multiple_of(index * size, size), size)
+
+
+def triangle(rows, cols):
+    return lax.broadcasted_iota(jnp.int32, (rows, cols), 0) <= lax.broadcasted_iota(
+        jnp.int32, (rows, cols), 1
+    )
+
+
+def slot_of(ids, lists, slots, block, step):
+    entry = lists[block, step]
+    return jnp.where(entry < 0, entry, lax.rem(entry - ids[9] + slots, slots))
+
+
+def head_of(ref, block, head):
+    value = ref[sublanes(block, BLK), :]
+    return jnp.where(head_lanes(value.shape, head), value, jnp.zeros_like(value))
+
+
+def attend_forward_kernel(slots, low, count, first, last, ids, lists, q, kv, *refs):
+    if not first:
         ins, refs = refs[:2], refs[2:]
     outs, (turned, state, acc) = refs[:2], refs[2:]
-    for slot in range(count):
-        turned[slot] = kv[slot * BLK : (slot + 1) * BLK, PAIR:].T
+    blocks = q.shape[0] // BLK
+
+    def turn(slot, unused):
+        turned[slot] = kv[sublanes(slot, BLK), PAIR:].T
+        return unused
+
+    lax.fori_loop(0, count, turn, 0)
     if not first:
         state[...] = ins[0][...]
         acc[...] = ins[1][...]
-    for block in range(q.shape[0] // BLK):
-        own = ids[0] + block
-        for head in range(2):
-            rows = slice(block * PAIR + head * HD, block * PAIR + (head + 1) * HD)
-            part = slice(head * HD, (head + 1) * HD)
-            line = block * 2 + head
-            tops, sums = slice(line, line + 1), slice(8 + line, 9 + line)
-            query = q[block * BLK : (block + 1) * BLK, :]
-            query = jnp.where(head_lanes(query.shape, head), query, jnp.zeros_like(query))
-
-            if first:
-                at = pl.ds(pl.multiple_of((own - low) * BLK, BLK), BLK)
-                scores = dot(kv[at, :PAIR], query, NT) * scale2
-                keep = lax.broadcasted_iota(jnp.int32, scores.shape, 0) <= lax.broadcasted_iota(
-                    jnp.int32, scores.shape, 1
+
+    def one(line, unused):
+        block, head = lax.div(line, 2), lax.rem(line, 2)
+        own = ids[8] + block
+        rows, part = sublanes(line, HD), sublanes(head, HD)
+        tops, sums = pl.ds(line, 1), pl.ds(8 + line, 1)
+        query = head_of(q, block, head)
+
+        if first:
+            upper, lower = sublanes(2 * (own - low), HALF), sublanes(2 * (own - low) + 1, HALF)
+            scores = dot(kv[upper, :PAIR], query, NT) * scale2
+            scores = jnp.where(triangle(HALF, BLK), scores, masked)
+            late = dot(kv[lower, :PAIR], query[HALF:, :], NT) * scale2
+            late = jnp.where(triangle(HALF, HALF), late, masked)
+            state[tops, :] = jnp.max(scores, axis=0, keepdims=True)
+            state[tops, HALF:] = jnp.maximum(
+                state[tops, HALF:], jnp.max(late, axis=0, keepdims=True)
+            )
+            weight = jnp.exp2(scores - state[tops, :])
+            late = jnp.exp2(late - state[tops, HALF:])
+            state[sums, :] = jnp.sum(weight, axis=0, keepdims=True)
+            state[sums, HALF:] += jnp.sum(late, axis=0, keepdims=True)
+            acc[rows, :] = dot(turned[own - low, part, :HALF], weight.astype(bf16), NN)
+            acc[rows, HALF:] += dot(turned[own - low, part, HALF:], late.astype(bf16), NN)
+
+        def entry(step, unused):
+            slot = slot_of(ids, lists, slots, block, step)
+
+            @pl.when((slot >= low) & (slot < low + count) & (slot != own))
+            def _():
+                scores = dot(kv[sublanes(slot - low, BLK), :PAIR], query, NT) * scale2
+                old = state[tops, :]
+                top = jnp.maximum(old, jnp.max(scores, axis=0, keepdims=True))
+                weight = jnp.exp2(scores - top)
+                shrink = jnp.exp2(old - top)
+                state[tops, :] = top
+                state[sums, :] = state[sums, :] * shrink + jnp.sum(weight, axis=0, keepdims=True)
+                acc[rows, :] = acc[rows, :] * shrink + dot(
+                    turned[slot - low, part, :], weight.astype(bf16), NN
                 )
-                scores = jnp.where(keep, scores, masked)
-                top = jnp.max(scores, axis=0, keepdims=True)
-                weight = jnp.exp2(scores - top)
-                state[tops, :] = top
-                state[sums, :] = jnp.sum(weight, axis=0, keepdims=True)
-                acc[rows, :] = dot(turned[own - low][part, :], weight.astype(bf16), NN)
-
-            def entry(step, unused):
-                slot = ids[2 + block * maxk + step]
-
-                @pl.when((slot >= low) & (slot < low + count) & (slot != own))
-                def _():
-                    at = pl.ds(pl.multiple_of((slot - low) * BLK, BLK), BLK)
-                    scores = dot(kv[at, :PAIR], query, NT) * scale2
-                    old = state[tops, :]
-                    top = jnp.maximum(old, jnp.max(scores, axis=0, keepdims=True))
-                    weight = jnp.exp2(scores - top)
-                    shrink = jnp.exp2(old - top)
-                    state[tops, :] = top
-                    state[sums, :] = state[sums, :] * shrink + jnp.sum(
-                        weight, axis=0, keepdims=True
-                    )
-                    acc[rows, :] = acc[rows, :] * shrink + dot(
-                        turned[slot - low][part, :], weight.astype(bf16), NN
-                    )
-
-                return unused
-
-            lax.fori_loop(0, maxk, entry, 0)
-            if last:
-                outs[1][line : line + 1, :] = state[tops, :] + jnp.log2(state[sums, :])
-                acc[rows, :] = acc[rows, :] * (1.0 / state[sums, :])
+
+            return unused
+
+        lax.fori_loop(0, lists.shape[1], entry, 0)
         if last:
-            outs[0][block * BLK : (block + 1) * BLK, :] = acc[
-                block * PAIR : (block + 1) * PAIR, :
-            ].T
-    if not last:
+            outs[1][pl.ds(line, 1), :] = state[tops, :] + jnp.log2(state[sums, :])
+            acc[rows, :] = acc[rows, :] * (1.0 / state[sums, :])
+        return unused
+
+    lax.fori_loop(0, 2 * blocks, one, 0)
+    if last:
+
+        def give(block, unused):
+            outs[0][sublanes(block, BLK), :] = acc[sublanes(block, PAIR), :].T
+            return unused
+
+        lax.fori_loop(0, blocks, give, 0)
+    else:
         outs[0][...] = state[...]
         outs[1][...] = acc[...]
 
 
-def attend_forward(ids, maxk, q, kv, low, carried, last, micros=0):
+def attend_forward(ids, lists, slots, q, kv, low, carried, last, micros=0):
     count = kv.shape[0] // BLK
     rows = q.shape[0]
     tall = rows // BLK * PAIR
@@ -201,8 +233,8 @@
         s((16, BLK), f32), s((tall, BLK), f32)
     ]
     return pl.pallas_call(
-        partial(attend_forward_kernel, maxk, low, count, carried is None, last),
-        in_specs=[smem] + [vmem] * (2 + len(carried or ())),
+        partial(attend_forward_kernel, slots, low, count, carried is None, last),
+        in_specs=[smem, smem] + [vmem] * (2 + len(carried or ())),
         out_specs=[vmem] * 2,
         out_shape=shapes,
         scratch_shapes=[
@@ -213,82 +245,98 @@
         compiler_params=params(8 + 2 * count),
         cost_estimate=cost(micros),
         name="attend_forward",
-    )(ids, q, kv, *(carried or ()))
-
-
-def attend_backward_kernel(slots, maxk, split, ids, q, g, o, lse, cos, sin, *refs):
+    )(ids, lists, q, kv, *(carried or ()))
+
+
+def attend_backward_kernel(slots, split, ids, lists, q, g, o, lse, cos, sin, *refs):
     outs = 2 if split else 1
-    parts = refs[: -5 - outs]
-    grads = refs[-5 - outs : -5]
-    qg, kv, turned, acc, total = refs[-5:]
-    load_keys(parts, kv)
-    for slot in range(slots):
-        turned[slot] = kv[slot][:, :PAIR].T
-    total[...] = jnp.zeros_like(total)
+    parts = refs[: -6 - outs]
+    grads = refs[-6 - outs : -6]
+    qg, kv, turned, acc, total, deltas = refs[-6:]
+    blocks = q.shape[0] // BLK
+    start = 0
+    for part in parts:
+        kv[start : start + part.shape[0], :] = part[...]
+        start += part.shape[0]
+
+    def prepare(slot, unused):
+        turned[slot] = kv[sublanes(slot, BLK), :PAIR].T
+        total[sublanes(slot, BLK), :] = jnp.zeros((BLK, 2 * PAIR), f32)
+        return unused
+
+    lax.fori_loop(0, slots, prepare, 0)
     pick = (
         lax.broadcasted_iota(jnp.int32, (8, PAIR), 1) // HD
         == lax.broadcasted_iota(jnp.int32, (8, PAIR), 0)
     ).astype(f32)
-    for block in range(q.shape[0] // BLK):
-        own = ids[0] + block
-        span = slice(block * BLK, (block + 1) * BLK)
-        deltas = lax.dot_general(
+
+    def delta_of(block, unused):
+        span = sublanes(block, BLK)
+        deltas[sublanes(block, 8), :] = lax.dot_general(
             pick,
             o[span, :] * g[span, :].astype(f32),
             NT,
             preferred_element_type=f32,
             precision=lax.Precision.HIGHEST,
         )
-        for head in range(2):
-            rows = slice(head * HD, (head + 1) * HD)
-            lanes = head_lanes((BLK, PAIR), head)
-            query = q[span, :]
-            query = jnp.where(lanes, query, jnp.zeros_like(query))
-            grad = g[span, :]
-            grad = jnp.where(lanes, grad, jnp.zeros_like(grad))
-            line = block * 2 + head
-            log_sum = lse[line : line + 1, :]
-            delta = deltas[head : head + 1, :]
-
-            def tile(slot, keep):
-                scores = dot(kv[slot][:, :PAIR], query, NT) * scale2
-                prob = jnp.exp2(scores - log_sum)
-                if keep is not None:
-                    prob = jnp.where(keep, prob, 0.0)
-                prob_grad = dot(kv[slot][:, PAIR:], grad, NT)
-                score_grad = (prob * (prob_grad - delta)).astype(bf16)
-                total[slot, :, PAIR:] += dot(prob.astype(bf16), grad, NN)
-                total[slot, :, :PAIR] += dot(score_grad, query, NN)
-                return dot(turned[slot][rows, :], score_grad, NN)
-
-            keep = lax.broadcasted_iota(jnp.int32, (BLK, BLK), 0) <= lax.broadcasted_iota(
-                jnp.int32, (BLK, BLK), 1
-            )
-            acc[rows, :] = tile(own, keep)
-
-            def entry(step, unused):
-                slot = ids[2 + block * maxk + step]
-
-                @pl.when((slot >= 0) & (slot != own))
-                def _():
-                    acc[rows, :] += tile(slot, None)
-
-                return unused
-
-            lax.fori_loop(0, maxk, entry, 0)
-        grad_q = acc[...].T * (HD ** (-0.5))
-        qg[span, :] = rotate_lanes(
-            grad_q, cos[span, :], sin[span, :], -1.0
-        ).astype(bf16)
+        return unused
+
+    lax.fori_loop(0, blocks, delta_of, 0)
+
+    def one(line, unused):
+        block, head = lax.div(line, 2), lax.rem(line, 2)
+        own = ids[8] + block
+        rows, part = sublanes(line, HD), sublanes(head, HD)
+        query, grad = head_of(q, block, head), head_of(g, block, head)
+        log_sum = lse[pl.ds(line, 1), :]
+        delta = deltas[pl.ds(block * 8 + head, 1), :]
+
+        def tile(here, keys, skip=0, keep=None):
+            scores = dot(kv[here, :PAIR], query[skip:, :], NT) * scale2
+            prob = jnp.exp2(scores - log_sum[:, skip:])
+            if keep is not None:
+                prob = jnp.where(keep, prob, 0.0)
+            prob_grad = dot(kv[here, PAIR:], grad[skip:, :], NT)
+            score_grad = (prob * (prob_grad - delta[:, skip:])).astype(bf16)
+            total[here, PAIR:] += dot(prob.astype(bf16), grad[skip:, :], NN)
+            total[here, :PAIR] += dot(score_grad, query[skip:, :], NN)
+            return dot(keys, score_grad, NN)
+
+        acc[rows, :] = tile(
+            sublanes(2 * own, HALF), turned[own, part, :HALF], 0, triangle(HALF, BLK)
+        )
+        acc[rows, HALF:] += tile(
+            sublanes(2 * own + 1, HALF), turned[own, part, HALF:], HALF, triangle(HALF, HALF)
+        )
+
+        def entry(step, unused):
+            slot = slot_of(ids, lists, slots, block, step)
+
+            @pl.when((slot >= 0) & (slot != own))
+            def _():
+                acc[rows, :] += tile(sublanes(slot, BLK), turned[slot, part, :])
+
+            return unused
+
+        lax.fori_loop(0, lists.shape[1], entry, 0)
+        return unused
+
+    lax.fori_loop(0, 2 * blocks, one, 0)
+
+    def give(block, unused):
+        span = sublanes(block, BLK)
+        grad_q = acc[sublanes(block, PAIR), :].T * (HD ** (-0.5))
+        qg[span, :] = rotate_lanes(grad_q, cos[span, :], sin[span, :], -1.0).astype(bf16)
+        return unused
+
+    lax.fori_loop(0, blocks, give, 0)
     start = 0
     for out in grads:
-        count = out.shape[0] // BLK
-        for block in range(count):
-            out[block * BLK : (block + 1) * BLK, :] = total[start + block].astype(out.dtype)
-        start += count
-
-
-def attend_backward(ids, maxk, q, g, o, lse, tables, kvs):
+        out[...] = total[start : start + out.shape[0], :].astype(out.dtype)
+        start += out.shape[0]
+
+
+def attend_backward(ids, lists, q, g, o, lse, tables, kvs):
     slots = sum(part.shape[0] for part in kvs) // BLK
     rows = q.shape[0]
     split = len(kvs) == 2
@@ -298,33 +346,72 @@
     shapes.append(jax.ShapeDtypeStruct((rows, PAIR), bf16))
     vmem = pl.BlockSpec(memory_space=pltpu.VMEM)
     return pl.pallas_call(
-        partial(attend_backward_kernel, slots, maxk, split),
+        partial(attend_backward_kernel, slots, split),
         grid=(),
-        in_specs=[smem] + [vmem] * (6 + len(kvs)),
+        in_specs=[smem, smem] + [vmem] * (6 + len(kvs)),
         out_specs=[vmem] * len(shapes),
         out_shape=shapes,
         scratch_shapes=[
-            pltpu.VMEM((slots, BLK, 2 * PAIR), bf16),
+            pltpu.VMEM((slots * BLK, 2 * PAIR), bf16),
             pltpu.VMEM((slots, PAIR, BLK), bf16),
-            pltpu.VMEM((PAIR, BLK), f32),
-            pltpu.VMEM((slots, BLK, 2 * PAIR), f32),
+            pltpu.VMEM((rows // BLK * PAIR, BLK), f32),
+            pltpu.VMEM((slots * BLK, 2 * PAIR), f32),
+            pltpu.VMEM((rows // BLK * 8, BLK), f32),
         ],
         compiler_params=params(14 + slots),
         cost_estimate=cost(0),
         name="attend_backward",
-    )(ids, q, g, o, lse, *tables, *kvs)
-
-
-def unpack(ids, pieces, units, up, down, dense):
+    )(ids, lists, q, g, o, lse, *tables, *kvs)
+
+
+def unpack_up(ids, pieces, up):
+    for i, piece in enumerate(pieces):
+        for n in range(up.shape[1] // SHARD):
+            up[columns(ids[i], SHARD), n * SHARD : (n + 1) * SHARD] = piece[
+                n * SHARD : (n + 1) * SHARD, :
+            ]
+
+
+def unpack_down(ids, pieces, down, dense):
+    units = down.shape[0]
     for i, piece in enumerate(pieces):
         where = columns(ids[i], SHARD)
         down[:, where] = piece[:units, :]
-        for n in range(units // SHARD):
-            up[where, n * SHARD : (n + 1) * SHARD] = piece[
-                units + n * SHARD : units + (n + 1) * SHARD, :
-            ]
         if dense is not None:
-            dense[:, where] = piece[2 * units :, :]
+            dense[:, where] = piece[units:, :]
+
+
+def mlp_up_kernel(ids, x, gain, shift, up_bias, p0, p1, p2, p3, n2, act, slope, up):
+    @pl.when(pl.program_id(0) == 0)
+    def _():
+        unpack_up(ids, (p0, p1, p2, p3), up)
+
+    normal, _ = norm_rows(x[...].astype(f32))
+    normed = (normal * gain[...] + shift[...]).astype(bf16)
+    n2[...] = normed
+    hidden = dot(normed, up[...], NN) + up_bias[...]
+    cdf = 0.5 + 0.5 * lax.erf(hidden * (2.0 ** -0.5))
+    pdf = jnp.exp(hidden * hidden * -0.5) * 0.3989422804014327
+    act[...] = (hidden * cdf).astype(bf16)
+    slope[...] = (cdf + hidden * pdf).astype(bf16)
+
+
+def mlp_up(ids, x, gain, shift, up_bias, pieces, tile=256):
+    rows, width = x.shape
+    units = up_bias.shape[1]
+    row = lambda w: pl.BlockSpec((tile, w), lambda i: (i, 0))
+    s = jax.ShapeDtypeStruct
+    return pl.pallas_call(
+        mlp_up_kernel,
+        grid=(rows // tile,),
+        in_specs=[smem, row(width)] + [whole(a.shape) for a in (gain, shift, up_bias, *pieces)],
+        out_specs=[row(width), row(units), row(units)],
+        out_shape=[s((rows, width), bf16), s((rows, units), bf16), s((rows, units), bf16)],
+        scratch_shapes=[pltpu.VMEM((width, units), bf16)],
+        compiler_params=params(24),
+        cost_estimate=cost(0),
+        name="mlp_up",
+    )(ids, x, gain, shift, up_bias, *pieces)
 
 
 def store_part(outs, sizes, value):
@@ -341,72 +428,54 @@
         start += count
 
 
-def mlp_forward_kernel(
-    rows, ids, x, cot, gain, shift, up_bias, p0, p1, p2, p3, o0, o1,
-    keep, send, n2, act, slope, ctx, g0, g1, up, down, dense,
+def mlp_down_kernel(
+    rows, ids, act, cot, p0, p1, p2, p3, o0, o1, first, second, ctx, g0, g1, down, dense
 ):
-    units = act.shape[1]
-
     @pl.when(pl.program_id(0) == 0)
     def _():
-        unpack(ids, (p0, p1, p2, p3), units, up, down, dense)
-
-    normal, _ = norm_rows(x[...].astype(f32))
-    normed = (normal * gain[...] + shift[...]).astype(bf16)
-    n2[...] = normed
-    hidden = dot(normed, up[...], NN) + up_bias[...]
-    cdf = 0.5 + 0.5 * lax.erf(hidden * (2.0 ** -0.5))
-    pdf = jnp.exp(hidden * hidden * -0.5) * 0.3989422804014327
-    low = (hidden * cdf).astype(bf16)
-    act[...] = low
-    slope[...] = (cdf + hidden * pdf).astype(bf16)
+        unpack_down(ids, (p0, p1, p2, p3), down, dense)
+
     context_grad = dot(cot[...], dense[...], NT)
     g0[...] = context_grad[:, :PAIR].astype(bf16)
     g1[...] = context_grad[:, PAIR:].astype(bf16)
     ctx[:, :PAIR] = o0[...].astype(bf16)
     ctx[:, PAIR:] = o1[...].astype(bf16)
-    value = dot(ctx[...], dense[...], NN) + dot(low, down[...], NN)
-    store_part((keep, send), (rows // 2, rows // 2), value.astype(bf16))
-
-
-def mlp_forward(ids, x, cot, gain, shift, up_bias, pieces, o0, o1, tile=256):
-    rows, width = x.shape
-    units = up_bias.shape[1]
+    value = dot(ctx[...], dense[...], NN) + dot(act[...], down[...], NN)
+    store_part((first, second), (rows // 2, rows // 2), value.astype(bf16))
+
+
+def mlp_down(ids, act, cot, pieces, o0, o1, tile=256):
+    rows, width = cot.shape
+    units = act.shape[1]
     row = lambda w: pl.BlockSpec((tile, w), lambda i: (i, 0))
     s = jax.ShapeDtypeStruct
     return pl.pallas_call(
-        partial(mlp_forward_kernel, rows),
+        partial(mlp_down_kernel, rows),
         grid=(rows // tile,),
-        in_specs=[smem, row(width), row(width)]
-        + [whole(a.shape) for a in (gain, shift, up_bias, *pieces)]
+        in_specs=[smem, row(units), row(width)]
+        + [whole(a.shape) for a in pieces]
         + [row(PAIR), row(PAIR)],
-        out_specs=[whole((rows // 2, width))] * 2
-        + [row(width), row(units), row(units), row(2 * PAIR), row(PAIR), row(PAIR)],
+        out_specs=[whole((rows // 2, width))] * 2 + [row(2 * PAIR), row(PAIR), row(PAIR)],
         out_shape=[s((rows // 2, width), bf16)] * 2
-        + [
-            s((rows, width), bf16), s((rows, units), bf16), s((rows, units), bf16),
-            s((rows, 2 * PAIR), bf16), s((rows, PAIR), bf16), s((rows, PAIR), bf16),
-        ],
+        + [s((rows, 2 * PAIR), bf16), s((rows, PAIR), bf16), s((rows, PAIR), bf16)],
         scratch_shapes=[
-            pltpu.VMEM((width, units), bf16),
             pltpu.VMEM((units, width), bf16),
             pltpu.VMEM((2 * PAIR, width), bf16),
         ],
-        compiler_params=params(28),
+        compiler_params=params(26),
         cost_estimate=cost(1),
-        name="mlp_forward",
-    )(ids, x, cot, gain, shift, up_bias, *pieces, o0, o1)
+        name="mlp_down",
+    )(ids, act, cot, *pieces, o0, o1)
 
 
 def mlp_backward_kernel(
-    ids, x, cot, gain, slope, p0, p1, p2, p3, hid, e2, sums, up, down
+    ids, x, cot, gain, slope, u0, u1, u2, u3, d0, d1, d2, d3, hid, e2, sums, up, down
 ):
-    units = hid.shape[1]
-
     @pl.when(pl.program_id(0) == 0)
     def _():
         sums[...] = jnp.zeros_like(sums)
-        unpack(ids, (p0, p1, p2, p3), units, up, down, None)
+        unpack_up(ids, (u0, u1, u2, u3), up)
+        unpack_down(ids, (d0, d1, d2, d3), down, None)
 
     low = (dot(cot[...], down[...], NT) * slope[...].astype(f32)).astype(bf16)
     hid[...] = low
@@ -444,7 +513,7 @@
 def mlp_weights_kernel(ids, act, cot, n2, hid, keep, near, far):
     units = act.shape[1]
     step = pl.program_id(0)
-    index = ids[step]
+    index = ids[4 + step]
     for out, when in ((near, step == 0), (far, step == 1), (keep, step >= 2)):
 
         @pl.when(when)
@@ -461,7 +530,7 @@
 def rest_weights_kernel(ids, ctx, cot, n1, pg, keep, near, far):
     width = ctx.shape[1]
     step = pl.program_id(0)
-    index = ids[step]
+    index = ids[4 + step]
     for out, when in ((near, step == 0), (far, step == 1), (keep, step >= 2)):
 
         @pl.when(when)
@@ -494,13 +563,12 @@
 
 
 def input_grad_kernel(
-    split, sizes, ids, x, e2, gain, sums_two, qg0, qg1, cos, sin, w0, w1, w2, w3, *refs
+    split, sizes, ids, x, e2, gain, sums_two, qg0, qg1, cos, sin, *refs
 ):
     count = 4 if split else 2
+    weights, refs = refs[:4], refs[4:]
     grads, es, (pg, sums, first) = refs[:count], refs[count:-3], refs[-3:]
-    weights = (w0, w1, w2, w3)
-    depth = w0.shape[0] // 3
-    width = w0.shape[1]
+    depth, width = weights[0].shape[0] // 3, 2 * PAIR
 
     @pl.when(pl.program_id(0) == 0)
     def _():
@@ -543,7 +611,7 @@
     rows, width = x.shape
     row = lambda w: pl.BlockSpec((tile, w), lambda i: (i, 0))
     s = jax.ShapeDtypeStruct
-    units = 3 * weights[0].shape[1]
+    units = 6 * PAIR
     sizes = (rows // 2,) * 2
     parts = [(sizes[0] + EXTRA, width), *[(size, width) for size in sizes[1:]]]
     return pl.pallas_call(
@@ -621,15 +689,17 @@
 
 
 def finish_in_kernel(rows, a, b, x, upstream, out):
-    tile = 128
-    for at in range(0, rows, tile):
-        here = slice(at, at + tile)
+    def one(step, unused):
+        here = sublanes(step, 128)
         total = a[here, :].astype(f32) + b[here, :].astype(f32)
         normal, factor = norm_rows(x[here, :].astype(f32))
         mean_e = jnp.mean(total, axis=-1, keepdims=True)
         mean_en = jnp.mean(total * normal, axis=-1, keepdims=True)
         result = upstream[here, :].astype(f32) + factor * (total - mean_e - normal * mean_en)
         out[here, :] = result.astype(bf16)
+        return unused
+
+    lax.fori_loop(0, rows // 128, one, 0)
     if a.shape[0] > rows:
         out[rows:, :] = split_terms(join_terms(a[rows:, :]) + join_terms(b[rows:, :]))
 
@@ -754,14 +824,19 @@
 
 
 def rotation_tables(positions):
-    lane = jnp.arange(PAIR, dtype=jnp.int32) % HD
     half = ROT // 2
     frequency = jnp.exp(
-        -jnp.log(10000.0) * (lane % half).astype(f32) * 2.0 / ROT
-    )
-    angle = positions.astype(f32)[:, None] * frequency[None, :]
-    rotated = lane < ROT
-    return jnp.where(rotated, jnp.cos(angle), 1.0), jnp.where(rotated, jnp.sin(angle), 0.0)
+        -jnp.log(10000.0) * jnp.arange(half, dtype=jnp.int32).astype(f32) * 2.0 / ROT
+    )
+    angle = frequency[:, None] * positions.astype(f32)[None, :]
+    lane = lax.broadcasted_iota(jnp.int32, (half, PAIR), 1) % HD
+    pick = lax.broadcasted_iota(jnp.int32, (half, PAIR), 0) == lane % half
+    pick = (pick & (lane < ROT)).astype(f32)
+    spread = lambda v: lax.dot_general(
+        v, pick, TN, precision=lax.Precision.HIGHEST, preferred_element_type=f32
+    )
+    plain = (jnp.arange(PAIR, dtype=jnp.int32) % HD >= ROT).astype(f32)
+    return spread(jnp.cos(angle)) + plain, spread(jnp.sin(angle))
 
 
 def body(
@@ -787,62 +862,59 @@
 ):
     rows, width = tokens.shape
     blocks = rows // BLK
-    maxk = block_lists.shape[1]
     me = lax.axis_index("fsdp")
-    place = lax.axis_index("context")
-    order = jnp.stack([me, me ^ 1, me ^ 2, me ^ 3]).astype(jnp.int32)
-    send_order = jnp.stack([me ^ 1, me ^ 3, me, me ^ 2]).astype(jnp.int32)
     split = contexts == 2
     slots = contexts * blocks
-    first_slot = place * blocks
-    if split:
-        lists = jnp.where(block_lists >= 0, (block_lists - first_slot) % slots, -1)
-        base = jnp.zeros((), jnp.int32)
-    else:
-        lists, base = block_lists, first_slot
-    ids = jnp.concatenate(
-        [jnp.stack([base, base]).astype(jnp.int32), lists.reshape(-1).astype(jnp.int32)]
-    )
-
-    blocks_of = lambda w: w.reshape(SHARD, -1, SHARD).transpose(1, 0, 2).reshape(-1, SHARD)
+    first_slot = lax.axis_index("context") * blocks
+    step = jnp.arange(10, dtype=jnp.int32)
+    flip = jnp.where(step < 4, step, jnp.where(step < 6, 2 * step - 7, 2 * step - 12))
+    ids = jnp.where(step < 8, me ^ flip, jnp.where(step == 8 if split else step < 8, 0, first_slot))
+    if not split:
+        ids = jnp.where(step == 9, 0, ids)
+    ids = ids.astype(jnp.int32)
+
+    blocks_of = lambda w: w.reshape(SHARD, -1, SHARD).transpose(1, 0, 2)
     units = up_bias.shape[0]
-    wp = blocks_of(project_weight)
-    wp1, wp2 = swap(wp, "fsdp", 4, 1), swap(wp, "fsdp", 4, 2)
-    wr = jnp.concatenate([down_weight, blocks_of(up_weight), dense_weight], axis=0)
-    wr = after(wr, wp)
-    wr1, wr2 = swap(wr, "fsdp", 4, 1), swap(wr, "fsdp", 4, 2)
-
+    near = lambda v: swap(v, "fsdp", 4, 1)
+    far = lambda v: swap(v, "fsdp", 4, 2)
+    wp = blocks_of(project_weight).reshape(-1, SHARD)
+    up = blocks_of(up_weight).reshape(-1, SHARD)
+    wp_far, up_far = far(wp), far(up)
     tables = rotation_tables(positions)
-    wp2 = after(wp2, tables, ids, send_order)
-    wp3 = swap(wp2, "fsdp", 4, 1)
-    projects = (wp, wp1, wp2, wp3)
-    q0, q1, kv0, kv1, normed_one = project(
-        order, tokens, first_gain[None], first_shift[None], projects, project_bias, tables
-    )
+    normed_one = norm(tokens, first_gain[None], first_shift[None])
+    wp_far = after(wp_far, tables, ids, normed_one, up)
+    projects = (wp, near(wp), wp_far, near(wp_far))
+    q0, q1, kv0, kv1 = project(ids, normed_one, projects, project_bias, tables)
+    down = jnp.concatenate(after([down_weight, dense_weight], kv1), axis=0)
+    down_far = far(down)
     if split:
         other0, other1 = swap(kv0, "context", 2, 1), swap(kv1, "context", 2, 1)
         keys = ((kv0, other0), (kv1, other1))
-        state0 = attend_forward(ids, maxk, q0, kv0, 0, None, False)
-        state1 = attend_forward(ids, maxk, after(q1, state0), kv1, 0, None, False)
+        state0 = attend_forward(ids, block_lists, slots, after(q0, kv1), kv0, 0, None, False)
+        state1 = attend_forward(ids, block_lists, slots, after(q1, state0), kv1, 0, None, False)
+        up_far = after(up_far, state1)
+        ups = (up, near(up), up_far, near(up_far))
         o0, lse0 = attend_forward(
-            ids, maxk, after(q0, state1), other0, blocks, state0, True
+            ids, block_lists, slots, after(q0, up_far), other0, blocks, state0, True
         )
-        wr2 = after(wr2, o0)
-        wr3 = swap(wr2, "fsdp", 4, 1)
+        normed_two, activated, slope = mlp_up(
+            ids, after(tokens, o0), second_gain[None], second_shift[None], up_bias[None], ups
+        )
         o1, lse1 = attend_forward(
-            ids, maxk, after(q1, o0), other1, blocks, state1, True, 10
+            ids, block_lists, slots, after(q1, activated), other1, blocks, state1, True, 10
         )
+        down_far = after(down_far, activated)
     else:
         keys = [(lax.all_gather(kv, "context", axis=0, tiled=True),) for kv in (kv0, kv1)]
-        wr3 = swap(wr2, "fsdp", 4, 1)
-        o0, lse0 = attend_forward(ids, maxk, q0, keys[0][0], 0, None, True)
-        o1, lse1 = attend_forward(ids, maxk, q1, keys[1][0], 0, None, True)
-
-    made = mlp_forward(
-        order, tokens, cotangent, second_gain[None], second_shift[None], up_bias[None],
-        (wr, wr1, wr2, wr3), o0, o1,
-    )
-    normed_two, activated, slope, context_low, g0, g1 = made[2:]
+        o0, lse0 = attend_forward(ids, block_lists, slots, q0, keys[0][0], 0, None, True)
+        o1, lse1 = attend_forward(ids, block_lists, slots, q1, keys[1][0], 0, None, True)
+        ups = (up, near(up), up_far, near(up_far))
+        normed_two, activated, slope = mlp_up(
+            ids, tokens, second_gain[None], second_shift[None], up_bias[None], ups
+        )
+    downs = (down, near(down), down_far, near(down_far))
+    made = mlp_down(ids, activated, cotangent, downs, o0, o1)
+    context_low, g0, g1 = made[2:]
     half = rows // 2
 
     out = LineSum(
@@ -855,8 +927,8 @@
             for start in (0, half)
         ],
     )
-    back0 = attend_backward(ids, maxk, q0, g0, o0, lse0, tables, keys[0])
-    back1 = attend_backward(ids, maxk, q1, after(g1, back0), o1, lse1, tables, keys[1])
+    back0 = attend_backward(ids, block_lists, q0, g0, o0, lse0, tables, keys[0])
+    back1 = attend_backward(ids, block_lists, q1, after(g1, back0), o1, lse1, tables, keys[1])
     if split:
         grads = []
         for own, other, _ in (back0, back1):
@@ -868,11 +940,11 @@
         ]
     mark = out.add(0, (back1, grads[1]) if split else back1)
     hidden_grad, e2, sums = mlp_backward(
-        order, tokens, after(cotangent, mark),
-        second_gain[None], slope, (wr, wr1, wr2, wr3),
+        ids, tokens, after(cotangent, mark),
+        second_gain[None], slope, ups + downs,
     )
     made = input_grad(
-        order, tokens, e2, first_gain[None], sums, (back0[-1], back1[-1]),
+        ids, tokens, e2, first_gain[None], sums, (back0[-1], back1[-1]),
         tables, projects, grads, split,
     )
     projected_grad, sums = made[2:]
@@ -888,13 +960,13 @@
     )
     mark = out.add(1, made[0])
     mlp_keep, *mlp_send = weight_parts(
-        mlp_weights_kernel, "mlp_weights", send_order, 2 * units,
+        mlp_weights_kernel, "mlp_weights", ids, 2 * units,
         activated, cotangent, normed_two, after(hidden_grad, mark),
     )
     mlp_got = swap(mlp_send, "fsdp", 4, 1)
     mark = out.end(0, mlp_keep)
     rest_keep, *rest_send = weight_parts(
-        rest_weights_kernel, "rest_weights", send_order, 4 * SHARD,
+        rest_weights_kernel, "rest_weights", ids, 4 * SHARD,
         context_low, cotangent, normed_one, after(projected_grad, mark),
     )
     rest_got = swap(rest_send, "fsdp", 4, 1)

time: 229 us -> 225 us (0.983)
  starting transfers between devices: 38.8 us -> 74.5 us
  waiting for transfers between devices: 85.3 us -> 50.4 us
  Pallas kernels: 92.3 us -> 84.5 us
  local copies, waits for them, and re-layouts: 4.74 us -> 9.01 us
  other arithmetic: 3.56 us -> 0.74 us
    ppermute x21 -> x24, starting transfers between devices: 13.1 us -> 48.2 us  [swap(): return jax.tree.map(lambda v: lax.ppermute(v, axis, pairs), values)]
    ppermute x21 -> x24, waiting for transfers between devices: 33.3 us -> 16.2 us  [swap(): return jax.tree.map(lambda v: lax.ppermute(v, axis, pairs), values)]
    ppermute x4, waiting for transfers between devices: 42.5 us -> 31.2 us  [end(): self.third[i] = lax.ppermute(self.finals[i], 'tensor', [(1, 0), (2, 3)])]
    pallas_call x7 -> x8, Pallas kernels: 45.2 us -> 37.8 us  [the longest x2 13.9 us: attend_backward(): pl.pallas_call(partial(attend_backward_kernel, slots, split), grid=(), in...]
    ppermute x4, waiting for transfers between devices: 9.54 us -> 3.08 us  [__init__(): lax.ppermute(part, 'tensor', [(0, 1), (3, 2)])]
    unnamed x45 -> x52, local copies, waits for them, and re-layouts: 2.11 us -> 6.67 us
    select_n x2 -> x1, other arithmetic: 2.61 us -> 0.01 us  [body(): jnp.where(step < 8, me ^ flip, jnp.where(step == 8 if split else step < 8...]
    pallas_call x21 -> x22, Pallas kernels: 17.7 us -> 19.3 us  [call(): pl.pallas_call(kernel, grid=(grid,), in_specs=in_specs or [whole(a.shape)...]
  transfers between devices with their start and end apart: 33 -> 36, of which waited for: 17 -> 14; matrix products, arithmetic and copies ran while one was open for 3% -> 2% of each run, Pallas kernels for 35% -> 35%
where the time goes in v1:
time: 225 us; the launch traced here: 222 us
  Pallas kernels  84.5 us (38%)
  starting transfers between devices  74.5 us (33%)
  waiting for transfers between devices  50.4 us (22%)
  local copies, waits for them, and re-layouts  9.01 us (4%)
    ppermute x24, starting transfers between devices, swap(): return jax.tree.map(lambda v: lax.ppermute(v, axis, pairs), values)  48.2 us
    ppermute x4, waiting for transfers between devices, end(): self.third[i] = lax.ppermute(self.finals[i], 'tensor', [(1, 0), (2, 3)])  31.2 us
    pallas_call x22, Pallas kernels, call(): pl.pallas_call(kernel, grid=(grid,), in_specs=in_specs or [whole(a.shape)...  19.3 us
    ppermute x4, starting transfers between devices, __init__(): lax.ppermute(part, 'tensor', [(0, 1), (3, 2)])  18 us
    ppermute x24, waiting for transfers between devices, swap(): return jax.tree.map(lambda v: lax.ppermute(v, axis, pairs), values)  16.2 us
    pallas_call x2, Pallas kernels, attend_backward(): pl.pallas_call(partial(attend_backward_kernel, slots, split), grid=(), in...  13.9 us
    pallas_call x4, Pallas kernels, attend_forward(): pl.pallas_call(partial(attend_forward_kernel, slots, low, count, carried...  12.4 us
    pallas_call x2, Pallas kernels, weight_parts(): pl.pallas_call(kernel, grid=(4,), in_specs=[smem] + [whole(a.shape) for a...  9.84 us
  transfers between devices with their start and end apart: 36, of which 14 were waited for; matrix products, arithmetic and copies ran while one was open for 2% of the time, Pallas kernels for 35%

profile of v1, /device:TPU:0, one launch (start us, length us, event | category | flops | bytes accessed | tf_op | source)
XLA Modules:
  0.0 222.0 jit_solution(14108431838035885887)
XLA Ops:
  0.6 3.0 %collective-permute-start.1 = (bf16[768,256]{1,0:T(8,128)(2,1)}, bf16[768,256]{1,0:T(8,128)(2,1)S(1)}, u32[]{:S(2)}, u32[]{:S(2)}) collective-permute-start(bf16[768,256]{1,0:T(8,128)(2,1)} %bitcast.29), channel_id=1, source_target_pairs={{0,16},{8,24},{16,0},{24,8},{1,17},{9,25},{17,1},{25,9},{2,18},{10... | collective-permute-start | bytes 1179656 | tf_op jit(solution)/shard_map/ppermute | solution.py:786
  14.8 3.6 %project.1 = (bf16[1024,128]{1,0:T(8,128)(2,1)S(1)}, bf16[1024,128]{1,0:T(8,128)(2,1)S(1)}, bf16[1024,256]{1,0:T(8,128)(2,1)S(1)}, bf16[1024,256]{1,0:T(8,128)(2,1)S(1)}) custom-call(s32[10]{0:T(128)S(1)} %compare_select_fusion.3.ids, bf16[1024,1024]{1,0:T(8,128)(2,1)S(1)} %norm.1.n1, bf16[768,256]{1,0:T(8,128)(2,1)S(1)} %bitcast.31, ...), custom_call_target="tpu_custom_call" | custom-call | flops 4944999936 | bytes 15910000 | tf_op jit(solution)/shard_map/project/pallas_call | solution.py:111
  21.8 4.8 %attend_forward.4 = (f32[16,512]{1,0:T(8,128)S(1)}, f32[256,512]{1,0:T(8,128)S(1)}) custom-call(s32[10]{0:T(128)S(1)} %compare_select_fusion.3.ids, s32[2,3]{1,0:T(2,128)S(1)} %copy-done.12, bf16[1024,128]{1,0:T(8,128)(2,1)S(1)} %get-tuple-element.113.q, bf16[1024,256]{1,0:T(8,128)(2,1)S(1)} %get-tuple-element.106.kv.refs_0_), custom_call_target="tpu_custom_call" | custom-call | tf_op jit(solution)/shard_map/attend_forward/pallas_call | solution.py:235
  26.5 4.8 %attend_forward.5 = (f32[16,512]{1,0:T(8,128)S(1)}, f32[256,512]{1,0:T(8,128)S(1)}) custom-call(s32[10]{0:T(128)S(1)} %compare_select_fusion.3.ids, s32[2,3]{1,0:T(2,128)S(1)} %copy-done.12, bf16[1024,128]{1,0:T(8,128)(2,1)S(1)} %get-tuple-element.120.q, bf16[1024,256]{1,0:T(8,128)(2,1)S(1)} %get-tuple-element.104.kv.refs_0_), custom_call_target="tpu_custom_call" | custom-call | tf_op jit(solution)/shard_map/attend_forward/pallas_call | solution.py:235
  32.1 2.5 %collective-permute-done.4.kv.refs_1_ = bf16[1024,256]{1,0:T(8,128)(2,1)S(1)} collective-permute-done((bf16[1024,256]{1,0:T(8,128)(2,1)S(1)}, bf16[1024,256]{1,0:T(8,128)(2,1)S(1)}, u32[]{:S(2)}, u32[]{:S(2)}) %collective-permute-start.4) | collective-permute-done | bytes 524320 | tf_op jit(solution)/shard_map/ppermute | solution.py:786
  36.1 6.4 %mlp_up.1 = (bf16[1024,1024]{1,0:T(8,128)(2,1)S(1)}, bf16[1024,1024]{1,0:T(8,128)(2,1)S(1)}, bf16[1024,1024]{1,0:T(8,128)(2,1)S(1)}) custom-call(s32[10]{0:T(128)S(1)} %compare_select_fusion.3.ids, bf16[1024,1024]{1,0:T(8,128)(2,1)S(1)} %copy-done.1, f32[1,1024]{1,0:T(1,128)S(1)} %bitcast.33, f32[1,1024]{1,0:T(1,128)S(1)} %bitcast.41, ...), custom_call_target="tpu_custom_call" | custom-call | tf_op jit(solution)/shard_map/mlp_up/pallas_call | solution.py:404
  42.6 3.2 %collective-permute-start.9 = (bf16[1280,256]{1,0:T(8,128)(2,1)S(1)}, bf16[1280,256]{1,0:T(8,128)(2,1)S(1)}, u32[]{:S(2)}, u32[]{:S(2)}) collective-permute-start(bf16[1280,256]{1,0:T(8,128)(2,1)S(1)} %collective-permute-done.8.p2.d2), channel_id=1, source_target_pairs={{0,8},{8,0},{16,24},{24,16},{1,9},{9,1},{17,25},{25,17},{2,10},{10... | collective-permute-start | bytes 1966088 | tf_op jit(solution)/shard_map/ppermute | solution.py:786
  47.4 5.2 %mlp_down.1 = (bf16[512,1024]{1,0:T(8,128)(2,1)S(1)}, bf16[512,1024]{1,0:T(8,128)(2,1)S(1)}, bf16[1024,256]{1,0:T(8,128)(2,1)S(1)}, bf16[1024,128]{1,0:T(8,128)(2,1)S(1)}, bf16[1024,128]{1,0:T(8,128)(2,1)S(1)}) custom-call(s32[10]{0:T(128)S(1)} %compare_select_fusion.3.ids, bf16[1024,1024]{1,0:T(8,128)(2,1)S(1)} %get-tuple-element.116.act, ...), custom_call_target="tpu_custom_call" | custom-call | flops 1150000000 | bytes 3700000 | tf_op jit(solution)/shard_map/mlp_down/pallas_call | solution.py:452
  52.6 3.6 %collective-permute-start.11 = (bf16[512,1024]{1,0:T(8,128)(2,1)S(1)}, bf16[512,1024]{1,0:T(8,128)(2,1)S(1)}, u32[]{:S(2)}, u32[]{:S(2)}) collective-permute-start(bf16[512,1024]{1,0:T(8,128)(2,1)S(1)} %get-tuple-element.122.a), channel_id=1, source_target_pairs={{0,1},{3,2},{4,5},{7,6},{8,9},{11,10},{12,13},{15,14},{16,17},{19,... | collective-permute-start | bytes 3145736 | tf_op jit(solution)/shard_map/ppermute | solution.py:798
  56.2 6.9 %attend_backward.2 = (bf16[1024,256]{1,0:T(8,128)(2,1)S(1)}, bf16[1024,256]{1,0:T(8,128)(2,1)S(1)}, bf16[1024,128]{1,0:T(8,128)(2,1)S(1)}) custom-call(s32[10]{0:T(128)S(1)} %compare_select_fusion.3.ids, s32[2,3]{1,0:T(2,128)S(1)} %copy-done.12, bf16[1024,128]{1,0:T(8,128)(2,1)S(1)} %get-tuple-element.113.q, bf16[1024,128]{1,0:T(8,128)(2,1)S(1)} %get-tuple-element.124.g, ...), custom_call_target="tpu_custom_call" | custom-call | tf_op jit(solution)/shard_map/attend_backward/pallas_call | solution.py:348
  63.1 13.6 %collective-permute-start.12 = (bf16[1024,256]{1,0:T(8,128)(2,1)S(1)}, bf16[1024,256]{1,0:T(8,128)(2,1)S(1)}, u32[]{:S(2)}, u32[]{:S(2)}) collective-permute-start(bf16[1024,256]{1,0:T(8,128)(2,1)S(1)} %get-tuple-element.127), channel_id=1, source_target_pairs={{0,4},{4,0},{1,5},{5,1},{2,6},{6,2},{3,7},{7,3},{8,12},{12,8},{9,1... | collective-permute-start | bytes 1572872 | tf_op jit(solution)/shard_map/ppermute | solution.py:786
  78.2 6.9 %attend_backward.3 = (bf16[1024,256]{1,0:T(8,128)(2,1)S(1)}, bf16[1024,256]{1,0:T(8,128)(2,1)S(1)}, bf16[1024,128]{1,0:T(8,128)(2,1)S(1)}) custom-call(s32[10]{0:T(128)S(1)} %compare_select_fusion.3.ids, s32[2,3]{1,0:T(2,128)S(1)} %copy-done.12, bf16[1024,128]{1,0:T(8,128)(2,1)S(1)} %get-tuple-element.120.q, bf16[1024,128]{1,0:T(8,128)(2,1)S(1)} %get-tuple-element.129.g, ...), custom_call_target="tpu_custom_call" | custom-call | tf_op jit(solution)/shard_map/attend_backward/pallas_call | solution.py:348
  85.1 4.7 %collective-permute-start.15 = (bf16[1024,256]{1,0:T(8,128)(2,1)S(1)}, bf16[1024,256]{1,0:T(8,128)(2,1)S(1)}, u32[]{:S(2)}, u32[]{:S(2)}) collective-permute-start(bf16[1024,256]{1,0:T(8,128)(2,1)S(1)} %get-tuple-element.132), channel_id=1, source_target_pairs={{0,4},{4,0},{1,5},{5,1},{2,6},{6,2},{3,7},{7,3},{8,12},{12,8},{9,1... | collective-permute-start | bytes 1572872 | tf_op jit(solution)/shard_map/ppermute | solution.py:786
  90.9 7.8 %mlp_backward.1 = (bf16[1024,1024]{1,0:T(8,128)(2,1)S(1)}, bf16[1024,1024]{1,0:T(8,128)(2,1)S(1)}, f32[8,1024]{1,0:T(8,128)S(1)}) custom-call(s32[10]{0:T(128)S(1)} %compare_select_fusion.3.ids, bf16[1024,1024]{1,0:T(8,128)(2,1)S(1)} %copy-done.1, bf16[1024,1024]{1,0:T(8,128)(2,1)S(1)} %copy-done.2, f32[1,1024]{1,0:T(1,128)S(1)} %bitcast.34, ...), custom_call_target="tpu_custom_call" | custom-call | flops 1150000000 | bytes 3700000 | tf_op jit(solution)/shard_map/mlp_backward/pallas_call | solution.py:496
  98.7 6.1 %input_grad.1 = (bf16[528,1024]{1,0:T(8,128)(2,1)S(1)}, bf16[512,1024]{1,0:T(8,128)(2,1)S(1)}, bf16[1024,768]{1,0:T(8,128)(2,1)S(1)}, f32[8,1024]{1,0:T(8,128)S(1)}) custom-call(s32[10]{0:T(128)S(1)} %compare_select_fusion.3.ids, bf16[1024,1024]{1,0:T(8,128)(2,1)S(1)} %copy-done.1, bf16[1024,1024]{1,0:T(8,128)(2,1)S(1)} %get-tuple-element.140.e2, ...), custom_call_target="tpu_custom_call" | custom-call | tf_op jit(solution)/shard_map/input_grad/pallas_call | solution.py:617
  104.8 4.0 %collective-permute-start.17 = (bf16[528,1024]{1,0:T(8,128)(2,1)S(1)}, bf16[528,1024]{1,0:T(8,128)(2,1)S(1)}, u32[]{:S(2)}, u32[]{:S(2)}) collective-permute-start(bf16[528,1024]{1,0:T(8,128)(2,1)S(1)} %get-tuple-element.142.a), channel_id=1, source_target_pairs={{0,1},{3,2},{4,5},{7,6},{8,9},{11,10},{12,13},{15,14},{16,17},{19,... | collective-permute-start | bytes 3244040 | tf_op jit(solution)/shard_map/ppermute | solution.py:798
  109.9 6.1 %mlp_weights.1 = (bf16[2,2048,256]{2,1,0:T(8,128)(2,1)S(1)}, bf16[1,2048,256]{2,1,0:T(8,128)(2,1)S(1)}, bf16[1,2048,256]{2,1,0:T(8,128)(2,1)S(1)}) custom-call(s32[10]{0:T(128)S(1)} %compare_select_fusion.3.ids, bf16[1024,1024]{1,0:T(8,128)(2,1)S(1)} %get-tuple-element.116.act, bf16[1024,1024]{1,0:T(8,128)(2,1)S(1)} %copy-done.2, ...), custom_call_target="tpu_custom_call" | custom-call | tf_op jit(solution)/shard_map/mlp_weights/pallas_call | solution.py:549
  118.5 3.8 %rest_weights.1 = (bf16[2,1024,256]{2,1,0:T(8,128)(2,1)S(1)}, bf16[1,1024,256]{2,1,0:T(8,128)(2,1)S(1)}, bf16[1,1024,256]{2,1,0:T(8,128)(2,1)S(1)}) custom-call(s32[10]{0:T(128)S(1)} %compare_select_fusion.3.ids, bf16[1024,256]{1,0:T(8,128)(2,1)S(1)} %get-tuple-element.147.ctx, bf16[1024,1024]{1,0:T(8,128)(2,1)S(1)} %copy-done.2, ...), custom_call_target="tpu_custom_call" | custom-call | tf_op jit(solution)/shard_map/rest_weights/pallas_call | solution.py:549
  122.3 3.1 %collective-permute-done.17.b = bf16[528,1024]{1,0:T(8,128)(2,1)S(1)} collective-permute-done((bf16[528,1024]{1,0:T(8,128)(2,1)S(1)}, bf16[528,1024]{1,0:T(8,128)(2,1)S(1)}, u32[]{:S(2)}, u32[]{:S(2)}) %collective-permute-start.17) | collective-permute-done | bytes 1081376 | tf_op jit(solution)/shard_map/ppermute | solution.py:798
  127.4 8.9 %collective-permute-start.25 = (bf16[512,1024]{1,0:T(8,128)(2,1)S(1)}, bf16[512,1024]{1,0:T(8,128)(2,1)S(1)}, u32[]{:S(2)}, u32[]{:S(2)}) collective-permute-start(bf16[512,1024]{1,0:T(8,128)(2,1)S(1)} %get-tuple-element.165.a), channel_id=1, source_target_pairs={{0,1},{3,2},{4,5},{7,6},{8,9},{11,10},{12,13},{15,14},{16,17},{19,... | collective-permute-start | bytes 3145736 | tf_op jit(solution)/shard_map/ppermute | solution.py:798
  137.1 7.8 %collective-permute-done.18.refs_2_ = bf16[512,1024]{1,0:T(8,128)(2,1)S(1)} collective-permute-done((bf16[512,1024]{1,0:T(8,128)(2,1)S(1)}, bf16[512,1024]{1,0:T(8,128)(2,1)S(1)}, u32[]{:S(2)}, u32[]{:S(2)}) %collective-permute-start.18) | collective-permute-done | bytes 1048608 | tf_op jit(solution)/shard_map/ppermute | solution.py:809
  148.2 18.4 %collective-permute-done.19.refs_3_ = bf16[512,1024]{1,0:T(8,128)(2,1)S(1)} collective-permute-done((bf16[512,1024]{1,0:T(8,128)(2,1)S(1)}, bf16[512,1024]{1,0:T(8,128)(2,1)S(1)}, u32[]{:S(2)}, u32[]{:S(2)}) %collective-permute-start.19) | collective-permute-done | bytes 1048608 | tf_op jit(solution)/shard_map/ppermute | solution.py:809
  173.3 4.8 %collective-permute-start.35 = (bf16[2048,256]{1,0:T(8,128)(2,1)}, bf16[2048,256]{1,0:T(8,128)(2,1)}, u32[]{:S(2)}, u32[]{:S(2)}) collective-permute-start(bf16[2048,256]{1,0:T(8,128)(2,1)} %add.63.a), channel_id=1, source_target_pairs={{0,4},{4,0},{1,5},{5,1},{2,6},{6,2},{3,7},{7,3},{8,12},{12,8},{9,1... | collective-permute-start | bytes 3145736 | tf_op jit(solution)/shard_map/ppermute | solution.py:786
  178.1 5.7 %collective-permute-done.28.b = bf16[1024,256]{1,0:T(8,128)(2,1)S(1)} collective-permute-done((bf16[1024,256]{1,0:T(8,128)(2,1)S(1)}, bf16[1024,256]{1,0:T(8,128)(2,1)S(1)}, u32[]{:S(2)}, u32[]{:S(2)}) %collective-permute-start.28) | collective-permute-done | bytes 524320 | tf_op jit(solution)/shard_map/ppermute | solution.py:786
  184.7 2.7 %finish_in.3.refs_0_ = bf16[512,1024]{1,0:T(8,128)(2,1)} custom-call(bf16[512,1024]{1,0:T(8,128)(2,1)S(1)} %add.62.a, bf16[512,1024]{1,0:T(8,128)(2,1)S(1)} %collective-permute-done.27.b, bf16[1024,1024]{1,0:T(8,128)(2,1)S(1)} %copy-done.1, bf16[1024,1024]{1,0:T(8,128)(2,1)S(1)} %copy-done.2), custom_call_target="tpu_custom_call" | custom-call | tf_op jit(solution)/shard_map/finish_in/pallas_call | solution.py:639
  188.7 5.5 %collective-permute-start.34 = (bf16[1024,256]{1,0:T(8,128)(2,1)}, bf16[1024,256]{1,0:T(8,128)(2,1)S(1)}, u32[]{:S(2)}, u32[]{:S(2)}) collective-permute-start(bf16[1024,256]{1,0:T(8,128)(2,1)} %copy-done.5), channel_id=1, source_target_pairs={{0,4},{4,0},{1,5},{5,1},{2,6},{6,2},{3,7},{7,3},{8,12},{12,8},{9,1... | collective-permute-start | bytes 1572872 | tf_op jit(solution)/shard_map/ppermute | solution.py:786
  194.2 2.2 collective-permute-done.26.theirs.refs_1_
  198.2 3.4 %collective-permute-done.31.b = f32[8,1024]{1,0:T(8,128)S(1)} collective-permute-done((f32[8,1024]{1,0:T(8,128)S(1)}, f32[8,1024]{1,0:T(8,128)S(1)}, u32[]{:S(2)}, u32[]{:S(2)}) %collective-permute-start.31) | collective-permute-done | bytes 32800 | tf_op jit(solution)/shard_map/ppermute | solution.py:786
  201.6 5.3 %collective-permute-start.33 = (f32[8,1024]{1,0:T(8,128)S(1)}, f32[8,1024]{1,0:T(8,128)S(1)}, u32[]{:S(2)}, u32[]{:S(2)}) collective-permute-start(f32[8,1024]{1,0:T(8,128)S(1)} %add.66.a), channel_id=1, source_target_pairs={{0,4},{4,0},{1,5},{5,1},{2,6},{6,2},{3,7},{7,3},{8,12},{12,8},{9,1... | collective-permute-start | bytes 98312 | tf_op jit(solution)/shard_map/ppermute | solution.py:786
  210.6 3.0 %mlp_last.1 = (f32[1024,256]{1,0:T(8,128)}, f32[256,1024]{1,0:T(8,128)}) custom-call(bf16[2048,256]{1,0:T(8,128)(2,1)} %add.63.a, bf16[2048,256]{1,0:T(8,128)(2,1)} %collective-permute-done.35.b), custom_call_target="tpu_custom_call" | custom-call | tf_op jit(solution)/shard_map/mlp_last/pallas_call | solution.py:639
  215.9 2.9 %collective-permute-done.32.refs_1_ = bf16[512,1024]{1,0:T(8,128)(2,1)} collective-permute-done((bf16[512,1024]{1,0:T(8,128)(2,1)}, bf16[512,1024]{1,0:T(8,128)(2,1)}, u32[]{:S(2)}, u32[]{:S(2)}) %collective-permute-start.32) | collective-permute-done | bytes 1048608 | tf_op jit(solution)/shard_map/ppermute | solution.py:809
  218.8 2.6 %choose.5 = bf16[1024,1024]{1,0:T(8,128)(2,1)} custom-call(s32[1]{0:T(128)} %bitcast.flag, bf16[512,1024]{1,0:T(8,128)(2,1)} %finish_in.3.refs_0_, bf16[512,1024]{1,0:T(8,128)(2,1)} %collective-permute-done.32.refs_1_, bf16[1024,1024]{1,0:T(8,128)(2,1)} %choose.4.refs_2_), custom_call_target="tpu_custom_call", output_to_operand_aliasing={{}: (3, {})} | custom-call | tf_op jit(solution)/shard_map/choose/pallas_call | solution.py:639
  (142 shorter events, 47.8 us)
Async XLA Ops:
  0.6 12.3 %collective-permute-start.1 = (bf16[768,256]{1,0:T(8,128)(2,1)}, bf16[768,256]{1,0:T(8,128)(2,1)S(1)}, u32[]{:S(2)}, u32[]{:S(2)}) collective-permute-start(bf16[768,256]{1,0:T(8,128)(2,1)} %bitcast.29), channel_id=1, source_target_pairs={{0,16},{8,24},{16,0},{24,8},{1,17},{9,25},{17,1},{25,9},{2,18},{10... | collective-permute-start | bytes 1179656 | tf_op jit(solution)/shard_map/ppermute | solution.py:786
  3.6 11.1 %collective-permute-start = (bf16[768,256]{1,0:T(8,128)(2,1)}, bf16[768,256]{1,0:T(8,128)(2,1)S(1)}, u32[]{:S(2)}, u32[]{:S(2)}) collective-permute-start(bf16[768,256]{1,0:T(8,128)(2,1)} %bitcast.30), channel_id=1, source_target_pairs={{0,8},{8,0},{16,24},{24,16},{1,9},{9,1},{17,25},{25,17},{2,10},{10... | collective-permute-start | bytes 1179656 | tf_op jit(solution)/shard_map/ppermute | solution.py:786
  13.0 18.3 %collective-permute-start.3 = (bf16[1024,256]{1,0:T(8,128)(2,1)S(1)}, bf16[1024,256]{1,0:T(8,128)(2,1)S(1)}, u32[]{:S(2)}, u32[]{:S(2)}) collective-permute-start(bf16[1024,256]{1,0:T(8,128)(2,1)S(1)} %bitcast.25), channel_id=1, source_target_pairs={{0,16},{8,24},{16,0},{24,8},{1,17},{9,25},{17,1},{25,9},{2,18},{10... | collective-permute-start | bytes 1572872 | tf_op jit(solution)/shard_map/ppermute | solution.py:786
  18.6 24.0 %collective-permute-start.8 = (bf16[1280,256]{1,0:T(8,128)(2,1)S(1)}, bf16[1280,256]{1,0:T(8,128)(2,1)S(1)}, u32[]{:S(2)}, u32[]{:S(2)}) collective-permute-start(bf16[1280,256]{1,0:T(8,128)(2,1)S(1)} %constant_dynamic-update-slice_fusion.p0.d0), channel_id=1, source_target_pairs={{0,16},{8,24},{16,0},{24,8},{1,17},{9,25},{17,1},{25,9},{2,18},{10... | collective-permute-start | bytes 1966088 | tf_op jit(solution)/shard_map/ppermute | solution.py:786
  20.2 15.8 %collective-permute-start.5 = (bf16[1024,256]{1,0:T(8,128)(2,1)S(1)}, bf16[1024,256]{1,0:T(8,128)(2,1)S(1)}, u32[]{:S(2)}, u32[]{:S(2)}) collective-permute-start(bf16[1024,256]{1,0:T(8,128)(2,1)S(1)} %bitcast.26), channel_id=1, source_target_pairs={{0,8},{8,0},{16,24},{24,16},{1,9},{9,1},{17,25},{25,17},{2,10},{10... | collective-permute-start | bytes 1572872 | tf_op jit(solution)/shard_map/ppermute | solution.py:786
  20.2 14.3 %collective-permute-start.4 = (bf16[1024,256]{1,0:T(8,128)(2,1)S(1)}, bf16[1024,256]{1,0:T(8,128)(2,1)S(1)}, u32[]{:S(2)}, u32[]{:S(2)}) collective-permute-start(bf16[1024,256]{1,0:T(8,128)(2,1)S(1)} %get-tuple-element.106.kv.refs_0_), channel_id=1, source_target_pairs={{0,4},{4,0},{1,5},{5,1},{2,6},{6,2},{3,7},{7,3},{8,12},{12,8},{9,1... | collective-permute-start | bytes 1572872 | tf_op jit(solution)/shard_map/ppermute | solution.py:786
  31.3 4.7 %collective-permute-start.6 = (bf16[1024,256]{1,0:T(8,128)(2,1)S(1)}, bf16[1024,256]{1,0:T(8,128)(2,1)S(1)}, u32[]{:S(2)}, u32[]{:S(2)}) collective-permute-start(bf16[1024,256]{1,0:T(8,128)(2,1)S(1)} %collective-permute-done.3.p2.u2), channel_id=1, source_target_pairs={{0,8},{8,0},{16,24},{24,16},{1,9},{9,1},{17,25},{25,17},{2,10},{10... | collective-permute-start | bytes 1572872 | tf_op jit(solution)/shard_map/ppermute | solution.py:786
  31.5 14.3 %collective-permute-start.10 = (bf16[1024,256]{1,0:T(8,128)(2,1)S(1)}, bf16[1024,256]{1,0:T(8,128)(2,1)S(1)}, u32[]{:S(2)}, u32[]{:S(2)}) collective-permute-start(bf16[1024,256]{1,0:T(8,128)(2,1)S(1)} %get-tuple-element.104.kv.refs_0_), channel_id=1, source_target_pairs={{0,4},{4,0},{1,5},{5,1},{2,6},{6,2},{3,7},{7,3},{8,12},{12,8},{9,1... | collective-permute-start | bytes 1572872 | tf_op jit(solution)/shard_map/ppermute | solution.py:786
  34.6 12.7 %collective-permute-start.7 = (bf16[1280,256]{1,0:T(8,128)(2,1)S(1)}, bf16[1280,256]{1,0:T(8,128)(2,1)S(1)}, u32[]{:S(2)}, u32[]{:S(2)}) collective-permute-start(bf16[1280,256]{1,0:T(8,128)(2,1)S(1)} %constant_dynamic-update-slice_fusion.p0.d0), channel_id=1, source_target_pairs={{0,8},{8,0},{16,24},{24,16},{1,9},{9,1},{17,25},{25,17},{2,10},{10... | collective-permute-start | bytes 1966088 | tf_op jit(solution)/shard_map/ppermute | solution.py:786
  42.6 4.9 %collective-permute-start.9 = (bf16[1280,256]{1,0:T(8,128)(2,1)S(1)}, bf16[1280,256]{1,0:T(8,128)(2,1)S(1)}, u32[]{:S(2)}, u32[]{:S(2)}) collective-permute-start(bf16[1280,256]{1,0:T(8,128)(2,1)S(1)} %collective-permute-done.8.p2.d2), channel_id=1, source_target_pairs={{0,8},{8,0},{16,24},{24,16},{1,9},{9,1},{17,25},{25,17},{2,10},{10... | collective-permute-start | bytes 1966088 | tf_op jit(solution)/shard_map/ppermute | solution.py:786
  52.6 37.2 %collective-permute-start.11 = (bf16[512,1024]{1,0:T(8,128)(2,1)S(1)}, bf16[512,1024]{1,0:T(8,128)(2,1)S(1)}, u32[]{:S(2)}, u32[]{:S(2)}) collective-permute-start(bf16[512,1024]{1,0:T(8,128)(2,1)S(1)} %get-tuple-element.122.a), channel_id=1, source_target_pairs={{0,1},{3,2},{4,5},{7,6},{8,9},{11,10},{12,13},{15,14},{16,17},{19,... | collective-permute-start | bytes 3145736 | tf_op jit(solution)/shard_map/ppermute | solution.py:798
  63.1 26.7 %collective-permute-start.12 = (bf16[1024,256]{1,0:T(8,128)(2,1)S(1)}, bf16[1024,256]{1,0:T(8,128)(2,1)S(1)}, u32[]{:S(2)}, u32[]{:S(2)}) collective-permute-start(bf16[1024,256]{1,0:T(8,128)(2,1)S(1)} %get-tuple-element.127), channel_id=1, source_target_pairs={{0,4},{4,0},{1,5},{5,1},{2,6},{6,2},{3,7},{7,3},{8,12},{12,8},{9,1... | collective-permute-start | bytes 1572872 | tf_op jit(solution)/shard_map/ppermute | solution.py:786
  76.7 32.2 %collective-permute-start.14 = (bf16[512,1024]{1,0:T(8,128)(2,1)S(1)}, bf16[512,1024]{1,0:T(8,128)(2,1)S(1)}, u32[]{:S(2)}, u32[]{:S(2)}) collective-permute-start(bf16[512,1024]{1,0:T(8,128)(2,1)S(1)} %get-tuple-element.139.a), channel_id=1, source_target_pairs={{0,1},{3,2},{4,5},{7,6},{8,9},{11,10},{12,13},{15,14},{16,17},{19,... | collective-permute-start | bytes 3145736 | tf_op jit(solution)/shard_map/ppermute | solution.py:798
  85.1 13.6 %collective-permute-start.15 = (bf16[1024,256]{1,0:T(8,128)(2,1)S(1)}, bf16[1024,256]{1,0:T(8,128)(2,1)S(1)}, u32[]{:S(2)}, u32[]{:S(2)}) collective-permute-start(bf16[1024,256]{1,0:T(8,128)(2,1)S(1)} %get-tuple-element.132), channel_id=1, source_target_pairs={{0,4},{4,0},{1,5},{5,1},{2,6},{6,2},{3,7},{7,3},{8,12},{12,8},{9,1... | collective-permute-start | bytes 1572872 | tf_op jit(solution)/shard_map/ppermute | solution.py:786
  90.1 26.4 %collective-permute-start.13 = (bf16[512,1024]{1,0:T(8,128)(2,1)S(1)}, bf16[512,1024]{1,0:T(8,128)(2,1)S(1)}, u32[]{:S(2)}, u32[]{:S(2)}) collective-permute-start(bf16[512,1024]{1,0:T(8,128)(2,1)S(1)} %add.60.a), channel_id=1, source_target_pairs={{1,2},{2,1},{5,6},{6,5},{9,10},{10,9},{13,14},{14,13},{17,18},{18,... | collective-permute-start | bytes 3145736 | tf_op jit(solution)/shard_map/ppermute | solution.py:804
  104.8 20.6 %collective-permute-start.17 = (bf16[528,1024]{1,0:T(8,128)(2,1)S(1)}, bf16[528,1024]{1,0:T(8,128)(2,1)S(1)}, u32[]{:S(2)}, u32[]{:S(2)}) collective-permute-start(bf16[528,1024]{1,0:T(8,128)(2,1)S(1)} %get-tuple-element.142.a), channel_id=1, source_target_pairs={{0,1},{3,2},{4,5},{7,6},{8,9},{11,10},{12,13},{15,14},{16,17},{19,... | collective-permute-start | bytes 3244040 | tf_op jit(solution)/shard_map/ppermute | solution.py:798
  109.1 16.5 %collective-permute-start.16 = (bf16[512,1024]{1,0:T(8,128)(2,1)S(1)}, bf16[512,1024]{1,0:T(8,128)(2,1)S(1)}, u32[]{:S(2)}, u32[]{:S(2)}) collective-permute-start(bf16[512,1024]{1,0:T(8,128)(2,1)S(1)} %add.61.a), channel_id=1, source_target_pairs={{1,2},{2,1},{5,6},{6,5},{9,10},{10,9},{13,14},{14,13},{17,18},{18,... | collective-permute-start | bytes 3145736 | tf_op jit(solution)/shard_map/ppermute | solution.py:804
  116.0 20.3 %collective-permute-start.22 = (bf16[1,2048,256]{2,1,0:T(8,128)(2,1)S(1)}, bf16[1,2048,256]{2,1,0:T(8,128)(2,1)S(1)}, u32[]{:S(2)}, u32[]{:S(2)}) collective-permute-start(bf16[1,2048,256]{2,1,0:T(8,128)(2,1)S(1)} %get-tuple-element.156), channel_id=1, source_target_pairs={{0,8},{8,0},{16,24},{24,16},{1,9},{9,1},{17,25},{25,17},{2,10},{10... | collective-permute-start | bytes 3145736 | tf_op jit(solution)/shard_map/ppermute | solution.py:786
  116.1 20.3 %collective-permute-start.23 = (bf16[1,2048,256]{2,1,0:T(8,128)(2,1)S(1)}, bf16[1,2048,256]{2,1,0:T(8,128)(2,1)S(1)}, u32[]{:S(2)}, u32[]{:S(2)}) collective-permute-start(bf16[1,2048,256]{2,1,0:T(8,128)(2,1)S(1)} %get-tuple-element.157), channel_id=1, source_target_pairs={{0,8},{8,0},{16,24},{24,16},{1,9},{9,1},{17,25},{25,17},{2,10},{10... | collective-permute-start | bytes 3145736 | tf_op jit(solution)/shard_map/ppermute | solution.py:786
  117.0 27.9 %collective-permute-start.18 = (bf16[512,1024]{1,0:T(8,128)(2,1)S(1)}, bf16[512,1024]{1,0:T(8,128)(2,1)S(1)}, u32[]{:S(2)}, u32[]{:S(2)}) collective-permute-start(bf16[512,1024]{1,0:T(8,128)(2,1)S(1)} %finish_out.2.refs_0_), channel_id=1, source_target_pairs={{1,0},{2,3},{5,4},{6,7},{9,8},{10,11},{13,12},{14,15},{17,16},{18,... | collective-permute-start | bytes 3145736 | tf_op jit(solution)/shard_map/ppermute | solution.py:809
  126.1 40.4 %collective-permute-start.19 = (bf16[512,1024]{1,0:T(8,128)(2,1)S(1)}, bf16[512,1024]{1,0:T(8,128)(2,1)S(1)}, u32[]{:S(2)}, u32[]{:S(2)}) collective-permute-start(bf16[512,1024]{1,0:T(8,128)(2,1)S(1)} %finish_out.3.refs_1_), channel_id=1, source_target_pairs={{1,0},{2,3},{5,4},{6,7},{9,8},{10,11},{13,12},{14,15},{17,16},{18,... | collective-permute-start | bytes 3145736 | tf_op jit(solution)/shard_map/ppermute | solution.py:809
  127.4 39.1 %collective-permute-start.25 = (bf16[512,1024]{1,0:T(8,128)(2,1)S(1)}, bf16[512,1024]{1,0:T(8,128)(2,1)S(1)}, u32[]{:S(2)}, u32[]{:S(2)}) collective-permute-start(bf16[512,1024]{1,0:T(8,128)(2,1)S(1)} %get-tuple-element.165.a), channel_id=1, source_target_pairs={{0,1},{3,2},{4,5},{7,6},{8,9},{11,10},{12,13},{15,14},{16,17},{19,... | collective-permute-start | bytes 3145736 | tf_op jit(solution)/shard_map/ppermute | solution.py:798
  136.3 10.2 %collective-permute-start.20 = (bf16[1,1024,256]{2,1,0:T(8,128)(2,1)S(1)}, bf16[1,1024,256]{2,1,0:T(8,128)(2,1)S(1)}, u32[]{:S(2)}, u32[]{:S(2)}) collective-permute-start(bf16[1,1024,256]{2,1,0:T(8,128)(2,1)S(1)} %get-tuple-element.154), channel_id=1, source_target_pairs={{0,8},{8,0},{16,24},{24,16},{1,9},{9,1},{17,25},{25,17},{2,10},{10... | collective-permute-start | bytes 1572872 | tf_op jit(solution)/shard_map/ppermute | solution.py:786
  136.4 31.1 %collective-permute-start.24 = (bf16[528,1024]{1,0:T(8,128)(2,1)S(1)}, bf16[528,1024]{1,0:T(8,128)(2,1)S(1)}, u32[]{:S(2)}, u32[]{:S(2)}) collective-permute-start(bf16[528,1024]{1,0:T(8,128)(2,1)S(1)} %add_extra.1.a), channel_id=1, source_target_pairs={{1,2},{2,1},{5,6},{6,5},{9,10},{10,9},{13,14},{14,13},{17,18},{18,... | collective-permute-start | bytes 3244040 | tf_op jit(solution)/shard_map/ppermute | solution.py:804
  146.6 25.6 %collective-permute-start.29 = (bf16[2048,256]{1,0:T(8,128)(2,1)S(1)}, bf16[2048,256]{1,0:T(8,128)(2,1)S(1)}, u32[]{:S(2)}, u32[]{:S(2)}) collective-permute-start(bf16[2048,256]{1,0:T(8,128)(2,1)S(1)} %get-tuple-element.169), channel_id=1, source_target_pairs={{0,16},{8,24},{16,0},{24,8},{1,17},{9,25},{17,1},{25,9},{2,18},{10... | collective-permute-start | bytes 3145736 | tf_op jit(solution)/shard_map/ppermute | solution.py:786
  166.8 17.9 %collective-permute-start.27 = (bf16[512,1024]{1,0:T(8,128)(2,1)S(1)}, bf16[512,1024]{1,0:T(8,128)(2,1)S(1)}, u32[]{:S(2)}, u32[]{:S(2)}) collective-permute-start(bf16[512,1024]{1,0:T(8,128)(2,1)S(1)} %add.62.a), channel_id=1, source_target_pairs={{1,2},{2,1},{5,6},{6,5},{9,10},{10,9},{13,14},{14,13},{17,18},{18,... | collective-permute-start | bytes 3145736 | tf_op jit(solution)/shard_map/ppermute | solution.py:804
  169.3 27.0 %collective-permute-start.26 = (bf16[528,1024]{1,0:T(8,128)(2,1)S(1)}, bf16[528,1024]{1,0:T(8,128)(2,1)S(1)}, u32[]{:S(2)}, u32[]{:S(2)}) collective-permute-start(bf16[528,1024]{1,0:T(8,128)(2,1)S(1)} %finish_in.2.ours.refs_0_), channel_id=1, source_target_pairs={{1,0},{2,3},{5,4},{6,7},{9,8},{10,11},{13,12},{14,15},{17,16},{18,... | collective-permute-start | bytes 3244040 | tf_op jit(solution)/shard_map/ppermute | solution.py:809
  170.6 13.1 %collective-permute-start.28 = (bf16[1024,256]{1,0:T(8,128)(2,1)S(1)}, bf16[1024,256]{1,0:T(8,128)(2,1)S(1)}, u32[]{:S(2)}, u32[]{:S(2)}) collective-permute-start(bf16[1024,256]{1,0:T(8,128)(2,1)S(1)} %get-tuple-element.168), channel_id=1, source_target_pairs={{0,16},{8,24},{16,0},{24,8},{1,17},{9,25},{17,1},{25,9},{2,18},{10... | collective-permute-start | bytes 1572872 | tf_op jit(solution)/shard_map/ppermute | solution.py:786
  173.3 37.3 %collective-permute-start.35 = (bf16[2048,256]{1,0:T(8,128)(2,1)}, bf16[2048,256]{1,0:T(8,128)(2,1)}, u32[]{:S(2)}, u32[]{:S(2)}) collective-permute-start(bf16[2048,256]{1,0:T(8,128)(2,1)} %add.63.a), channel_id=1, source_target_pairs={{0,4},{4,0},{1,5},{5,1},{2,6},{6,2},{3,7},{7,3},{8,12},{12,8},{9,1... | collective-permute-start | bytes 3145736 | tf_op jit(solution)/shard_map/ppermute | solution.py:786
  187.4 31.4 %collective-permute-start.32 = (bf16[512,1024]{1,0:T(8,128)(2,1)}, bf16[512,1024]{1,0:T(8,128)(2,1)}, u32[]{:S(2)}, u32[]{:S(2)}) collective-permute-start(bf16[512,1024]{1,0:T(8,128)(2,1)} %finish_in.3.refs_0_), channel_id=1, source_target_pairs={{1,0},{2,3},{5,4},{6,7},{9,8},{10,11},{13,12},{14,15},{17,16},{18,... | collective-permute-start | bytes 3145736 | tf_op jit(solution)/shard_map/ppermute | solution.py:809
  188.7 25.0 %collective-permute-start.34 = (bf16[1024,256]{1,0:T(8,128)(2,1)}, bf16[1024,256]{1,0:T(8,128)(2,1)S(1)}, u32[]{:S(2)}, u32[]{:S(2)}) collective-permute-start(bf16[1024,256]{1,0:T(8,128)(2,1)} %copy-done.5), channel_id=1, source_target_pairs={{0,4},{4,0},{1,5},{5,1},{2,6},{6,2},{3,7},{7,3},{8,12},{12,8},{9,1... | collective-permute-start | bytes 1572872 | tf_op jit(solution)/shard_map/ppermute | solution.py:786
  201.6 13.0 %collective-permute-start.33 = (f32[8,1024]{1,0:T(8,128)S(1)}, f32[8,1024]{1,0:T(8,128)S(1)}, u32[]{:S(2)}, u32[]{:S(2)}) collective-permute-start(f32[8,1024]{1,0:T(8,128)S(1)} %add.66.a), channel_id=1, source_target_pairs={{0,4},{4,0},{1,5},{5,1},{2,6},{6,2},{3,7},{7,3},{8,12},{12,8},{9,1... | collective-permute-start | bytes 98312 | tf_op jit(solution)/shard_map/ppermute | solution.py:786
  (29 other events, 210.7 us)

commit v2 on v1

--- a/solution.py
+++ b/solution.py
@@ -33,12 +33,9 @@
     return pltpu.CompilerParams(vmem_limit_bytes=mib * 1024 * 1024)
 
 
-SCALE = 1.0
-
-
 def cost(micros):
     return pl.CostEstimate(
-        flops=int(1.15e9 * micros * SCALE), bytes_accessed=int(3.7e6 * micros * SCALE), transcendentals=0
+        flops=int(1.15e9 * micros), bytes_accessed=int(3.7e6 * micros), transcendentals=0
     )
 
 
@@ -627,12 +624,12 @@
         + [s((rows, units), bf16), s((8, width), f32)],
         scratch_shapes=[pltpu.VMEM((tile, width), f32)],
         compiler_params=params(24),
-        cost_estimate=cost(0),
+        cost_estimate=cost(4),
         name="input_grad",
     )(ids, x, e2, gain, sums, *qgs, *tables, *weights, *grads)
 
 
-def call(kernel, name, args, shapes, grid=1, in_specs=None, out_specs=None, aliases=None, mib=16):
+def call(kernel, name, args, shapes, grid=1, in_specs=None, out_specs=None, aliases=None, mib=16, micros=0):
     s = jax.ShapeDtypeStruct
     many = isinstance(shapes, list)
     shapes = [s(*shape) for shape in (shapes if many else [shapes])]
@@ -644,7 +641,7 @@
         out_shape=shapes,
         input_output_aliases=aliases or {},
         compiler_params=params(mib),
-        cost_estimate=cost(0),
+        cost_estimate=cost(micros),
         name=name,
     )(*args)
     return out if many else out[0]
@@ -756,13 +753,13 @@
     there[...] = (keep[1].astype(f32) + far[0].astype(f32)).astype(bf16)
 
 
-def halves(keep, got, grid=2):
+def halves(keep, got, grid=2, micros=0):
     tall, width = keep.shape[1:]
     block = lambda n: pl.BlockSpec((n, tall // grid, width), lambda i: (0, i, 0))
     row = pl.BlockSpec((tall // grid, width), lambda i: (i, 0))
     return call(
         halves_kernel, "halves", (keep, *got), [((tall, width), f32), ((tall, width), bf16)],
-        grid, [block(2), block(1), block(1)], [row, row],
+        grid, [block(2), block(1), block(1)], [row, row], micros=micros,
     )
 
 
@@ -959,34 +956,38 @@
         ],
     )
     mark = out.add(1, made[0])
+    mark = out.end(0, mark)
     mlp_keep, *mlp_send = weight_parts(
         mlp_weights_kernel, "mlp_weights", ids, 2 * units,
         activated, cotangent, normed_two, after(hidden_grad, mark),
     )
+    mark = mlp_keep
     mlp_got = swap(mlp_send, "fsdp", 4, 1)
-    mark = out.end(0, mlp_keep)
+    mark = line.add(0, mark)
+    mark = out.end(1, mark)
+    mark = out.arrive(0, mark)
+    mlp_here, mlp_there = halves(mlp_keep, after(mlp_got, mark), micros=0)
+    mlp_got = swap(mlp_there, "fsdp", 4, 2)
+    mark = mlp_here
     rest_keep, *rest_send = weight_parts(
         rest_weights_kernel, "rest_weights", ids, 4 * SHARD,
         context_low, cotangent, normed_one, after(projected_grad, mark),
     )
     rest_got = swap(rest_send, "fsdp", 4, 1)
-    mark = line.add(0, rest_keep)
-    mark = out.end(1, mark)
-    mark = out.arrive(0, mark)
-    mlp_here, mlp_there = halves(mlp_keep, after(mlp_got, mark))
-    mlp_got = swap(mlp_there, "fsdp", 4, 2)
-    rest_here, rest_there = halves(rest_keep, after(rest_got, mlp_here))
-    rest_got = swap(rest_there, "fsdp", 4, 2)
-    mark = out.arrive(1, rest_here)
+    mark = rest_keep
     mark = line.add(1, mark)
     mark = line.end(0, mark)
+    mark = out.arrive(1, mark)
     mlp_part = add(mlp_here, after(mlp_got, mark))
     if split:
         mlp_got = swap(mlp_part, "context", 2, 1)
-    rest_part = add(rest_here, after(rest_got, mlp_part))
+    rest_here, rest_there = halves(rest_keep, after(rest_got, mlp_part))
+    rest_got = swap(rest_there, "fsdp", 4, 2)
+    mark = line.end(1, rest_here)
+    rest_part = add(rest_here, after(rest_got, mark))
     if split:
         rest_got = swap(rest_part, "context", 2, 1)
-    mark = line.end(1, rest_part)
+    mark = rest_part
     norms = line.decode(mark)
     sums = jnp.concatenate([norms[0:2], sums[2:4], norms[2:4], sums[6:8]], axis=0)
     mark = sums

time: 225 us -> 216 us (0.960); the launches traced: 222 us -> 216 us
  starting transfers between devices: 74.5 us -> 62.4 us
  waiting for transfers between devices: 50.4 us -> 56.2 us
    ppermute x4, waiting for transfers between devices: 3.08 us -> 18.3 us  [__init__(): lax.ppermute(part, 'tensor', [(0, 1), (3, 2)])]
    ppermute x4, waiting for transfers between devices: 31.2 us -> 21.4 us  [end(): self.third[i] = lax.ppermute(self.finals[i], 'tensor', [(1, 0), (2, 3)])]
    ppermute x24, starting transfers between devices: 48.2 us -> 40.7 us  [swap(): return jax.tree.map(lambda v: lax.ppermute(v, axis, pairs), values)]
    ppermute x4, starting transfers between devices: 18 us -> 13.5 us  [__init__(): lax.ppermute(part, 'tensor', [(0, 1), (3, 2)])]
    unnamed x52 -> x56, local copies, waits for them, and re-layouts: 6.67 us -> 4.93 us
  transfers between devices with their start and end apart: 36 -> 36, of which waited for: 14 -> 12; matrix products, arithmetic and copies ran while one was open for 2% -> 2% of each run, Pallas kernels for 35% -> 36%
where the time goes in v2:
time: 216 us
  Pallas kernels  86.7 us (40%)
  starting transfers between devices  62.4 us (29%)
  waiting for transfers between devices  56.2 us (26%)
  local copies, waits for them, and re-layouts  7.27 us (3%)
    ppermute x24, starting transfers between devices, swap(): return jax.tree.map(lambda v: lax.ppermute(v, axis, pairs), values)  40.7 us
    ppermute x4, waiting for transfers between devices, end(): self.third[i] = lax.ppermute(self.finals[i], 'tensor', [(1, 0), (2, 3)])  21.4 us
    pallas_call x22, Pallas kernels, call(): pl.pallas_call(kernel, grid=(grid,), in_specs=in_specs or [whole(a.shape)...  21.1 us
    ppermute x4, waiting for transfers between devices, __init__(): lax.ppermute(part, 'tensor', [(0, 1), (3, 2)])  18.3 us
    ppermute x24, waiting for transfers between devices, swap(): return jax.tree.map(lambda v: lax.ppermute(v, axis, pairs), values)  16.5 us
    pallas_call x2, Pallas kernels, attend_backward(): pl.pallas_call(partial(attend_backward_kernel, slots, split), grid=(), in...  13.9 us
    ppermute x4, starting transfers between devices, __init__(): lax.ppermute(part, 'tensor', [(0, 1), (3, 2)])  13.5 us
    pallas_call x4, Pallas kernels, attend_forward(): pl.pallas_call(partial(attend_forward_kernel, slots, low, count, carried...  12.4 us
  transfers between devices with their start and end apart: 36, of which 12 were waited for; matrix products, arithmetic and copies ran while one was open for 2% of the time, Pallas kernels for 36%

profile of v2, /device:TPU:0, one launch (start us, length us, event | category | flops | bytes accessed | tf_op | source)
XLA Modules:
  0.0 216.2 jit_solution(2181835680602613205)
XLA Ops:
  0.6 3.0 %collective-permute-start.1 = (bf16[768,256]{1,0:T(8,128)(2,1)}, bf16[768,256]{1,0:T(8,128)(2,1)S(1)}, u32[]{:S(2)}, u32[]{:S(2)}) collective-permute-start(bf16[768,256]{1,0:T(8,128)(2,1)} %bitcast.40), channel_id=1, source_target_pairs={{0,16},{8,24},{16,0},{24,8},{1,17},{9,25},{17,1},{25,9},{2,18},{10... | collective-permute-start | bytes 1179656 | tf_op jit(solution)/shard_map/ppermute | solution.py:783
  13.0 1.8 collective-permute-start.3
  14.8 3.7 %project.1 = (bf16[1024,128]{1,0:T(8,128)(2,1)S(1)}, bf16[1024,128]{1,0:T(8,128)(2,1)S(1)}, bf16[1024,256]{1,0:T(8,128)(2,1)S(1)}, bf16[1024,256]{1,0:T(8,128)(2,1)S(1)}) custom-call(s32[10]{0:T(128)S(1)} %compare_select_fusion.3.ids, bf16[1024,1024]{1,0:T(8,128)(2,1)S(1)} %norm.1.n1, bf16[768,256]{1,0:T(8,128)(2,1)S(1)} %bitcast.42, ...), custom_call_target="tpu_custom_call" | custom-call | flops 4944999936 | bytes 15910000 | tf_op jit(solution)/shard_map/project/pallas_call | solution.py:108
  21.9 4.8 %attend_forward.4 = (f32[16,512]{1,0:T(8,128)S(1)}, f32[256,512]{1,0:T(8,128)S(1)}) custom-call(s32[10]{0:T(128)S(1)} %compare_select_fusion.3.ids, s32[2,3]{1,0:T(2,128)S(1)} %copy-done.11, bf16[1024,128]{1,0:T(8,128)(2,1)S(1)} %get-tuple-element.113.q, bf16[1024,256]{1,0:T(8,128)(2,1)S(1)} %get-tuple-element.106.kv.refs_0_), custom_call_target="tpu_custom_call" | custom-call | tf_op jit(solution)/shard_map/attend_forward/pallas_call | solution.py:232
  26.6 4.8 %attend_forward.5 = (f32[16,512]{1,0:T(8,128)S(1)}, f32[256,512]{1,0:T(8,128)S(1)}) custom-call(s32[10]{0:T(128)S(1)} %compare_select_fusion.3.ids, s32[2,3]{1,0:T(2,128)S(1)} %copy-done.11, bf16[1024,128]{1,0:T(8,128)(2,1)S(1)} %get-tuple-element.120.q, bf16[1024,256]{1,0:T(8,128)(2,1)S(1)} %get-tuple-element.104.kv.refs_0_), custom_call_target="tpu_custom_call" | custom-call | tf_op jit(solution)/shard_map/attend_forward/pallas_call | solution.py:232
  32.1 2.6 %collective-permute-done.4.kv.refs_1_ = bf16[1024,256]{1,0:T(8,128)(2,1)S(1)} collective-permute-done((bf16[1024,256]{1,0:T(8,128)(2,1)S(1)}, bf16[1024,256]{1,0:T(8,128)(2,1)S(1)}, u32[]{:S(2)}, u32[]{:S(2)}) %collective-permute-start.4) | collective-permute-done | bytes 524320 | tf_op jit(solution)/shard_map/ppermute | solution.py:783
  36.2 6.4 %mlp_up.1 = (bf16[1024,1024]{1,0:T(8,128)(2,1)S(1)}, bf16[1024,1024]{1,0:T(8,128)(2,1)S(1)}, bf16[1024,1024]{1,0:T(8,128)(2,1)S(1)}) custom-call(s32[10]{0:T(128)S(1)} %compare_select_fusion.3.ids, bf16[1024,1024]{1,0:T(8,128)(2,1)S(1)} %copy-done.1, f32[1,1024]{1,0:T(1,128)S(1)} %bitcast.29, f32[1,1024]{1,0:T(1,128)S(1)} %bitcast.35, ...), custom_call_target="tpu_custom_call" | custom-call | tf_op jit(solution)/shard_map/mlp_up/pallas_call | solution.py:401
  42.7 1.9 collective-permute-start.9
  47.4 5.3 %mlp_down.1 = (bf16[512,1024]{1,0:T(8,128)(2,1)S(1)}, bf16[512,1024]{1,0:T(8,128)(2,1)S(1)}, bf16[1024,256]{1,0:T(8,128)(2,1)S(1)}, bf16[1024,128]{1,0:T(8,128)(2,1)S(1)}, bf16[1024,128]{1,0:T(8,128)(2,1)S(1)}) custom-call(s32[10]{0:T(128)S(1)} %compare_select_fusion.3.ids, bf16[1024,1024]{1,0:T(8,128)(2,1)S(1)} %get-tuple-element.116.act, ...), custom_call_target="tpu_custom_call" | custom-call | flops 1150000000 | bytes 3700000 | tf_op jit(solution)/shard_map/mlp_down/pallas_call | solution.py:449
  52.7 3.5 %collective-permute-start.11 = (bf16[512,1024]{1,0:T(8,128)(2,1)S(1)}, bf16[512,1024]{1,0:T(8,128)(2,1)S(1)}, u32[]{:S(2)}, u32[]{:S(2)}) collective-permute-start(bf16[512,1024]{1,0:T(8,128)(2,1)S(1)} %get-tuple-element.122.a), channel_id=1, source_target_pairs={{0,1},{3,2},{4,5},{7,6},{8,9},{11,10},{12,13},{15,14},{16,17},{19,... | collective-permute-start | bytes 3145736 | tf_op jit(solution)/shard_map/ppermute | solution.py:795
  56.2 6.9 %attend_backward.2 = (bf16[1024,256]{1,0:T(8,128)(2,1)S(1)}, bf16[1024,256]{1,0:T(8,128)(2,1)S(1)}, bf16[1024,128]{1,0:T(8,128)(2,1)S(1)}) custom-call(s32[10]{0:T(128)S(1)} %compare_select_fusion.3.ids, s32[2,3]{1,0:T(2,128)S(1)} %copy-done.11, bf16[1024,128]{1,0:T(8,128)(2,1)S(1)} %get-tuple-element.113.q, bf16[1024,128]{1,0:T(8,128)(2,1)S(1)} %get-tuple-element.124.g, ...), custom_call_target="tpu_custom_call" | custom-call | tf_op jit(solution)/shard_map/attend_backward/pallas_call | solution.py:345
  63.2 13.7 %collective-permute-start.12 = (bf16[1024,256]{1,0:T(8,128)(2,1)S(1)}, bf16[1024,256]{1,0:T(8,128)(2,1)S(1)}, u32[]{:S(2)}, u32[]{:S(2)}) collective-permute-start(bf16[1024,256]{1,0:T(8,128)(2,1)S(1)} %get-tuple-element.127), channel_id=1, source_target_pairs={{0,4},{4,0},{1,5},{5,1},{2,6},{6,2},{3,7},{7,3},{8,12},{12,8},{9,1... | collective-permute-start | bytes 1572872 | tf_op jit(solution)/shard_map/ppermute | solution.py:783
  78.4 7.0 %attend_backward.3 = (bf16[1024,256]{1,0:T(8,128)(2,1)S(1)}, bf16[1024,256]{1,0:T(8,128)(2,1)S(1)}, bf16[1024,128]{1,0:T(8,128)(2,1)S(1)}) custom-call(s32[10]{0:T(128)S(1)} %compare_select_fusion.3.ids, s32[2,3]{1,0:T(2,128)S(1)} %copy-done.11, bf16[1024,128]{1,0:T(8,128)(2,1)S(1)} %get-tuple-element.120.q, bf16[1024,128]{1,0:T(8,128)(2,1)S(1)} %get-tuple-element.129.g, ...), custom_call_target="tpu_custom_call" | custom-call | tf_op jit(solution)/shard_map/attend_backward/pallas_call | solution.py:345
  85.4 4.7 %collective-permute-start.15 = (bf16[1024,256]{1,0:T(8,128)(2,1)S(1)}, bf16[1024,256]{1,0:T(8,128)(2,1)S(1)}, u32[]{:S(2)}, u32[]{:S(2)}) collective-permute-start(bf16[1024,256]{1,0:T(8,128)(2,1)S(1)} %get-tuple-element.132), channel_id=1, source_target_pairs={{0,4},{4,0},{1,5},{5,1},{2,6},{6,2},{3,7},{7,3},{8,12},{12,8},{9,1... | collective-permute-start | bytes 1572872 | tf_op jit(solution)/shard_map/ppermute | solution.py:783
  91.1 8.0 %mlp_backward.1 = (bf16[1024,1024]{1,0:T(8,128)(2,1)S(1)}, bf16[1024,1024]{1,0:T(8,128)(2,1)S(1)}, f32[8,1024]{1,0:T(8,128)S(1)}) custom-call(s32[10]{0:T(128)S(1)} %compare_select_fusion.3.ids, bf16[1024,1024]{1,0:T(8,128)(2,1)S(1)} %copy-done.1, bf16[1024,1024]{1,0:T(8,128)(2,1)S(1)} %copy-done.2, f32[1,1024]{1,0:T(1,128)S(1)} %bitcast.30, ...), custom_call_target="tpu_custom_call" | custom-call | flops 1150000000 | bytes 3700000 | tf_op jit(solution)/shard_map/mlp_backward/pallas_call | solution.py:493
  99.2 6.1 %input_grad.1 = (bf16[528,1024]{1,0:T(8,128)(2,1)S(1)}, bf16[512,1024]{1,0:T(8,128)(2,1)S(1)}, bf16[1024,768]{1,0:T(8,128)(2,1)S(1)}, f32[8,1024]{1,0:T(8,128)S(1)}) custom-call(s32[10]{0:T(128)S(1)} %compare_select_fusion.3.ids, bf16[1024,1024]{1,0:T(8,128)(2,1)S(1)} %copy-done.1, bf16[1024,1024]{1,0:T(8,128)(2,1)S(1)} %get-tuple-element.138.e2, ...), custom_call_target="tpu_custom_call" | custom-call | flops 4600000000 | bytes 14800000 | tf_op jit(solution)/shard_map/input_grad/pallas_call | solution.py:614
  105.3 4.0 %collective-permute-start.17 = (bf16[528,1024]{1,0:T(8,128)(2,1)S(1)}, bf16[528,1024]{1,0:T(8,128)(2,1)S(1)}, u32[]{:S(2)}, u32[]{:S(2)}) collective-permute-start(bf16[528,1024]{1,0:T(8,128)(2,1)S(1)} %get-tuple-element.140.a), channel_id=1, source_target_pairs={{0,1},{3,2},{4,5},{7,6},{8,9},{11,10},{12,13},{15,14},{16,17},{19,... | collective-permute-start | bytes 3244040 | tf_op jit(solution)/shard_map/ppermute | solution.py:795
  112.1 6.2 %mlp_weights.1 = (bf16[2,2048,256]{2,1,0:T(8,128)(2,1)S(1)}, bf16[1,2048,256]{2,1,0:T(8,128)(2,1)S(1)}, bf16[1,2048,256]{2,1,0:T(8,128)(2,1)S(1)}) custom-call(s32[10]{0:T(128)S(1)} %compare_select_fusion.3.ids, bf16[1024,1024]{1,0:T(8,128)(2,1)S(1)} %get-tuple-element.116.act, bf16[1024,1024]{1,0:T(8,128)(2,1)S(1)} %copy-done.2, ...), custom_call_target="tpu_custom_call" | custom-call | tf_op jit(solution)/shard_map/mlp_weights/pallas_call | solution.py:546
  118.9 10.0 %collective-permute-done.17.b = bf16[528,1024]{1,0:T(8,128)(2,1)S(1)} collective-permute-done((bf16[528,1024]{1,0:T(8,128)(2,1)S(1)}, bf16[528,1024]{1,0:T(8,128)(2,1)S(1)}, u32[]{:S(2)}, u32[]{:S(2)}) %collective-permute-start.17) | collective-permute-done | bytes 1081376 | tf_op jit(solution)/shard_map/ppermute | solution.py:795
  128.9 4.4 %collective-permute-start.21 = (bf16[512,1024]{1,0:T(8,128)(2,1)S(1)}, bf16[512,1024]{1,0:T(8,128)(2,1)S(1)}, u32[]{:S(2)}, u32[]{:S(2)}) collective-permute-start(bf16[512,1024]{1,0:T(8,128)(2,1)S(1)} %get-tuple-element.150.a), channel_id=1, source_target_pairs={{0,1},{3,2},{4,5},{7,6},{8,9},{11,10},{12,13},{15,14},{16,17},{19,... | collective-permute-start | bytes 3145736 | tf_op jit(solution)/shard_map/ppermute | solution.py:795
  137.1 3.8 %rest_weights.1 = (bf16[2,1024,256]{2,1,0:T(8,128)(2,1)S(1)}, bf16[1,1024,256]{2,1,0:T(8,128)(2,1)S(1)}, bf16[1,1024,256]{2,1,0:T(8,128)(2,1)S(1)}) custom-call(s32[10]{0:T(128)S(1)} %compare_select_fusion.3.ids, bf16[1024,256]{1,0:T(8,128)(2,1)S(1)} %get-tuple-element.151.ctx, bf16[1024,1024]{1,0:T(8,128)(2,1)S(1)} %copy-done.2, ...), custom_call_target="tpu_custom_call" | custom-call | tf_op jit(solution)/shard_map/rest_weights/pallas_call | solution.py:546
  140.9 8.3 %collective-permute-done.21.b = bf16[512,1024]{1,0:T(8,128)(2,1)S(1)} collective-permute-done((bf16[512,1024]{1,0:T(8,128)(2,1)S(1)}, bf16[512,1024]{1,0:T(8,128)(2,1)S(1)}, u32[]{:S(2)}, u32[]{:S(2)}) %collective-permute-start.21) | collective-permute-done | bytes 1048608 | tf_op jit(solution)/shard_map/ppermute | solution.py:795
  152.6 7.3 %collective-permute-done.19.refs_3_ = bf16[512,1024]{1,0:T(8,128)(2,1)S(1)} collective-permute-done((bf16[512,1024]{1,0:T(8,128)(2,1)S(1)}, bf16[512,1024]{1,0:T(8,128)(2,1)S(1)}, u32[]{:S(2)}, u32[]{:S(2)}) %collective-permute-start.19) | collective-permute-done | bytes 1048608 | tf_op jit(solution)/shard_map/ppermute | solution.py:806
  164.1 3.4 %collective-permute-start.35 = (bf16[2048,256]{1,0:T(8,128)(2,1)}, bf16[2048,256]{1,0:T(8,128)(2,1)}, u32[]{:S(2)}, u32[]{:S(2)}) collective-permute-start(bf16[2048,256]{1,0:T(8,128)(2,1)} %add.63.a), channel_id=1, source_target_pairs={{0,4},{4,0},{1,5},{5,1},{2,6},{6,2},{3,7},{7,3},{8,12},{12,8},{9,1... | collective-permute-start | bytes 3145736 | tf_op jit(solution)/shard_map/ppermute | solution.py:783
  167.5 2.7 %finish_in.3.refs_0_ = bf16[512,1024]{1,0:T(8,128)(2,1)} custom-call(bf16[512,1024]{1,0:T(8,128)(2,1)S(1)} %add.62.a, bf16[512,1024]{1,0:T(8,128)(2,1)S(1)} %collective-permute-done.29.b, bf16[1024,1024]{1,0:T(8,128)(2,1)S(1)} %copy-done.1, bf16[1024,1024]{1,0:T(8,128)(2,1)S(1)} %copy-done.2), custom_call_target="tpu_custom_call" | custom-call | tf_op jit(solution)/shard_map/finish_in/pallas_call | solution.py:636
  171.5 5.5 %collective-permute-done.28.b = bf16[1024,256]{1,0:T(8,128)(2,1)} collective-permute-done((bf16[1024,256]{1,0:T(8,128)(2,1)}, bf16[1024,256]{1,0:T(8,128)(2,1)}, u32[]{:S(2)}, u32[]{:S(2)}) %collective-permute-start.28) | collective-permute-done | bytes 524320 | tf_op jit(solution)/shard_map/ppermute | solution.py:783
  179.3 4.6 %collective-permute-start.34 = (bf16[1024,256]{1,0:T(8,128)(2,1)S(1)}, bf16[1024,256]{1,0:T(8,128)(2,1)S(1)}, u32[]{:S(2)}, u32[]{:S(2)}) collective-permute-start(bf16[1024,256]{1,0:T(8,128)(2,1)S(1)} %add.64.a), channel_id=1, source_target_pairs={{0,4},{4,0},{1,5},{5,1},{2,6},{6,2},{3,7},{7,3},{8,12},{12,8},{9,1... | collective-permute-start | bytes 1572872 | tf_op jit(solution)/shard_map/ppermute | solution.py:783
  183.9 6.2 %collective-permute-done.24.theirs.refs_1_ = bf16[528,1024]{1,0:T(8,128)(2,1)S(1)} collective-permute-done((bf16[528,1024]{1,0:T(8,128)(2,1)S(1)}, bf16[528,1024]{1,0:T(8,128)(2,1)S(1)}, u32[]{:S(2)}, u32[]{:S(2)}) %collective-permute-start.24) | collective-permute-done | bytes 1081376 | tf_op jit(solution)/shard_map/ppermute | solution.py:806
  192.4 2.9 %collective-permute-done.31.b = f32[8,1024]{1,0:T(8,128)S(1)} collective-permute-done((f32[8,1024]{1,0:T(8,128)S(1)}, f32[8,1024]{1,0:T(8,128)S(1)}, u32[]{:S(2)}, u32[]{:S(2)}) %collective-permute-start.31) | collective-permute-done | bytes 32800 | tf_op jit(solution)/shard_map/ppermute | solution.py:783
  198.5 3.0 %mlp_last.1 = (f32[1024,256]{1,0:T(8,128)}, f32[256,1024]{1,0:T(8,128)}) custom-call(bf16[2048,256]{1,0:T(8,128)(2,1)} %add.63.a, bf16[2048,256]{1,0:T(8,128)(2,1)} %collective-permute-done.35.b), custom_call_target="tpu_custom_call" | custom-call | tf_op jit(solution)/shard_map/mlp_last/pallas_call | solution.py:636
  204.5 8.0 %collective-permute-done.32.refs_1_ = bf16[512,1024]{1,0:T(8,128)(2,1)} collective-permute-done((bf16[512,1024]{1,0:T(8,128)(2,1)}, bf16[512,1024]{1,0:T(8,128)(2,1)}, u32[]{:S(2)}, u32[]{:S(2)}) %collective-permute-start.32) | collective-permute-done | bytes 1048608 | tf_op jit(solution)/shard_map/ppermute | solution.py:806
  212.5 2.6 %choose.5 = bf16[1024,1024]{1,0:T(8,128)(2,1)} custom-call(s32[1]{0:T(128)} %bitcast.flag, bf16[512,1024]{1,0:T(8,128)(2,1)} %finish_in.3.refs_0_, bf16[512,1024]{1,0:T(8,128)(2,1)} %collective-permute-done.32.refs_1_, bf16[1024,1024]{1,0:T(8,128)(2,1)} %choose.4.refs_2_), custom_call_target="tpu_custom_call", output_to_operand_aliasing={{}: (3, {})} | custom-call | tf_op jit(solution)/shard_map/choose/pallas_call | solution.py:636
  (146 shorter events, 48.0 us)
Async XLA Ops:
  0.6 12.3 %collective-permute-start.1 = (bf16[768,256]{1,0:T(8,128)(2,1)}, bf16[768,256]{1,0:T(8,128)(2,1)S(1)}, u32[]{:S(2)}, u32[]{:S(2)}) collective-permute-start(bf16[768,256]{1,0:T(8,128)(2,1)} %bitcast.40), channel_id=1, source_target_pairs={{0,16},{8,24},{16,0},{24,8},{1,17},{9,25},{17,1},{25,9},{2,18},{10... | collective-permute-start | bytes 1179656 | tf_op jit(solution)/shard_map/ppermute | solution.py:783
  3.6 11.1 %collective-permute-start = (bf16[768,256]{1,0:T(8,128)(2,1)}, bf16[768,256]{1,0:T(8,128)(2,1)S(1)}, u32[]{:S(2)}, u32[]{:S(2)}) collective-permute-start(bf16[768,256]{1,0:T(8,128)(2,1)} %bitcast.41), channel_id=1, source_target_pairs={{0,8},{8,0},{16,24},{24,16},{1,9},{9,1},{17,25},{25,17},{2,10},{10... | collective-permute-start | bytes 1179656 | tf_op jit(solution)/shard_map/ppermute | solution.py:783
  13.0 18.4 %collective-permute-start.3 = (bf16[1024,256]{1,0:T(8,128)(2,1)S(1)}, bf16[1024,256]{1,0:T(8,128)(2,1)S(1)}, u32[]{:S(2)}, u32[]{:S(2)}) collective-permute-start(bf16[1024,256]{1,0:T(8,128)(2,1)S(1)} %bitcast.25), channel_id=1, source_target_pairs={{0,16},{8,24},{16,0},{24,8},{1,17},{9,25},{17,1},{25,9},{2,18},{10... | collective-permute-start | bytes 1572872 | tf_op jit(solution)/shard_map/ppermute | solution.py:783
  18.7 24.0 %collective-permute-start.8 = (bf16[1280,256]{1,0:T(8,128)(2,1)S(1)}, bf16[1280,256]{1,0:T(8,128)(2,1)S(1)}, u32[]{:S(2)}, u32[]{:S(2)}) collective-permute-start(bf16[1280,256]{1,0:T(8,128)(2,1)S(1)} %constant_dynamic-update-slice_fusion.p0.d0), channel_id=1, source_target_pairs={{0,16},{8,24},{16,0},{24,8},{1,17},{9,25},{17,1},{25,9},{2,18},{10... | collective-permute-start | bytes 1966088 | tf_op jit(solution)/shard_map/ppermute | solution.py:783
  20.3 15.8 %collective-permute-start.5 = (bf16[1024,256]{1,0:T(8,128)(2,1)S(1)}, bf16[1024,256]{1,0:T(8,128)(2,1)S(1)}, u32[]{:S(2)}, u32[]{:S(2)}) collective-permute-start(bf16[1024,256]{1,0:T(8,128)(2,1)S(1)} %bitcast.26), channel_id=1, source_target_pairs={{0,8},{8,0},{16,24},{24,16},{1,9},{9,1},{17,25},{25,17},{2,10},{10... | collective-permute-start | bytes 1572872 | tf_op jit(solution)/shard_map/ppermute | solution.py:783
  20.4 14.4 %collective-permute-start.4 = (bf16[1024,256]{1,0:T(8,128)(2,1)S(1)}, bf16[1024,256]{1,0:T(8,128)(2,1)S(1)}, u32[]{:S(2)}, u32[]{:S(2)}) collective-permute-start(bf16[1024,256]{1,0:T(8,128)(2,1)S(1)} %get-tuple-element.106.kv.refs_0_), channel_id=1, source_target_pairs={{0,4},{4,0},{1,5},{5,1},{2,6},{6,2},{3,7},{7,3},{8,12},{12,8},{9,1... | collective-permute-start | bytes 1572872 | tf_op jit(solution)/shard_map/ppermute | solution.py:783
  31.4 4.7 %collective-permute-start.6 = (bf16[1024,256]{1,0:T(8,128)(2,1)S(1)}, bf16[1024,256]{1,0:T(8,128)(2,1)S(1)}, u32[]{:S(2)}, u32[]{:S(2)}) collective-permute-start(bf16[1024,256]{1,0:T(8,128)(2,1)S(1)} %collective-permute-done.3.p2.u2), channel_id=1, source_target_pairs={{0,8},{8,0},{16,24},{24,16},{1,9},{9,1},{17,25},{25,17},{2,10},{10... | collective-permute-start | bytes 1572872 | tf_op jit(solution)/shard_map/ppermute | solution.py:783
  31.7 14.2 %collective-permute-start.10 = (bf16[1024,256]{1,0:T(8,128)(2,1)S(1)}, bf16[1024,256]{1,0:T(8,128)(2,1)S(1)}, u32[]{:S(2)}, u32[]{:S(2)}) collective-permute-start(bf16[1024,256]{1,0:T(8,128)(2,1)S(1)} %get-tuple-element.104.kv.refs_0_), channel_id=1, source_target_pairs={{0,4},{4,0},{1,5},{5,1},{2,6},{6,2},{3,7},{7,3},{8,12},{12,8},{9,1... | collective-permute-start | bytes 1572872 | tf_op jit(solution)/shard_map/ppermute | solution.py:783
  34.7 12.6 %collective-permute-start.7 = (bf16[1280,256]{1,0:T(8,128)(2,1)S(1)}, bf16[1280,256]{1,0:T(8,128)(2,1)S(1)}, u32[]{:S(2)}, u32[]{:S(2)}) collective-permute-start(bf16[1280,256]{1,0:T(8,128)(2,1)S(1)} %constant_dynamic-update-slice_fusion.p0.d0), channel_id=1, source_target_pairs={{0,8},{8,0},{16,24},{24,16},{1,9},{9,1},{17,25},{25,17},{2,10},{10... | collective-permute-start | bytes 1966088 | tf_op jit(solution)/shard_map/ppermute | solution.py:783
  52.7 37.4 %collective-permute-start.11 = (bf16[512,1024]{1,0:T(8,128)(2,1)S(1)}, bf16[512,1024]{1,0:T(8,128)(2,1)S(1)}, u32[]{:S(2)}, u32[]{:S(2)}) collective-permute-start(bf16[512,1024]{1,0:T(8,128)(2,1)S(1)} %get-tuple-element.122.a), channel_id=1, source_target_pairs={{0,1},{3,2},{4,5},{7,6},{8,9},{11,10},{12,13},{15,14},{16,17},{19,... | collective-permute-start | bytes 3145736 | tf_op jit(solution)/shard_map/ppermute | solution.py:795
  63.2 26.9 %collective-permute-start.12 = (bf16[1024,256]{1,0:T(8,128)(2,1)S(1)}, bf16[1024,256]{1,0:T(8,128)(2,1)S(1)}, u32[]{:S(2)}, u32[]{:S(2)}) collective-permute-start(bf16[1024,256]{1,0:T(8,128)(2,1)S(1)} %get-tuple-element.127), channel_id=1, source_target_pairs={{0,4},{4,0},{1,5},{5,1},{2,6},{6,2},{3,7},{7,3},{8,12},{12,8},{9,1... | collective-permute-start | bytes 1572872 | tf_op jit(solution)/shard_map/ppermute | solution.py:783
  76.9 32.4 %collective-permute-start.14 = (bf16[512,1024]{1,0:T(8,128)(2,1)S(1)}, bf16[512,1024]{1,0:T(8,128)(2,1)S(1)}, u32[]{:S(2)}, u32[]{:S(2)}) collective-permute-start(bf16[512,1024]{1,0:T(8,128)(2,1)S(1)} %get-tuple-element.135.a), channel_id=1, source_target_pairs={{0,1},{3,2},{4,5},{7,6},{8,9},{11,10},{12,13},{15,14},{16,17},{19,... | collective-permute-start | bytes 3145736 | tf_op jit(solution)/shard_map/ppermute | solution.py:795
  85.4 13.8 %collective-permute-start.15 = (bf16[1024,256]{1,0:T(8,128)(2,1)S(1)}, bf16[1024,256]{1,0:T(8,128)(2,1)S(1)}, u32[]{:S(2)}, u32[]{:S(2)}) collective-permute-start(bf16[1024,256]{1,0:T(8,128)(2,1)S(1)} %get-tuple-element.132), channel_id=1, source_target_pairs={{0,4},{4,0},{1,5},{5,1},{2,6},{6,2},{3,7},{7,3},{8,12},{12,8},{9,1... | collective-permute-start | bytes 1572872 | tf_op jit(solution)/shard_map/ppermute | solution.py:783
  90.4 20.0 %collective-permute-start.13 = (bf16[512,1024]{1,0:T(8,128)(2,1)S(1)}, bf16[512,1024]{1,0:T(8,128)(2,1)S(1)}, u32[]{:S(2)}, u32[]{:S(2)}) collective-permute-start(bf16[512,1024]{1,0:T(8,128)(2,1)S(1)} %add.60.a), channel_id=1, source_target_pairs={{1,2},{2,1},{5,6},{6,5},{9,10},{10,9},{13,14},{14,13},{17,18},{18,... | collective-permute-start | bytes 3145736 | tf_op jit(solution)/shard_map/ppermute | solution.py:801
  105.3 23.6 %collective-permute-start.17 = (bf16[528,1024]{1,0:T(8,128)(2,1)S(1)}, bf16[528,1024]{1,0:T(8,128)(2,1)S(1)}, u32[]{:S(2)}, u32[]{:S(2)}) collective-permute-start(bf16[528,1024]{1,0:T(8,128)(2,1)S(1)} %get-tuple-element.140.a), channel_id=1, source_target_pairs={{0,1},{3,2},{4,5},{7,6},{8,9},{11,10},{12,13},{15,14},{16,17},{19,... | collective-permute-start | bytes 3244040 | tf_op jit(solution)/shard_map/ppermute | solution.py:795
  109.6 24.0 %collective-permute-start.16 = (bf16[512,1024]{1,0:T(8,128)(2,1)S(1)}, bf16[512,1024]{1,0:T(8,128)(2,1)S(1)}, u32[]{:S(2)}, u32[]{:S(2)}) collective-permute-start(bf16[512,1024]{1,0:T(8,128)(2,1)S(1)} %add.61.a), channel_id=1, source_target_pairs={{1,2},{2,1},{5,6},{6,5},{9,10},{10,9},{13,14},{14,13},{17,18},{18,... | collective-permute-start | bytes 3145736 | tf_op jit(solution)/shard_map/ppermute | solution.py:801
  110.8 24.0 %collective-permute-start.18 = (bf16[512,1024]{1,0:T(8,128)(2,1)S(1)}, bf16[512,1024]{1,0:T(8,128)(2,1)S(1)}, u32[]{:S(2)}, u32[]{:S(2)}) collective-permute-start(bf16[512,1024]{1,0:T(8,128)(2,1)S(1)} %finish_out.2.refs_0_), channel_id=1, source_target_pairs={{1,0},{2,3},{5,4},{6,7},{9,8},{10,11},{13,12},{14,15},{17,16},{18,... | collective-permute-start | bytes 3145736 | tf_op jit(solution)/shard_map/ppermute | solution.py:806
  118.3 18.0 %collective-permute-start.22 = (bf16[1,2048,256]{2,1,0:T(8,128)(2,1)S(1)}, bf16[1,2048,256]{2,1,0:T(8,128)(2,1)S(1)}, u32[]{:S(2)}, u32[]{:S(2)}) collective-permute-start(bf16[1,2048,256]{2,1,0:T(8,128)(2,1)S(1)} %get-tuple-element.153), channel_id=1, source_target_pairs={{0,8},{8,0},{16,24},{24,16},{1,9},{9,1},{17,25},{25,17},{2,10},{10... | collective-permute-start | bytes 3145736 | tf_op jit(solution)/shard_map/ppermute | solution.py:783
  118.4 18.0 %collective-permute-start.23 = (bf16[1,2048,256]{2,1,0:T(8,128)(2,1)S(1)}, bf16[1,2048,256]{2,1,0:T(8,128)(2,1)S(1)}, u32[]{:S(2)}, u32[]{:S(2)}) collective-permute-start(bf16[1,2048,256]{2,1,0:T(8,128)(2,1)S(1)} %get-tuple-element.154), channel_id=1, source_target_pairs={{0,8},{8,0},{16,24},{24,16},{1,9},{9,1},{17,25},{25,17},{2,10},{10... | collective-permute-start | bytes 3145736 | tf_op jit(solution)/shard_map/ppermute | solution.py:783
  128.9 20.3 %collective-permute-start.21 = (bf16[512,1024]{1,0:T(8,128)(2,1)S(1)}, bf16[512,1024]{1,0:T(8,128)(2,1)S(1)}, u32[]{:S(2)}, u32[]{:S(2)}) collective-permute-start(bf16[512,1024]{1,0:T(8,128)(2,1)S(1)} %get-tuple-element.150.a), channel_id=1, source_target_pairs={{0,1},{3,2},{4,5},{7,6},{8,9},{11,10},{12,13},{15,14},{16,17},{19,... | collective-permute-start | bytes 3145736 | tf_op jit(solution)/shard_map/ppermute | solution.py:795
  133.6 16.7 %collective-permute-start.20 = (bf16[528,1024]{1,0:T(8,128)(2,1)S(1)}, bf16[528,1024]{1,0:T(8,128)(2,1)S(1)}, u32[]{:S(2)}, u32[]{:S(2)}) collective-permute-start(bf16[528,1024]{1,0:T(8,128)(2,1)S(1)} %add_extra.1.a), channel_id=1, source_target_pairs={{1,2},{2,1},{5,6},{6,5},{9,10},{10,9},{13,14},{14,13},{17,18},{18,... | collective-permute-start | bytes 3244040 | tf_op jit(solution)/shard_map/ppermute | solution.py:801
  134.8 25.0 %collective-permute-start.19 = (bf16[512,1024]{1,0:T(8,128)(2,1)S(1)}, bf16[512,1024]{1,0:T(8,128)(2,1)S(1)}, u32[]{:S(2)}, u32[]{:S(2)}) collective-permute-start(bf16[512,1024]{1,0:T(8,128)(2,1)S(1)} %finish_out.3.refs_1_), channel_id=1, source_target_pairs={{1,0},{2,3},{5,4},{6,7},{9,8},{10,11},{13,12},{14,15},{17,16},{18,... | collective-permute-start | bytes 3145736 | tf_op jit(solution)/shard_map/ppermute | solution.py:806
  137.1 24.1 %collective-permute-start.27 = (bf16[2048,256]{1,0:T(8,128)(2,1)S(1)}, bf16[2048,256]{1,0:T(8,128)(2,1)S(1)}, u32[]{:S(2)}, u32[]{:S(2)}) collective-permute-start(bf16[2048,256]{1,0:T(8,128)(2,1)S(1)} %get-tuple-element.165), channel_id=1, source_target_pairs={{0,16},{8,24},{16,0},{24,8},{1,17},{9,25},{17,1},{25,9},{2,18},{10... | collective-permute-start | bytes 3145736 | tf_op jit(solution)/shard_map/ppermute | solution.py:783
  149.5 18.0 %collective-permute-start.29 = (bf16[512,1024]{1,0:T(8,128)(2,1)S(1)}, bf16[512,1024]{1,0:T(8,128)(2,1)S(1)}, u32[]{:S(2)}, u32[]{:S(2)}) collective-permute-start(bf16[512,1024]{1,0:T(8,128)(2,1)S(1)} %add.62.a), channel_id=1, source_target_pairs={{1,2},{2,1},{5,6},{6,5},{9,10},{10,9},{13,14},{14,13},{17,18},{18,... | collective-permute-start | bytes 3145736 | tf_op jit(solution)/shard_map/ppermute | solution.py:801
  150.2 12.1 %collective-permute-start.25 = (bf16[1,1024,256]{2,1,0:T(8,128)(2,1)S(1)}, bf16[1,1024,256]{2,1,0:T(8,128)(2,1)S(1)}, u32[]{:S(2)}, u32[]{:S(2)}) collective-permute-start(bf16[1,1024,256]{2,1,0:T(8,128)(2,1)S(1)} %get-tuple-element.163), channel_id=1, source_target_pairs={{0,8},{8,0},{16,24},{24,16},{1,9},{9,1},{17,25},{25,17},{2,10},{10... | collective-permute-start | bytes 1572872 | tf_op jit(solution)/shard_map/ppermute | solution.py:783
  150.3 12.0 %collective-permute-start.26 = (bf16[1,1024,256]{2,1,0:T(8,128)(2,1)S(1)}, bf16[1,1024,256]{2,1,0:T(8,128)(2,1)S(1)}, u32[]{:S(2)}, u32[]{:S(2)}) collective-permute-start(bf16[1,1024,256]{2,1,0:T(8,128)(2,1)S(1)} %get-tuple-element.164), channel_id=1, source_target_pairs={{0,8},{8,0},{16,24},{24,16},{1,9},{9,1},{17,25},{25,17},{2,10},{10... | collective-permute-start | bytes 1572872 | tf_op jit(solution)/shard_map/ppermute | solution.py:783
  159.9 30.2 %collective-permute-start.24 = (bf16[528,1024]{1,0:T(8,128)(2,1)S(1)}, bf16[528,1024]{1,0:T(8,128)(2,1)S(1)}, u32[]{:S(2)}, u32[]{:S(2)}) collective-permute-start(bf16[528,1024]{1,0:T(8,128)(2,1)S(1)} %finish_in.2.ours.refs_0_), channel_id=1, source_target_pairs={{1,0},{2,3},{5,4},{6,7},{9,8},{10,11},{13,12},{14,15},{17,16},{18,... | collective-permute-start | bytes 3244040 | tf_op jit(solution)/shard_map/ppermute | solution.py:806
  163.3 13.7 %collective-permute-start.28 = (bf16[1024,256]{1,0:T(8,128)(2,1)}, bf16[1024,256]{1,0:T(8,128)(2,1)}, u32[]{:S(2)}, u32[]{:S(2)}) collective-permute-start(bf16[1024,256]{1,0:T(8,128)(2,1)} %get-tuple-element.170), channel_id=1, source_target_pairs={{0,16},{8,24},{16,0},{24,8},{1,17},{9,25},{17,1},{25,9},{2,18},{10... | collective-permute-start | bytes 1572872 | tf_op jit(solution)/shard_map/ppermute | solution.py:783
  164.1 34.4 %collective-permute-start.35 = (bf16[2048,256]{1,0:T(8,128)(2,1)}, bf16[2048,256]{1,0:T(8,128)(2,1)}, u32[]{:S(2)}, u32[]{:S(2)}) collective-permute-start(bf16[2048,256]{1,0:T(8,128)(2,1)} %add.63.a), channel_id=1, source_target_pairs={{0,4},{4,0},{1,5},{5,1},{2,6},{6,2},{3,7},{7,3},{8,12},{12,8},{9,1... | collective-permute-start | bytes 3145736 | tf_op jit(solution)/shard_map/ppermute | solution.py:783
  170.2 42.3 %collective-permute-start.32 = (bf16[512,1024]{1,0:T(8,128)(2,1)}, bf16[512,1024]{1,0:T(8,128)(2,1)}, u32[]{:S(2)}, u32[]{:S(2)}) collective-permute-start(bf16[512,1024]{1,0:T(8,128)(2,1)} %finish_in.3.refs_0_), channel_id=1, source_target_pairs={{1,0},{2,3},{5,4},{6,7},{9,8},{10,11},{13,12},{14,15},{17,16},{18,... | collective-permute-start | bytes 3145736 | tf_op jit(solution)/shard_map/ppermute | solution.py:806
  179.3 23.5 %collective-permute-start.34 = (bf16[1024,256]{1,0:T(8,128)(2,1)S(1)}, bf16[1024,256]{1,0:T(8,128)(2,1)S(1)}, u32[]{:S(2)}, u32[]{:S(2)}) collective-permute-start(bf16[1024,256]{1,0:T(8,128)(2,1)S(1)} %add.64.a), channel_id=1, source_target_pairs={{0,4},{4,0},{1,5},{5,1},{2,6},{6,2},{3,7},{7,3},{8,12},{12,8},{9,1... | collective-permute-start | bytes 1572872 | tf_op jit(solution)/shard_map/ppermute | solution.py:783
  195.3 8.5 %collective-permute-start.33 = (f32[8,1024]{1,0:T(8,128)S(1)}, f32[8,1024]{1,0:T(8,128)S(1)}, u32[]{:S(2)}, u32[]{:S(2)}) collective-permute-start(f32[8,1024]{1,0:T(8,128)S(1)} %add.66.a), channel_id=1, source_target_pairs={{0,4},{4,0},{1,5},{5,1},{2,6},{6,2},{3,7},{7,3},{8,12},{12,8},{9,1... | collective-permute-start | bytes 98312 | tf_op jit(solution)/shard_map/ppermute | solution.py:783
  (31 other events, 250.9 us)

commit v3 on v2

--- a/solution.py
+++ b/solution.py
@@ -101,7 +101,7 @@
                 kv[:, (part - 1) * PAIR : part * PAIR] = half.astype(bf16)
 
 
-def project(ids, n1, weights, bias, tables, tile=256):
+def project(ids, n1, weights, bias, tables, tile=512):
     rows, wide = n1.shape
     row = lambda w: pl.BlockSpec((tile, w), lambda i: (i, 0))
     s = jax.ShapeDtypeStruct
@@ -393,7 +393,7 @@
     slope[...] = (cdf + hidden * pdf).astype(bf16)
 
 
-def mlp_up(ids, x, gain, shift, up_bias, pieces, tile=256):
+def mlp_up(ids, x, gain, shift, up_bias, pieces, tile=512):
     rows, width = x.shape
     units = up_bias.shape[1]
     row = lambda w: pl.BlockSpec((tile, w), lambda i: (i, 0))
@@ -441,7 +441,7 @@
     store_part((first, second), (rows // 2, rows // 2), value.astype(bf16))
 
 
-def mlp_down(ids, act, cot, pieces, o0, o1, tile=256):
+def mlp_down(ids, act, cot, pieces, o0, o1, tile=512):
     rows, width = cot.shape
     units = act.shape[1]
     row = lambda w: pl.BlockSpec((tile, w), lambda i: (i, 0))

time: 216 us -> 214 us (level)
  the two profiles are of different devices: /device:TPU:0 before, /device:TPU:4 now
where the time goes in v3:
time: 214 us; the launch traced here: 212 us
  Pallas kernels  90.7 us (42%)
  waiting for transfers between devices  74.1 us (35%)
  starting transfers between devices  36.4 us (17%)
  local copies, waits for them, and re-layouts  7.27 us (3%)
    ppermute x4, waiting for transfers between devices, end(): self.third[i] = lax.ppermute(self.finals[i], 'tensor', [(1, 0), (2, 3)])  27.1 us
    ppermute x4, waiting for transfers between devices, __init__(): lax.ppermute(part, 'tensor', [(0, 1), (3, 2)])  25.1 us
    ppermute x24, waiting for transfers between devices, swap(): return jax.tree.map(lambda v: lax.ppermute(v, axis, pairs), values)  21.9 us
    pallas_call x22, Pallas kernels, call(): pl.pallas_call(kernel, grid=(grid,), in_specs=in_specs or [whole(a.shape)...  21 us
    pallas_call x2, Pallas kernels, attend_backward(): pl.pallas_call(partial(attend_backward_kernel, slots, split), grid=(), in...  17 us
    ppermute x24, starting transfers between devices, swap(): return jax.tree.map(lambda v: lax.ppermute(v, axis, pairs), values)  15.2 us
    pallas_call x4, Pallas kernels, attend_forward(): pl.pallas_call(partial(attend_forward_kernel, slots, low, count, carried...  14.9 us
    ppermute x4, starting transfers between devices, __init__(): lax.ppermute(part, 'tensor', [(0, 1), (3, 2)])  12.9 us
  transfers between devices with their start and end apart: 36, of which 16 were waited for; matrix products, arithmetic and copies ran while one was open for 2% of the time, Pallas kernels for 39%

profile of v3, /device:TPU:4, one launch (start us, length us, event | category | flops | bytes accessed | tf_op | source)
XLA Modules:
  0.0 212.1 jit_solution(2575957733332382442)
XLA Ops:
  13.5 3.1 %project.1 = (bf16[1024,128]{1,0:T(8,128)(2,1)S(1)}, bf16[1024,128]{1,0:T(8,128)(2,1)S(1)}, bf16[1024,256]{1,0:T(8,128)(2,1)S(1)}, bf16[1024,256]{1,0:T(8,128)(2,1)S(1)}) custom-call(s32[10]{0:T(128)S(1)} %compare_select_fusion.3.ids, bf16[1024,1024]{1,0:T(8,128)(2,1)S(1)} %norm.1.n1, bf16[768,256]{1,0:T(8,128)(2,1)S(1)} %bitcast.42, ...), custom_call_target="tpu_custom_call" | custom-call | flops 4944999936 | bytes 15910000 | tf_op jit(solution)/shard_map/project/pallas_call | solution.py:108
  18.9 4.8 %attend_forward.4 = (f32[16,512]{1,0:T(8,128)S(1)}, f32[256,512]{1,0:T(8,128)S(1)}) custom-call(s32[10]{0:T(128)S(1)} %compare_select_fusion.3.ids, s32[2,3]{1,0:T(2,128)S(1)} %copy-done.11, bf16[1024,128]{1,0:T(8,128)(2,1)S(1)} %get-tuple-element.113.q, bf16[1024,256]{1,0:T(8,128)(2,1)S(1)} %get-tuple-element.106.kv.refs_0_), custom_call_target="tpu_custom_call" | custom-call | tf_op jit(solution)/shard_map/attend_forward/pallas_call | solution.py:232
  23.6 4.8 %attend_forward.5 = (f32[16,512]{1,0:T(8,128)S(1)}, f32[256,512]{1,0:T(8,128)S(1)}) custom-call(s32[10]{0:T(128)S(1)} %compare_select_fusion.3.ids, s32[2,3]{1,0:T(2,128)S(1)} %copy-done.11, bf16[1024,128]{1,0:T(8,128)(2,1)S(1)} %get-tuple-element.120.q, bf16[1024,256]{1,0:T(8,128)(2,1)S(1)} %get-tuple-element.104.kv.refs_0_), custom_call_target="tpu_custom_call" | custom-call | tf_op jit(solution)/shard_map/attend_forward/pallas_call | solution.py:232
  30.2 2.8 %collective-permute-done.4.kv.refs_1_ = bf16[1024,256]{1,0:T(8,128)(2,1)S(1)} collective-permute-done((bf16[1024,256]{1,0:T(8,128)(2,1)S(1)}, bf16[1024,256]{1,0:T(8,128)(2,1)S(1)}, u32[]{:S(2)}, u32[]{:S(2)}) %collective-permute-start.4) | collective-permute-done | bytes 524320 | tf_op jit(solution)/shard_map/ppermute | solution.py:783
  33.1 2.7 %attend_forward.6 = (f32[1024,128]{1,0:T(8,128)S(1)}, f32[8,512]{1,0:T(8,128)S(1)}) custom-call(s32[10]{0:T(128)S(1)} %compare_select_fusion.3.ids, s32[2,3]{1,0:T(2,128)S(1)} %copy-done.11, bf16[1024,128]{1,0:T(8,128)(2,1)S(1)} %get-tuple-element.113.q, bf16[1024,256]{1,0:T(8,128)(2,1)S(1)} %collective-permute-done.4.kv.refs_1_, ...), custom_call_target="tpu_custom_call" | custom-call | tf_op jit(solution)/shard_map/attend_forward/pallas_call | solution.py:232
  35.9 5.8 %mlp_up.1 = (bf16[1024,1024]{1,0:T(8,128)(2,1)S(1)}, bf16[1024,1024]{1,0:T(8,128)(2,1)S(1)}, bf16[1024,1024]{1,0:T(8,128)(2,1)S(1)}) custom-call(s32[10]{0:T(128)S(1)} %compare_select_fusion.3.ids, bf16[1024,1024]{1,0:T(8,128)(2,1)S(1)} %copy-done.1, f32[1,1024]{1,0:T(1,128)S(1)} %bitcast.29, f32[1,1024]{1,0:T(1,128)S(1)} %bitcast.35, ...), custom_call_target="tpu_custom_call" | custom-call | tf_op jit(solution)/shard_map/mlp_up/pallas_call | solution.py:401
  41.7 1.9 collective-permute-start.9
  43.9 2.7 %attend_forward.7 = (f32[1024,128]{1,0:T(8,128)S(1)}, f32[8,512]{1,0:T(8,128)S(1)}) custom-call(s32[10]{0:T(128)S(1)} %compare_select_fusion.3.ids, s32[2,3]{1,0:T(2,128)S(1)} %copy-done.11, bf16[1024,128]{1,0:T(8,128)(2,1)S(1)} %get-tuple-element.120.q, bf16[1024,256]{1,0:T(8,128)(2,1)S(1)} %collective-permute-done.10.kv.refs_1_, ...), custom_call_target="tpu_custom_call" | custom-call | flops 11500000256 | bytes 37000000 | tf_op jit(solution)/shard_map/attend_forward/pallas_call | solution.py:232
  46.7 4.8 %mlp_down.1 = (bf16[512,1024]{1,0:T(8,128)(2,1)S(1)}, bf16[512,1024]{1,0:T(8,128)(2,1)S(1)}, bf16[1024,256]{1,0:T(8,128)(2,1)S(1)}, bf16[1024,128]{1,0:T(8,128)(2,1)S(1)}, bf16[1024,128]{1,0:T(8,128)(2,1)S(1)}) custom-call(s32[10]{0:T(128)S(1)} %compare_select_fusion.3.ids, bf16[1024,1024]{1,0:T(8,128)(2,1)S(1)} %get-tuple-element.116.act, ...), custom_call_target="tpu_custom_call" | custom-call | flops 1150000000 | bytes 3700000 | tf_op jit(solution)/shard_map/mlp_down/pallas_call | solution.py:449
  51.5 3.7 %collective-permute-start.11 = (bf16[512,1024]{1,0:T(8,128)(2,1)S(1)}, bf16[512,1024]{1,0:T(8,128)(2,1)S(1)}, u32[]{:S(2)}, u32[]{:S(2)}) collective-permute-start(bf16[512,1024]{1,0:T(8,128)(2,1)S(1)} %get-tuple-element.122.a), channel_id=1, source_target_pairs={{0,1},{3,2},{4,5},{7,6},{8,9},{11,10},{12,13},{15,14},{16,17},{19,... | collective-permute-start | bytes 3145736 | tf_op jit(solution)/shard_map/ppermute | solution.py:795
  55.3 8.5 %attend_backward.2 = (bf16[1024,256]{1,0:T(8,128)(2,1)S(1)}, bf16[1024,256]{1,0:T(8,128)(2,1)S(1)}, bf16[1024,128]{1,0:T(8,128)(2,1)S(1)}) custom-call(s32[10]{0:T(128)S(1)} %compare_select_fusion.3.ids, s32[2,3]{1,0:T(2,128)S(1)} %copy-done.11, bf16[1024,128]{1,0:T(8,128)(2,1)S(1)} %get-tuple-element.113.q, bf16[1024,128]{1,0:T(8,128)(2,1)S(1)} %get-tuple-element.124.g, ...), custom_call_target="tpu_custom_call" | custom-call | tf_op jit(solution)/shard_map/attend_backward/pallas_call | solution.py:345
  63.7 3.4 %collective-permute-start.12 = (bf16[1024,256]{1,0:T(8,128)(2,1)S(1)}, bf16[1024,256]{1,0:T(8,128)(2,1)S(1)}, u32[]{:S(2)}, u32[]{:S(2)}) collective-permute-start(bf16[1024,256]{1,0:T(8,128)(2,1)S(1)} %get-tuple-element.127), channel_id=1, source_target_pairs={{0,4},{4,0},{1,5},{5,1},{2,6},{6,2},{3,7},{7,3},{8,12},{12,8},{9,1... | collective-permute-start | bytes 1572872 | tf_op jit(solution)/shard_map/ppermute | solution.py:783
  68.5 8.5 %attend_backward.3 = (bf16[1024,256]{1,0:T(8,128)(2,1)S(1)}, bf16[1024,256]{1,0:T(8,128)(2,1)S(1)}, bf16[1024,128]{1,0:T(8,128)(2,1)S(1)}) custom-call(s32[10]{0:T(128)S(1)} %compare_select_fusion.3.ids, s32[2,3]{1,0:T(2,128)S(1)} %copy-done.11, bf16[1024,128]{1,0:T(8,128)(2,1)S(1)} %get-tuple-element.120.q, bf16[1024,128]{1,0:T(8,128)(2,1)S(1)} %get-tuple-element.129.g, ...), custom_call_target="tpu_custom_call" | custom-call | tf_op jit(solution)/shard_map/attend_backward/pallas_call | solution.py:345
  81.0 8.0 %mlp_backward.1 = (bf16[1024,1024]{1,0:T(8,128)(2,1)S(1)}, bf16[1024,1024]{1,0:T(8,128)(2,1)S(1)}, f32[8,1024]{1,0:T(8,128)S(1)}) custom-call(s32[10]{0:T(128)S(1)} %compare_select_fusion.3.ids, bf16[1024,1024]{1,0:T(8,128)(2,1)S(1)} %copy-done.1, bf16[1024,1024]{1,0:T(8,128)(2,1)S(1)} %copy-done.2, f32[1,1024]{1,0:T(1,128)S(1)} %bitcast.30, ...), custom_call_target="tpu_custom_call" | custom-call | flops 1150000000 | bytes 3700000 | tf_op jit(solution)/shard_map/mlp_backward/pallas_call | solution.py:493
  88.9 2.4 %collective-permute-done.15.refs_7_ = bf16[1024,256]{1,0:T(8,128)(2,1)S(1)} collective-permute-done((bf16[1024,256]{1,0:T(8,128)(2,1)S(1)}, bf16[1024,256]{1,0:T(8,128)(2,1)S(1)}, u32[]{:S(2)}, u32[]{:S(2)}) %collective-permute-start.15) | collective-permute-done | bytes 524320 | tf_op jit(solution)/shard_map/ppermute | solution.py:783
  91.4 6.1 %input_grad.1 = (bf16[528,1024]{1,0:T(8,128)(2,1)S(1)}, bf16[512,1024]{1,0:T(8,128)(2,1)S(1)}, bf16[1024,768]{1,0:T(8,128)(2,1)S(1)}, f32[8,1024]{1,0:T(8,128)S(1)}) custom-call(s32[10]{0:T(128)S(1)} %compare_select_fusion.3.ids, bf16[1024,1024]{1,0:T(8,128)(2,1)S(1)} %copy-done.1, bf16[1024,1024]{1,0:T(8,128)(2,1)S(1)} %get-tuple-element.138.e2, ...), custom_call_target="tpu_custom_call" | custom-call | flops 4600000000 | bytes 14800000 | tf_op jit(solution)/shard_map/input_grad/pallas_call | solution.py:614
  97.5 3.4 %collective-permute-start.17 = (bf16[528,1024]{1,0:T(8,128)(2,1)S(1)}, bf16[528,1024]{1,0:T(8,128)(2,1)S(1)}, u32[]{:S(2)}, u32[]{:S(2)}) collective-permute-start(bf16[528,1024]{1,0:T(8,128)(2,1)S(1)} %get-tuple-element.140.a), channel_id=1, source_target_pairs={{0,1},{3,2},{4,5},{7,6},{8,9},{11,10},{12,13},{15,14},{16,17},{19,... | collective-permute-start | bytes 3244040 | tf_op jit(solution)/shard_map/ppermute | solution.py:795
  104.0 6.2 %mlp_weights.1 = (bf16[2,2048,256]{2,1,0:T(8,128)(2,1)S(1)}, bf16[1,2048,256]{2,1,0:T(8,128)(2,1)S(1)}, bf16[1,2048,256]{2,1,0:T(8,128)(2,1)S(1)}) custom-call(s32[10]{0:T(128)S(1)} %compare_select_fusion.3.ids, bf16[1024,1024]{1,0:T(8,128)(2,1)S(1)} %get-tuple-element.116.act, bf16[1024,1024]{1,0:T(8,128)(2,1)S(1)} %copy-done.2, ...), custom_call_target="tpu_custom_call" | custom-call | tf_op jit(solution)/shard_map/mlp_weights/pallas_call | solution.py:546
  110.7 13.4 %collective-permute-done.17.b = bf16[528,1024]{1,0:T(8,128)(2,1)S(1)} collective-permute-done((bf16[528,1024]{1,0:T(8,128)(2,1)S(1)}, bf16[528,1024]{1,0:T(8,128)(2,1)S(1)}, u32[]{:S(2)}, u32[]{:S(2)}) %collective-permute-start.17) | collective-permute-done | bytes 1081376 | tf_op jit(solution)/shard_map/ppermute | solution.py:795
  124.2 4.4 %collective-permute-start.21 = (bf16[512,1024]{1,0:T(8,128)(2,1)S(1)}, bf16[512,1024]{1,0:T(8,128)(2,1)S(1)}, u32[]{:S(2)}, u32[]{:S(2)}) collective-permute-start(bf16[512,1024]{1,0:T(8,128)(2,1)S(1)} %get-tuple-element.150.a), channel_id=1, source_target_pairs={{0,1},{3,2},{4,5},{7,6},{8,9},{11,10},{12,13},{15,14},{16,17},{19,... | collective-permute-start | bytes 3145736 | tf_op jit(solution)/shard_map/ppermute | solution.py:795
  130.1 2.8 %collective-permute-done.18.refs_2_ = bf16[512,1024]{1,0:T(8,128)(2,1)S(1)} collective-permute-done((bf16[512,1024]{1,0:T(8,128)(2,1)S(1)}, bf16[512,1024]{1,0:T(8,128)(2,1)S(1)}, u32[]{:S(2)}, u32[]{:S(2)}) %collective-permute-start.18) | collective-permute-done | bytes 1048608 | tf_op jit(solution)/shard_map/ppermute | solution.py:806
  134.9 3.8 %rest_weights.1 = (bf16[2,1024,256]{2,1,0:T(8,128)(2,1)S(1)}, bf16[1,1024,256]{2,1,0:T(8,128)(2,1)S(1)}, bf16[1,1024,256]{2,1,0:T(8,128)(2,1)S(1)}) custom-call(s32[10]{0:T(128)S(1)} %compare_select_fusion.3.ids, bf16[1024,256]{1,0:T(8,128)(2,1)S(1)} %get-tuple-element.151.ctx, bf16[1024,1024]{1,0:T(8,128)(2,1)S(1)} %copy-done.2, ...), custom_call_target="tpu_custom_call" | custom-call | tf_op jit(solution)/shard_map/rest_weights/pallas_call | solution.py:546
  138.7 11.6 %collective-permute-done.21.b = bf16[512,1024]{1,0:T(8,128)(2,1)S(1)} collective-permute-done((bf16[512,1024]{1,0:T(8,128)(2,1)S(1)}, bf16[512,1024]{1,0:T(8,128)(2,1)S(1)}, u32[]{:S(2)}, u32[]{:S(2)}) %collective-permute-start.21) | collective-permute-done | bytes 1048608 | tf_op jit(solution)/shard_map/ppermute | solution.py:795
  151.9 1.8 finish_in.2.ours.refs_0_
  153.6 5.0 %collective-permute-done.19.refs_3_ = bf16[512,1024]{1,0:T(8,128)(2,1)S(1)} collective-permute-done((bf16[512,1024]{1,0:T(8,128)(2,1)S(1)}, bf16[512,1024]{1,0:T(8,128)(2,1)S(1)}, u32[]{:S(2)}, u32[]{:S(2)}) %collective-permute-start.19) | collective-permute-done | bytes 1048608 | tf_op jit(solution)/shard_map/ppermute | solution.py:806
  162.1 2.7 %finish_in.3.refs_0_ = bf16[512,1024]{1,0:T(8,128)(2,1)} custom-call(bf16[512,1024]{1,0:T(8,128)(2,1)S(1)} %add.62.a, bf16[512,1024]{1,0:T(8,128)(2,1)S(1)} %collective-permute-done.29.b, bf16[1024,1024]{1,0:T(8,128)(2,1)S(1)} %copy-done.1, bf16[1024,1024]{1,0:T(8,128)(2,1)S(1)} %copy-done.2), custom_call_target="tpu_custom_call" | custom-call | tf_op jit(solution)/shard_map/finish_in/pallas_call | solution.py:636
  166.2 8.0 %collective-permute-done.28.b = bf16[1024,256]{1,0:T(8,128)(2,1)} collective-permute-done((bf16[1024,256]{1,0:T(8,128)(2,1)}, bf16[1024,256]{1,0:T(8,128)(2,1)}, u32[]{:S(2)}, u32[]{:S(2)}) %collective-permute-start.28) | collective-permute-done | bytes 524320 | tf_op jit(solution)/shard_map/ppermute | solution.py:783
  176.6 10.4 %collective-permute-done.24.theirs.refs_1_ = bf16[528,1024]{1,0:T(8,128)(2,1)S(1)} collective-permute-done((bf16[528,1024]{1,0:T(8,128)(2,1)S(1)}, bf16[528,1024]{1,0:T(8,128)(2,1)S(1)}, u32[]{:S(2)}, u32[]{:S(2)}) %collective-permute-start.24) | collective-permute-done | bytes 1081376 | tf_op jit(solution)/shard_map/ppermute | solution.py:806
  188.3 3.9 %collective-permute-done.31.b = f32[8,1024]{1,0:T(8,128)S(1)} collective-permute-done((f32[8,1024]{1,0:T(8,128)S(1)}, f32[8,1024]{1,0:T(8,128)S(1)}, u32[]{:S(2)}, u32[]{:S(2)}) %collective-permute-start.31) | collective-permute-done | bytes 32800 | tf_op jit(solution)/shard_map/ppermute | solution.py:783
  194.7 3.0 %mlp_last.1 = (f32[1024,256]{1,0:T(8,128)}, f32[256,1024]{1,0:T(8,128)}) custom-call(bf16[2048,256]{1,0:T(8,128)(2,1)} %add.63.a, bf16[2048,256]{1,0:T(8,128)(2,1)} %collective-permute-done.35.b), custom_call_target="tpu_custom_call" | custom-call | tf_op jit(solution)/shard_map/mlp_last/pallas_call | solution.py:636
  199.4 9.0 %collective-permute-done.32.refs_1_ = bf16[512,1024]{1,0:T(8,128)(2,1)} collective-permute-done((bf16[512,1024]{1,0:T(8,128)(2,1)}, bf16[512,1024]{1,0:T(8,128)(2,1)}, u32[]{:S(2)}, u32[]{:S(2)}) %collective-permute-start.32) | collective-permute-done | bytes 1048608 | tf_op jit(solution)/shard_map/ppermute | solution.py:806
  208.4 2.6 %choose.5 = bf16[1024,1024]{1,0:T(8,128)(2,1)} custom-call(s32[1]{0:T(128)} %bitcast.flag, bf16[512,1024]{1,0:T(8,128)(2,1)} %finish_in.3.refs_0_, bf16[512,1024]{1,0:T(8,128)(2,1)} %collective-permute-done.32.refs_1_, bf16[1024,1024]{1,0:T(8,128)(2,1)} %choose.4.refs_2_), custom_call_target="tpu_custom_call", output_to_operand_aliasing={{}: (3, {})} | custom-call | tf_op jit(solution)/shard_map/choose/pallas_call | solution.py:636
  (146 shorter events, 44.9 us)
Async XLA Ops:
  0.6 11.1 %collective-permute-start.1 = (bf16[768,256]{1,0:T(8,128)(2,1)}, bf16[768,256]{1,0:T(8,128)(2,1)S(1)}, u32[]{:S(2)}, u32[]{:S(2)}) collective-permute-start(bf16[768,256]{1,0:T(8,128)(2,1)} %bitcast.40), channel_id=1, source_target_pairs={{0,16},{8,24},{16,0},{24,8},{1,17},{9,25},{17,1},{25,9},{2,18},{10... | collective-permute-start | bytes 1179656 | tf_op jit(solution)/shard_map/ppermute | solution.py:783
  2.2 11.1 %collective-permute-start = (bf16[768,256]{1,0:T(8,128)(2,1)}, bf16[768,256]{1,0:T(8,128)(2,1)S(1)}, u32[]{:S(2)}, u32[]{:S(2)}) collective-permute-start(bf16[768,256]{1,0:T(8,128)(2,1)} %bitcast.41), channel_id=1, source_target_pairs={{0,8},{8,0},{16,24},{24,16},{1,9},{9,1},{17,25},{25,17},{2,10},{10... | collective-permute-start | bytes 1179656 | tf_op jit(solution)/shard_map/ppermute | solution.py:783
  11.8 16.6 %collective-permute-start.3 = (bf16[1024,256]{1,0:T(8,128)(2,1)S(1)}, bf16[1024,256]{1,0:T(8,128)(2,1)S(1)}, u32[]{:S(2)}, u32[]{:S(2)}) collective-permute-start(bf16[1024,256]{1,0:T(8,128)(2,1)S(1)} %bitcast.25), channel_id=1, source_target_pairs={{0,16},{8,24},{16,0},{24,8},{1,17},{9,25},{17,1},{25,9},{2,18},{10... | collective-permute-start | bytes 1572872 | tf_op jit(solution)/shard_map/ppermute | solution.py:783
  16.8 24.9 %collective-permute-start.8 = (bf16[1280,256]{1,0:T(8,128)(2,1)S(1)}, bf16[1280,256]{1,0:T(8,128)(2,1)S(1)}, u32[]{:S(2)}, u32[]{:S(2)}) collective-permute-start(bf16[1280,256]{1,0:T(8,128)(2,1)S(1)} %constant_dynamic-update-slice_fusion.p0.d0), channel_id=1, source_target_pairs={{0,16},{8,24},{16,0},{24,8},{1,17},{9,25},{17,1},{25,9},{2,18},{10... | collective-permute-start | bytes 1966088 | tf_op jit(solution)/shard_map/ppermute | solution.py:783
  18.4 17.4 %collective-permute-start.5 = (bf16[1024,256]{1,0:T(8,128)(2,1)S(1)}, bf16[1024,256]{1,0:T(8,128)(2,1)S(1)}, u32[]{:S(2)}, u32[]{:S(2)}) collective-permute-start(bf16[1024,256]{1,0:T(8,128)(2,1)S(1)} %bitcast.26), channel_id=1, source_target_pairs={{0,8},{8,0},{16,24},{24,16},{1,9},{9,1},{17,25},{25,17},{2,10},{10... | collective-permute-start | bytes 1572872 | tf_op jit(solution)/shard_map/ppermute | solution.py:783
  18.4 14.7 %collective-permute-start.4 = (bf16[1024,256]{1,0:T(8,128)(2,1)S(1)}, bf16[1024,256]{1,0:T(8,128)(2,1)S(1)}, u32[]{:S(2)}, u32[]{:S(2)}) collective-permute-start(bf16[1024,256]{1,0:T(8,128)(2,1)S(1)} %get-tuple-element.106.kv.refs_0_), channel_id=1, source_target_pairs={{0,4},{4,0},{1,5},{5,1},{2,6},{6,2},{3,7},{7,3},{8,12},{12,8},{9,1... | collective-permute-start | bytes 1572872 | tf_op jit(solution)/shard_map/ppermute | solution.py:783
  28.4 7.4 %collective-permute-start.6 = (bf16[1024,256]{1,0:T(8,128)(2,1)S(1)}, bf16[1024,256]{1,0:T(8,128)(2,1)S(1)}, u32[]{:S(2)}, u32[]{:S(2)}) collective-permute-start(bf16[1024,256]{1,0:T(8,128)(2,1)S(1)} %collective-permute-done.3.p2.u2), channel_id=1, source_target_pairs={{0,8},{8,0},{16,24},{24,16},{1,9},{9,1},{17,25},{25,17},{2,10},{10... | collective-permute-start | bytes 1572872 | tf_op jit(solution)/shard_map/ppermute | solution.py:783
  28.6 15.3 %collective-permute-start.10 = (bf16[1024,256]{1,0:T(8,128)(2,1)S(1)}, bf16[1024,256]{1,0:T(8,128)(2,1)S(1)}, u32[]{:S(2)}, u32[]{:S(2)}) collective-permute-start(bf16[1024,256]{1,0:T(8,128)(2,1)S(1)} %get-tuple-element.104.kv.refs_0_), channel_id=1, source_target_pairs={{0,4},{4,0},{1,5},{5,1},{2,6},{6,2},{3,7},{7,3},{8,12},{12,8},{9,1... | collective-permute-start | bytes 1572872 | tf_op jit(solution)/shard_map/ppermute | solution.py:783
  33.1 13.6 %collective-permute-start.7 = (bf16[1280,256]{1,0:T(8,128)(2,1)S(1)}, bf16[1280,256]{1,0:T(8,128)(2,1)S(1)}, u32[]{:S(2)}, u32[]{:S(2)}) collective-permute-start(bf16[1280,256]{1,0:T(8,128)(2,1)S(1)} %constant_dynamic-update-slice_fusion.p0.d0), channel_id=1, source_target_pairs={{0,8},{8,0},{16,24},{24,16},{1,9},{9,1},{17,25},{25,17},{2,10},{10... | collective-permute-start | bytes 1966088 | tf_op jit(solution)/shard_map/ppermute | solution.py:783
  51.5 28.4 %collective-permute-start.11 = (bf16[512,1024]{1,0:T(8,128)(2,1)S(1)}, bf16[512,1024]{1,0:T(8,128)(2,1)S(1)}, u32[]{:S(2)}, u32[]{:S(2)}) collective-permute-start(bf16[512,1024]{1,0:T(8,128)(2,1)S(1)} %get-tuple-element.122.a), channel_id=1, source_target_pairs={{0,1},{3,2},{4,5},{7,6},{8,9},{11,10},{12,13},{15,14},{16,17},{19,... | collective-permute-start | bytes 3145736 | tf_op jit(solution)/shard_map/ppermute | solution.py:795
  63.7 16.2 %collective-permute-start.12 = (bf16[1024,256]{1,0:T(8,128)(2,1)S(1)}, bf16[1024,256]{1,0:T(8,128)(2,1)S(1)}, u32[]{:S(2)}, u32[]{:S(2)}) collective-permute-start(bf16[1024,256]{1,0:T(8,128)(2,1)S(1)} %get-tuple-element.127), channel_id=1, source_target_pairs={{0,4},{4,0},{1,5},{5,1},{2,6},{6,2},{3,7},{7,3},{8,12},{12,8},{9,1... | collective-permute-start | bytes 1572872 | tf_op jit(solution)/shard_map/ppermute | solution.py:783
  67.1 33.8 %collective-permute-start.14 = (bf16[512,1024]{1,0:T(8,128)(2,1)S(1)}, bf16[512,1024]{1,0:T(8,128)(2,1)S(1)}, u32[]{:S(2)}, u32[]{:S(2)}) collective-permute-start(bf16[512,1024]{1,0:T(8,128)(2,1)S(1)} %get-tuple-element.135.a), channel_id=1, source_target_pairs={{0,1},{3,2},{4,5},{7,6},{8,9},{11,10},{12,13},{15,14},{16,17},{19,... | collective-permute-start | bytes 3145736 | tf_op jit(solution)/shard_map/ppermute | solution.py:795
  77.0 14.4 %collective-permute-start.15 = (bf16[1024,256]{1,0:T(8,128)(2,1)S(1)}, bf16[1024,256]{1,0:T(8,128)(2,1)S(1)}, u32[]{:S(2)}, u32[]{:S(2)}) collective-permute-start(bf16[1024,256]{1,0:T(8,128)(2,1)S(1)} %get-tuple-element.132), channel_id=1, source_target_pairs={{0,4},{4,0},{1,5},{5,1},{2,6},{6,2},{3,7},{7,3},{8,12},{12,8},{9,1... | collective-permute-start | bytes 1572872 | tf_op jit(solution)/shard_map/ppermute | solution.py:783
  80.2 21.8 %collective-permute-start.13 = (bf16[512,1024]{1,0:T(8,128)(2,1)S(1)}, bf16[512,1024]{1,0:T(8,128)(2,1)S(1)}, u32[]{:S(2)}, u32[]{:S(2)}) collective-permute-start(bf16[512,1024]{1,0:T(8,128)(2,1)S(1)} %add.60.a), channel_id=1, source_target_pairs={{1,2},{2,1},{5,6},{6,5},{9,10},{10,9},{13,14},{14,13},{17,18},{18,... | collective-permute-start | bytes 3145736 | tf_op jit(solution)/shard_map/ppermute | solution.py:801
  97.5 26.7 %collective-permute-start.17 = (bf16[528,1024]{1,0:T(8,128)(2,1)S(1)}, bf16[528,1024]{1,0:T(8,128)(2,1)S(1)}, u32[]{:S(2)}, u32[]{:S(2)}) collective-permute-start(bf16[528,1024]{1,0:T(8,128)(2,1)S(1)} %get-tuple-element.140.a), channel_id=1, source_target_pairs={{0,1},{3,2},{4,5},{7,6},{8,9},{11,10},{12,13},{15,14},{16,17},{19,... | collective-permute-start | bytes 3244040 | tf_op jit(solution)/shard_map/ppermute | solution.py:795
  101.2 27.7 %collective-permute-start.16 = (bf16[512,1024]{1,0:T(8,128)(2,1)S(1)}, bf16[512,1024]{1,0:T(8,128)(2,1)S(1)}, u32[]{:S(2)}, u32[]{:S(2)}) collective-permute-start(bf16[512,1024]{1,0:T(8,128)(2,1)S(1)} %add.61.a), channel_id=1, source_target_pairs={{1,2},{2,1},{5,6},{6,5},{9,10},{10,9},{13,14},{14,13},{17,18},{18,... | collective-permute-start | bytes 3145736 | tf_op jit(solution)/shard_map/ppermute | solution.py:801
  102.5 30.4 %collective-permute-start.18 = (bf16[512,1024]{1,0:T(8,128)(2,1)S(1)}, bf16[512,1024]{1,0:T(8,128)(2,1)S(1)}, u32[]{:S(2)}, u32[]{:S(2)}) collective-permute-start(bf16[512,1024]{1,0:T(8,128)(2,1)S(1)} %finish_out.2.refs_0_), channel_id=1, source_target_pairs={{1,0},{2,3},{5,4},{6,7},{9,8},{10,11},{13,12},{14,15},{17,16},{18,... | collective-permute-start | bytes 3145736 | tf_op jit(solution)/shard_map/ppermute | solution.py:806
  110.2 24.0 %collective-permute-start.22 = (bf16[1,2048,256]{2,1,0:T(8,128)(2,1)S(1)}, bf16[1,2048,256]{2,1,0:T(8,128)(2,1)S(1)}, u32[]{:S(2)}, u32[]{:S(2)}) collective-permute-start(bf16[1,2048,256]{2,1,0:T(8,128)(2,1)S(1)} %get-tuple-element.153), channel_id=1, source_target_pairs={{0,8},{8,0},{16,24},{24,16},{1,9},{9,1},{17,25},{25,17},{2,10},{10... | collective-permute-start | bytes 3145736 | tf_op jit(solution)/shard_map/ppermute | solution.py:783
  110.4 23.8 %collective-permute-start.23 = (bf16[1,2048,256]{2,1,0:T(8,128)(2,1)S(1)}, bf16[1,2048,256]{2,1,0:T(8,128)(2,1)S(1)}, u32[]{:S(2)}, u32[]{:S(2)}) collective-permute-start(bf16[1,2048,256]{2,1,0:T(8,128)(2,1)S(1)} %get-tuple-element.154), channel_id=1, source_target_pairs={{0,8},{8,0},{16,24},{24,16},{1,9},{9,1},{17,25},{25,17},{2,10},{10... | collective-permute-start | bytes 3145736 | tf_op jit(solution)/shard_map/ppermute | solution.py:783
  124.2 26.1 %collective-permute-start.21 = (bf16[512,1024]{1,0:T(8,128)(2,1)S(1)}, bf16[512,1024]{1,0:T(8,128)(2,1)S(1)}, u32[]{:S(2)}, u32[]{:S(2)}) collective-permute-start(bf16[512,1024]{1,0:T(8,128)(2,1)S(1)} %get-tuple-element.150.a), channel_id=1, source_target_pairs={{0,1},{3,2},{4,5},{7,6},{8,9},{11,10},{12,13},{15,14},{16,17},{19,... | collective-permute-start | bytes 3145736 | tf_op jit(solution)/shard_map/ppermute | solution.py:795
  128.9 22.4 %collective-permute-start.20 = (bf16[528,1024]{1,0:T(8,128)(2,1)S(1)}, bf16[528,1024]{1,0:T(8,128)(2,1)S(1)}, u32[]{:S(2)}, u32[]{:S(2)}) collective-permute-start(bf16[528,1024]{1,0:T(8,128)(2,1)S(1)} %add_extra.1.a), channel_id=1, source_target_pairs={{1,2},{2,1},{5,6},{6,5},{9,10},{10,9},{13,14},{14,13},{17,18},{18,... | collective-permute-start | bytes 3244040 | tf_op jit(solution)/shard_map/ppermute | solution.py:801
  132.9 25.7 %collective-permute-start.19 = (bf16[512,1024]{1,0:T(8,128)(2,1)S(1)}, bf16[512,1024]{1,0:T(8,128)(2,1)S(1)}, u32[]{:S(2)}, u32[]{:S(2)}) collective-permute-start(bf16[512,1024]{1,0:T(8,128)(2,1)S(1)} %finish_out.3.refs_1_), channel_id=1, source_target_pairs={{1,0},{2,3},{5,4},{6,7},{9,8},{10,11},{13,12},{14,15},{17,16},{18,... | collective-permute-start | bytes 3145736 | tf_op jit(solution)/shard_map/ppermute | solution.py:806
  134.9 25.1 %collective-permute-start.27 = (bf16[2048,256]{1,0:T(8,128)(2,1)S(1)}, bf16[2048,256]{1,0:T(8,128)(2,1)S(1)}, u32[]{:S(2)}, u32[]{:S(2)}) collective-permute-start(bf16[2048,256]{1,0:T(8,128)(2,1)S(1)} %get-tuple-element.165), channel_id=1, source_target_pairs={{0,16},{8,24},{16,0},{24,8},{1,17},{9,25},{17,1},{25,9},{2,18},{10... | collective-permute-start | bytes 3145736 | tf_op jit(solution)/shard_map/ppermute | solution.py:783
  150.6 11.6 %collective-permute-start.29 = (bf16[512,1024]{1,0:T(8,128)(2,1)S(1)}, bf16[512,1024]{1,0:T(8,128)(2,1)S(1)}, u32[]{:S(2)}, u32[]{:S(2)}) collective-permute-start(bf16[512,1024]{1,0:T(8,128)(2,1)S(1)} %add.62.a), channel_id=1, source_target_pairs={{1,2},{2,1},{5,6},{6,5},{9,10},{10,9},{13,14},{14,13},{17,18},{18,... | collective-permute-start | bytes 3145736 | tf_op jit(solution)/shard_map/ppermute | solution.py:801
  151.3 9.8 %collective-permute-start.25 = (bf16[1,1024,256]{2,1,0:T(8,128)(2,1)S(1)}, bf16[1,1024,256]{2,1,0:T(8,128)(2,1)S(1)}, u32[]{:S(2)}, u32[]{:S(2)}) collective-permute-start(bf16[1,1024,256]{2,1,0:T(8,128)(2,1)S(1)} %get-tuple-element.163), channel_id=1, source_target_pairs={{0,8},{8,0},{16,24},{24,16},{1,9},{9,1},{17,25},{25,17},{2,10},{10... | collective-permute-start | bytes 1572872 | tf_op jit(solution)/shard_map/ppermute | solution.py:783
  151.4 9.7 %collective-permute-start.26 = (bf16[1,1024,256]{2,1,0:T(8,128)(2,1)S(1)}, bf16[1,1024,256]{2,1,0:T(8,128)(2,1)S(1)}, u32[]{:S(2)}, u32[]{:S(2)}) collective-permute-start(bf16[1,1024,256]{2,1,0:T(8,128)(2,1)S(1)} %get-tuple-element.164), channel_id=1, source_target_pairs={{0,8},{8,0},{16,24},{24,16},{1,9},{9,1},{17,25},{25,17},{2,10},{10... | collective-permute-start | bytes 1572872 | tf_op jit(solution)/shard_map/ppermute | solution.py:783
  158.6 28.3 %collective-permute-start.24 = (bf16[528,1024]{1,0:T(8,128)(2,1)S(1)}, bf16[528,1024]{1,0:T(8,128)(2,1)S(1)}, u32[]{:S(2)}, u32[]{:S(2)}) collective-permute-start(bf16[528,1024]{1,0:T(8,128)(2,1)S(1)} %finish_in.2.ours.refs_0_), channel_id=1, source_target_pairs={{1,0},{2,3},{5,4},{6,7},{9,8},{10,11},{13,12},{14,15},{17,16},{18,... | collective-permute-start | bytes 3244040 | tf_op jit(solution)/shard_map/ppermute | solution.py:806
  162.1 12.0 %collective-permute-start.28 = (bf16[1024,256]{1,0:T(8,128)(2,1)}, bf16[1024,256]{1,0:T(8,128)(2,1)}, u32[]{:S(2)}, u32[]{:S(2)}) collective-permute-start(bf16[1024,256]{1,0:T(8,128)(2,1)} %get-tuple-element.170), channel_id=1, source_target_pairs={{0,16},{8,24},{16,0},{24,8},{1,17},{9,25},{17,1},{25,9},{2,18},{10... | collective-permute-start | bytes 1572872 | tf_op jit(solution)/shard_map/ppermute | solution.py:783
  162.1 32.6 %collective-permute-start.35 = (bf16[2048,256]{1,0:T(8,128)(2,1)}, bf16[2048,256]{1,0:T(8,128)(2,1)}, u32[]{:S(2)}, u32[]{:S(2)}) collective-permute-start(bf16[2048,256]{1,0:T(8,128)(2,1)} %add.63.a), channel_id=1, source_target_pairs={{0,4},{4,0},{1,5},{5,1},{2,6},{6,2},{3,7},{7,3},{8,12},{12,8},{9,1... | collective-permute-start | bytes 3145736 | tf_op jit(solution)/shard_map/ppermute | solution.py:783
  164.8 43.5 %collective-permute-start.32 = (bf16[512,1024]{1,0:T(8,128)(2,1)}, bf16[512,1024]{1,0:T(8,128)(2,1)}, u32[]{:S(2)}, u32[]{:S(2)}) collective-permute-start(bf16[512,1024]{1,0:T(8,128)(2,1)} %finish_in.3.refs_0_), channel_id=1, source_target_pairs={{1,0},{2,3},{5,4},{6,7},{9,8},{10,11},{13,12},{14,15},{17,16},{18,... | collective-permute-start | bytes 3145736 | tf_op jit(solution)/shard_map/ppermute | solution.py:806
  176.5 21.2 %collective-permute-start.34 = (bf16[1024,256]{1,0:T(8,128)(2,1)S(1)}, bf16[1024,256]{1,0:T(8,128)(2,1)S(1)}, u32[]{:S(2)}, u32[]{:S(2)}) collective-permute-start(bf16[1024,256]{1,0:T(8,128)(2,1)S(1)} %add.64.a), channel_id=1, source_target_pairs={{0,4},{4,0},{1,5},{5,1},{2,6},{6,2},{3,7},{7,3},{8,12},{12,8},{9,1... | collective-permute-start | bytes 1572872 | tf_op jit(solution)/shard_map/ppermute | solution.py:783
  192.2 6.5 %collective-permute-start.33 = (f32[8,1024]{1,0:T(8,128)S(1)}, f32[8,1024]{1,0:T(8,128)S(1)}, u32[]{:S(2)}, u32[]{:S(2)}) collective-permute-start(f32[8,1024]{1,0:T(8,128)S(1)} %add.66.a), channel_id=1, source_target_pairs={{0,4},{4,0},{1,5},{5,1},{2,6},{6,2},{3,7},{7,3},{8,12},{12,8},{9,1... | collective-permute-start | bytes 98312 | tf_op jit(solution)/shard_map/ppermute | solution.py:783
  (31 other events, 261.6 us)
